TPU v7x, 256 devices: a whole 4x4x8 slice. The times are simulated.
256 devices in a mesh: grp: 64 (over y, x, z_lo, core), band: 4 (over z_hi).
Axes of the slice: x: 4, y: 4, z: 8 (z_hi: 4, z_lo: 2; z = z_hi * 2 + z_lo), core: 2. Of those that a mesh axis runs over, the one named last changes fastest.
Arguments:
- voltages: bfloat16 [64, 2048, 2048], P('band', 'grp'), may hold values from -6 to 6
- steering: int32 [2, 1024], replicated, may hold values from 0 to 255, as said below
- chan_sub: int32 [1024], P('band'), may hold values from 0 to 15, as said below
- delays: int32 [512, 16], P(None, 'band'), may hold values from 0 to 63
Outputs:
- dedispersed: float32 [64, 1024, 512], P(None, 'grp', 'band')
Inputs may be any that keep to these rules, and one draw needn't show every extreme that they name: Every pair (steering[0, b], steering[1, b]) with the first below 256 and the second below 4 occurs for exactly one beam b. chan_sub[c] // 4 == c // 256: a channel belongs to a subband of its own quarter of the band.
All inputs are finite; a program needn't handle non-finite values.
Results may differ from a plain program's by a relative error of at most 0.0041.
Values may be sent and summed in bfloat16 or wider, within the bound.
No kernel may reach another device: no remote copies, remote signals or barrier semaphores. Data moves between devices by JAX's collectives and lax.ppermute only.
A program may use at most 64 MiB of HBM per device.

v0:
```python
import math

import jax
import jax.numpy as jnp
import numpy as np
from jax import lax
from jax.experimental import pallas as pl
from jax.experimental.pallas import tpu as pltpu
from jax.sharding import PartitionSpec as P

A = 2048
FEEDS = 1024
C = 1024
SAMP = 2048
BEAMS = 1024
TRIALS = 512
F32 = jnp.float32
BF16 = jnp.bfloat16
NT = (((1,), (1,)), ((), ()))
NN = (((1,), (0,)), ((), ()))


def window_taps():
    tap_pos = np.arange(4 * SAMP) + 0.5
    taper = 0.5 - 0.5 * np.cos(2.0 * np.pi / (4 * SAMP) * tap_pos)
    window = taper * np.sinc((tap_pos - 2 * SAMP) / SAMP)
    window = window * np.sqrt(SAMP / np.sum(window * window))
    return window.reshape(4, SAMP).astype(np.float32)


def lane_tables():
    r = np.arange(16)[:, None, None]
    k = np.arange(64)[None, :, None]
    lane = np.arange(128)[None, None, :]
    angle = 2.0 * np.pi / SAMP * (((16 * k + r) * lane) % SAMP)
    cos, sin = np.cos(angle) / np.sqrt(SAMP), np.sin(angle) / np.sqrt(SAMP)
    sign = np.where(r > 8, -1.0, 1.0)
    top = np.concatenate([cos, -sin * sign], axis=2)
    low = np.concatenate([-sin, -cos * sign], axis=2)
    return np.concatenate([top, low], axis=1).astype(jnp.bfloat16)


def real_dft16(x):
    h, c1, c3 = math.sqrt(0.5), math.cos(math.pi / 8), math.cos(3 * math.pi / 8)
    s = [x[j] + x[j + 8] for j in range(8)]
    d = [x[j] - x[j + 8] for j in range(8)]
    ss = [s[j] + s[j + 4] for j in range(4)]
    sd = [s[j] - s[j + 4] for j in range(4)]
    t0, t1 = ss[0] + ss[2], ss[1] + ss[3]
    out = [None] * 9
    out[0] = (t0 + t1, None)
    out[8] = (t0 - t1, None)
    out[4] = (ss[0] - ss[2], ss[1] - ss[3])
    dif, tot = h * (sd[1] - sd[3]), h * (sd[1] + sd[3])
    out[2] = (sd[0] + dif, sd[2] + tot)
    out[6] = (sd[0] - dif, tot - sd[2])
    p = [None] + [d[j] - d[8 - j] for j in (1, 2, 3)]
    q = [None] + [d[j] + d[8 - j] for j in (1, 2, 3)]
    hp, hq = h * p[2], h * q[2]
    ea, eb = d[0] + hp, d[0] - hp
    u, v = c1 * p[1] + c3 * p[3], c3 * p[1] - c1 * p[3]
    fa, fb = d[4] + hq, hq - d[4]
    y, z = c3 * q[1] + c1 * q[3], c1 * q[1] - c3 * q[3]
    out[1] = (ea + u, y + fa)
    out[7] = (ea - u, y - fa)
    out[3] = (eb + v, z + fb)
    out[5] = (eb - v, z - fb)
    return out


def spectra_kernel(v_ref, halo_ref, win_ref, tab_ref, out_ref, part_ref, turn_ref):
    frames = v_ref.shape[0]

    def bins(m, half, rows):
        a0 = 16 * half
        lanes = []
        for jb in range(16):
            cols = slice(128 * jb, 128 * jb + 128)
            total = None
            for p in range(4):
                term = rows(p)[pl.ds(a0, 16), cols].astype(F32) * win_ref[p : p + 1, cols]
                total = term if total is None else total + term
            lanes.append(total)
        row0 = pl.multiple_of(m * 32 + a0, 16)
        for at, (re, im) in enumerate(real_dft16(lanes)):
            part_ref[at, pl.ds(row0, 16), 0:128] = re.astype(BF16)
            if im is None:
                part_ref[at, pl.ds(row0, 16), 128:256] = jnp.zeros((16, 128), BF16)
            else:
                part_ref[at, pl.ds(row0, 16), 128:256] = im.astype(BF16)

    for m in range(3):
        for half in range(2):
            bins(m, half, lambda p, m=m: halo_ref.at[m + p] if m + p < 3 else v_ref.at[m + p - 3])

    def body(step, carry):
        m = step // 2
        bins(m, pl.multiple_of(step % 2, 1), lambda p: v_ref.at[m - 3 + p])
        return carry

    lax.fori_loop(6, 2 * frames, body, 0)

    def transform(r, carry):
        at = jnp.minimum(r, 16 - r)
        rows = lax.dot_general(tab_ref[r], part_ref[at], NT, preferred_element_type=F32)
        for reim in range(2):
            for mb in range(4):
                turn_ref[pl.ds(reim * 4 + mb, 64, stride=8), :] = rows[
                    64 * reim : 64 * reim + 64, 128 * mb : 128 * mb + 128
                ]
        for q in range(4):
            out_ref[q, r] = turn_ref[128 * q : 128 * q + 128, :].astype(BF16)
        return carry

    lax.fori_loop(0, 16, transform, 0)


def spectra(voltages, halo):
    return pl.pallas_call(
        spectra_kernel,
        out_shape=jax.ShapeDtypeStruct((4, 16, 128, 128), BF16),
        in_specs=[pl.BlockSpec(memory_space=pltpu.VMEM)] * 4,
        out_specs=pl.BlockSpec(memory_space=pltpu.VMEM),
        scratch_shapes=[pltpu.VMEM((9, 512, 256), BF16), pltpu.VMEM((512, 128), F32)],
        cost_estimate=pl.CostEstimate(
            flops=600_000_000, bytes_accessed=6_000_000, transcendentals=0
        ),
    )(voltages, halo, jnp.asarray(window_taps()), jnp.asarray(lane_tables()))


def turn_blocks(tiles):
    lane = lax.broadcasted_iota(jnp.int32, tiles[0].shape, 1)
    odd, high = (lane // 32) % 2 == 1, lane // 64 == 1
    one = [None] * 4
    for a, b in ((0, 1), (2, 3)):
        one[a] = jnp.where(odd, pltpu.roll(tiles[b], 32, 1), tiles[a])
        one[b] = jnp.where(odd, tiles[b], pltpu.roll(tiles[a], 96, 1))
    two = [None] * 4
    for a, b in ((0, 2), (1, 3)):
        two[a] = jnp.where(high, pltpu.roll(one[b], 64, 1), one[a])
        two[b] = jnp.where(high, one[b], pltpu.roll(one[a], 64, 1))
    return two


def beam_kernel(east_ref, sub_ref, x_ref, w_ref, hot_ref, out_ref, left_ref, prod_ref, acc_ref):
    acc_ref[...] = jnp.zeros_like(acc_ref)
    sign = jnp.where(lax.broadcasted_iota(jnp.int32, (8, 128), 0) < 4, -1.0, 1.0).astype(F32)

    def times_i(x):
        return sign * pltpu.roll(x, 4, 0)

    def pair(step, carry):
        row0 = pl.multiple_of(16 * step, 16)
        for pe in range(8):
            for h in range(2):
                src = pe * 8 + h * 4
                tiles = turn_blocks([x_ref[src + n, pl.ds(row0, 16), :] for n in range(4)])
                tiles = [t.astype(F32) for t in tiles]
                for ch in range(2):
                    for mm in range(2):
                        both = jnp.concatenate(
                            [tiles[2 * mm][8 * ch : 8 * ch + 8], tiles[2 * mm + 1][8 * ch : 8 * ch + 8]], axis=0
                        )
                        left_ref[ch, pe * 32 + mm * 16 : pe * 32 + mm * 16 + 16, 128 * h : 128 * h + 128] = both.astype(BF16)
        for ch in range(2):
            i = 2 * step + ch
            prod_ref[ch] = lax.dot_general(left_ref[ch], w_ref[i], NN, preferred_element_type=F32)
        for ch in range(2):
            i = 2 * step + ch
            sub = sub_ref[i]
            re = [[east_ref[i, s * 4 + e] for e in range(4)] for s in range(4)]
            im = [[east_ref[i, 16 + s * 4 + e] for e in range(4)] for s in range(4)]

            def frame_block(m4, carry):
                for h in range(2):
                    power = [None] * 4
                    for p in range(2):
                        y, iy = [], []
                        for e in range(4):
                            rows = pl.ds(pl.multiple_of((p * 4 + e) * 32 + m4 * 8, 8), 8)
                            both = prod_ref[ch, rows, 128 * h : 128 * h + 128] + times_i(
                                prod_ref[ch, rows, 256 + 128 * h : 384 + 128 * h]
                            )
                            y.append(both)
                            iy.append(times_i(both))
                        for s in range(4):
                            beam = y[0]
                            for e in range(1, 4):
                                if s == 0:
                                    beam = beam + y[e]
                                else:
                                    beam = beam + re[s][e] * y[e] + im[s][e] * iy[e]
                            square = beam * beam
                            power[s] = square if p == 0 else power[s] + square
                    for s in range(4):
                        cols = slice(s * 256 + h * 128, s * 256 + h * 128 + 128)
                        acc_ref[sub, m4, :, cols] += power[s]
                return carry

            lax.fori_loop(0, 4, frame_block, 0)
        return carry

    lax.fori_loop(0, 8, pair, 0)
    total = acc_ref[...].reshape(128, 1024)
    low_half = lax.broadcasted_iota(jnp.int32, (128, 1024), 0) % 8 < 4
    turned = acc_ref[...].reshape(16, 8, 1024)
    turned = jnp.concatenate([turned[:, 4:8], turned[:, 0:4]], axis=1).reshape(128, 1024)
    total = total + turned
    top = total.astype(BF16)
    rest = (total - top.astype(F32)).astype(BF16)
    parts = jnp.where(low_half, top, rest)
    out_ref[...] = lax.dot_general(hot_ref[...], parts, NT, preferred_element_type=F32).astype(BF16)


def beams(turned, east, subs, weights, hot):
    vmem, smem = pl.BlockSpec(memory_space=pltpu.VMEM), pl.BlockSpec(memory_space=pltpu.SMEM)
    return pl.pallas_call(
        beam_kernel,
        out_shape=jax.ShapeDtypeStruct((1024, 128), BF16),
        in_specs=[smem, smem, vmem, vmem, vmem],
        out_specs=vmem,
        scratch_shapes=[
            pltpu.VMEM((2, 256, 256), BF16),
            pltpu.VMEM((2, 256, 512), F32),
            pltpu.VMEM((4, 4, 8, 1024), F32),
        ],
        cost_estimate=pl.CostEstimate(
            flops=2_000_000_000, bytes_accessed=9_000_000, transcendentals=0
        ),
    )(east, subs, turned, weights, hot)


def beam_weights(channels):
    scale = 2 * C
    steps = scale - channels
    north = jnp.arange(256, dtype=jnp.int32)
    turns = steps[:, None, None] * (north[:, None] * north[None, :])[None] % (scale * 256)
    phases = (2.0 * math.pi / (scale * 256)) * turns.astype(F32)
    norm = 1.0 / math.sqrt(FEEDS)
    weights = jnp.concatenate([jnp.cos(phases), jnp.sin(phases)], axis=2) * norm
    four = jnp.arange(4, dtype=jnp.int32)
    turns = steps[:, None] * (four[:, None] * four[None, :]).reshape(1, 16) % (scale * 4)
    phases = (2.0 * math.pi / (scale * 4)) * turns.astype(F32)
    return weights.astype(BF16), jnp.concatenate([jnp.cos(phases), jnp.sin(phases)], axis=1)


def frame_tables():
    table = np.zeros((4, 4, 4, 2, 4, 4, 64), np.float32)
    for block in range(4):
        for m4 in range(4):
            for mb in range(4):
                row = np.full(64, -1.0 / 64.0)
                row[16 * block + 4 * mb + m4] += 1.0
                for sub in range(4):
                    table[block, sub, m4, :, mb, sub, :] = row / math.sqrt(C)
    return table.reshape(4, 128, 256).astype(jnp.bfloat16)


def three_parts(x):
    top = x.astype(BF16)
    rest = x - top.astype(F32)
    mid = rest.astype(BF16)
    return top, mid, (rest - mid.astype(F32)).astype(BF16)


def series_kernel(band_ref, s0_ref, s1_ref, s2_ref, s3_ref, tab_ref, delay_ref, out_ref, hot_ref, left_ref):
    series = None
    for back, ref in enumerate((s0_ref, s1_ref, s2_ref, s3_ref)):
        table = tab_ref[(4 - back) % 4]
        for part in three_parts(ref[...]):
            term = lax.dot_general(part, table, NN, preferred_element_type=F32)
            series = term if series is None else series + term
    back_shift = lax.broadcasted_iota(jnp.int32, (64, 128), 0)
    for s in range(16):
        hit = (back_shift + delay_ref[s : s + 1, :]) % 64 == 0
        hot_ref[64 * s : 64 * s + 64, :] = jnp.where(hit, 1.0, 0.0).astype(BF16)
    lane = lax.broadcasted_iota(jnp.int32, (16, 128), 1) % 64
    first = band_ref[0] * 16
    blocks = [series[16 * (at // 2) : 16 * (at // 2) + 16, 128 * (at % 2) : 128 * (at % 2) + 128] for at in range(8)]
    for t in range(64):
        for at in range(8):
            x = blocks[at]
            if t:
                x = jnp.where(lane < 64 - t, pltpu.roll(x, 128 - t, 1), pltpu.roll(x, 64 - t, 1))
            top = x.astype(BF16)
            left_ref[0, 16 * t : 16 * t + 16, 128 * at : 128 * at + 128] = top
            left_ref[1, 16 * t : 16 * t + 16, 128 * at : 128 * at + 128] = (x - top.astype(F32)).astype(BF16)

    def frames(step, carry):
        rows = pl.ds(pl.multiple_of(256 * step, 256), 256)
        hot = hot_ref[...]
        out = lax.dot_general(left_ref[0, rows, :], hot, NN, preferred_element_type=F32)
        out = out + lax.dot_general(left_ref[1, rows, :], hot, NN, preferred_element_type=F32)
        at = (first + 16 * step) % 64
        out_ref[pl.ds(at, 16)] = out.reshape(16, 16, 128)
        return carry

    lax.fori_loop(0, 4, frames, 0)


def series(band_at, sums, delays):
    vmem, smem = pl.BlockSpec(memory_space=pltpu.VMEM), pl.BlockSpec(memory_space=pltpu.SMEM)
    return pl.pallas_call(
        series_kernel,
        out_shape=jax.ShapeDtypeStruct((64, 16, 128), F32),
        in_specs=[smem] + [vmem] * 6,
        out_specs=vmem,
        scratch_shapes=[pltpu.VMEM((1024, 128), BF16), pltpu.VMEM((2, 1024, 1024), BF16)],
        cost_estimate=pl.CostEstimate(
            flops=600_000_000, bytes_accessed=1_000_000, transcendentals=0
        ),
    )(band_at.reshape(1), *sums, jnp.asarray(frame_tables()), delays)


def from_band(block, back):
    count = lax.axis_size("band")
    return lax.ppermute(block, "band", [(i, (i + back) % count) for i in range(count)])


def local(voltages, steering, chan_sub, delays):
    band_count = lax.axis_size("band")
    grp_at = lax.axis_index("grp")
    band_at = lax.axis_index("band")
    local_frames = voltages.shape[0]
    halo = lax.ppermute(
        voltages[local_frames - 3 :], "band", [(i, i + 1) for i in range(band_count - 1)]
    )
    turned_delays = jnp.transpose(delays)
    small = []
    for back in range(band_count):
        trials = lax.dynamic_slice_in_dim(
            turned_delays, (band_at + back) % band_count * 128, 128, axis=1
        )
        note = jnp.concatenate([chan_sub.reshape(2, 128), jnp.zeros((2, 128), jnp.int32), trials])
        small.append(note if back == 0 else from_band(note, back))
    quarter_at = grp_at // 16
    residue = grp_at % 16

    def owned_by(owner):
        found = small[0] * 0
        for back in range(band_count):
            found = found + jnp.where((band_at - back) % band_count == owner, small[back], 0)
        return found

    quarter_subs = owned_by(quarter_at)[0:2].reshape(16, 16)
    subs = lax.dynamic_slice_in_dim(quarter_subs, residue, 1, axis=1).reshape(16) % 4
    all_delays = jnp.concatenate([owned_by(owner)[4:8] for owner in range(band_count)])

    chunks = spectra(voltages, halo).reshape(64, 128, 128)
    turned = lax.all_to_all(chunks, "grp", split_axis=0, concat_axis=0, tiled=True)

    channels = quarter_at * 256 + 16 * jnp.arange(16, dtype=jnp.int32) + residue
    weights, east = beam_weights(channels)
    grid_at = steering[1] * 256 + steering[0]
    hot = (grid_at[:, None] == jnp.arange(1024, dtype=jnp.int32)[None, :]).astype(BF16)
    sums = beams(turned, east, subs, weights, hot).reshape(64, 16, 128)
    owned = lax.all_to_all(sums, "grp", split_axis=0, concat_axis=0, tiled=True)
    own = jnp.sum(owned.reshape(4, 16, 16, 128).astype(F32), axis=1).reshape(64, 128)
    every = [own if back == 0 else from_band(own, back) for back in range(band_count)]
    return series(band_at, every, all_delays)


def solution(mesh):
    in_specs = (P("band", "grp", None), P(), P("band"), P(None, "band"))
    out_specs = P(None, "grp", "band")
    return jax.shard_map(local, mesh=mesh, in_specs=in_specs, out_specs=out_specs, check_vma=False)
```

profile of v0, /device:TPU:1, one launch (start us, length us, event | category | flops | bytes accessed | tf_op | source)
XLA Modules:
  0.0 125.9 jit_solution(10255366094605648633)
XLA Ops:
  0.0 1.0 slice.25
  1.0 0.0 copy-start.5
  1.0 0.0 copy-start.3
  1.0 0.0 copy-start.4
  1.1 5.9 %collective-permute-start.3 = (bf16[3,32,2048]{2,1,0:T(8,128)(2,1)S(1)}, bf16[3,32,2048]{2,1,0:T(8,128)(2,1)S(1)}, u32[]{:S(2)}, u32[]{:S(2)}) collective-permute-start(bf16[3,32,2048]{2,1,0:T(8,128)(2,1)S(1)} %slice.25), channel_id=1, source_target_pairs={{0,1},{1,2},{2,3},{4,5},{5,6},{6,7},{8,9},{9,10},{10,11},{12,13},{... | collective-permute-start | bytes 1179656 | tf_op jit(solution)/shard_map/ppermute | solution.py:325
  6.9 7.8 %collective-permute-done.3.halo_ref = bf16[3,32,2048]{2,1,0:T(8,128)(2,1)S(1)} collective-permute-done((bf16[3,32,2048]{2,1,0:T(8,128)(2,1)S(1)}, bf16[3,32,2048]{2,1,0:T(8,128)(2,1)S(1)}, u32[]{:S(2)}, u32[]{:S(2)}) %collective-permute-start.3) | collective-permute-done | bytes 393248 | tf_op jit(solution)/shard_map/ppermute | solution.py:325
  14.7 0.0 copy-start.1
  14.7 0.7 copy-done.1
  15.5 9.7 %shard_map.73 = bf16[4,16,128,128]{3,2,1,0:T(8,128)(2,1)} custom-call(bf16[16,32,2048]{2,1,0:T(8,128)(2,1)} %v_ref.1, bf16[3,32,2048]{2,1,0:T(8,128)(2,1)} %copy-done.1, f32[4,2048]{1,0:T(4,128)} %constant.173.clone.win_ref, bf16[16,128,256]{2,1,0:T(8,128)(2,1)} %constant.174.clone.tab_ref), custom_call_target="tpu_custom_call" | custom-call | flops 600000000 | bytes 6000000 | tf_op jit(solution)/shard_map/pallas_call | solution.py:119
  25.2 18.3 %all-to-all-start = ((bf16[64,128,128]{2,1,0:T(8,128)(2,1)}), bf16[64,128,128]{2,1,0:T(8,128)(2,1)S(1)}, u32[]{:S(2)}, u32[]{:S(2)}) async-start(bf16[64,128,128]{2,1,0:T(8,128)(2,1)} %bitcast.19), calls=%async_computation | async-start | bytes 4194304 | tf_op jit(solution)/shard_map/all_to_all | solution.py:350
  43.6 0.1 pad.16.clone
  43.7 0.0 copy-done.5
  43.7 0.0 copy-done.3
  43.7 0.1 fusion.12
  43.7 3.2 %collective-permute-start = (s32[8,128]{1,0:T(8,128)S(1)}, s32[8,128]{1,0:T(8,128)S(1)}, u32[]{:S(2)}, u32[]{:S(2)}) collective-permute-start(s32[8,128]{1,0:T(8,128)S(1)} %get-tuple-element.15), channel_id=1, source_target_pairs={{0,1},{1,2},{2,3},{3,0},{4,5},{5,6},{6,7},{7,4},{8,9},{9,10},{10,1... | collective-permute-start | bytes 12296 | tf_op jit(solution)/shard_map/ppermute | solution.py:317
  47.0 4.2 %collective-permute-start.1 = (s32[8,128]{1,0:T(8,128)S(1)}, s32[8,128]{1,0:T(8,128)S(1)}, u32[]{:S(2)}, u32[]{:S(2)}) collective-permute-start(s32[8,128]{1,0:T(8,128)S(1)} %get-tuple-element.16), channel_id=1, source_target_pairs={{0,2},{1,3},{2,0},{3,1},{4,6},{5,7},{6,4},{7,5},{8,10},{9,11},{10,... | collective-permute-start | bytes 12296 | tf_op jit(solution)/shard_map/ppermute | solution.py:317
  51.2 3.4 %collective-permute-start.2 = (s32[8,128]{1,0:T(8,128)S(1)}, s32[8,128]{1,0:T(8,128)S(1)}, u32[]{:S(2)}, u32[]{:S(2)}) collective-permute-start(s32[8,128]{1,0:T(8,128)S(1)} %get-tuple-element.17), channel_id=1, source_target_pairs={{0,3},{1,0},{2,1},{3,2},{4,7},{5,4},{6,5},{7,6},{8,11},{9,8},{10,9... | collective-permute-start | bytes 12296 | tf_op jit(solution)/shard_map/ppermute | solution.py:317
  54.6 0.1 mul.124
  54.7 0.0 copy-done.4
  54.7 0.1 fusion.14
  54.8 16.4 %fusion.6 = (f32[16,256,256]{2,1,0:T(8,128)S(1)}, f32[16,256,256]{2,1,0:T(8,128)S(1)}) fusion(s32[256,256]{1,0:T(8,128)S(1)} %iota_multiply_fusion, s32[16]{0:T(128)S(1)} %add_subtract_fusion), kind=kLoop, calls=%fused_computation.13 | loop fusion | flops 14680064 | bytes 8650816 | tf_op jit(solution)/shard_map/cos | solution.py:240
  71.2 2.4 %fusion.w_ref = bf16[16,256,512]{2,1,0:T(8,128)(2,1)} fusion(f32[16,256,256]{2,1,0:T(8,128)S(1)} %get-tuple-element.6, f32[16,256,256]{2,1,0:T(8,128)S(1)} %get-tuple-element.5), kind=kLoop, calls=%fused_computation.1 | loop fusion | flops 6291456 | bytes 12582912 | tf_op jit(solution)/shard_map/convert_element_type | solution.py:244
  73.7 1.8 %fusion.4.hot_ref = bf16[1024,1024]{1,0:T(8,128)(2,1)} fusion(s32[1024]{0:T(1024)S(1)} %bitcast.25), kind=kLoop, calls=%fused_computation.11 | loop fusion | flops 2097152 | bytes 2101248 | tf_op jit(solution)/shard_map/convert_element_type | solution.py:355
  75.4 0.7 pad_maximum_fusion.east_ref
  76.1 0.0 collective-permute-done
  76.1 0.0 collective-permute-done.1
  76.1 0.0 collective-permute-done.2
  76.1 0.1 select_add_fusion.4
  76.2 0.1 reshape.83
  76.3 0.1 constant_dynamic-slice_fusion
  76.4 0.1 copy.9
  76.4 0.6 and_select_fusion.sub_ref
  77.0 0.0 all-to-all-done.x_ref
  77.0 0.0 copy-start
  77.0 1.3 %copy-done = bf16[64,128,128]{2,1,0:T(8,128)(2,1)} copy-done((bf16[64,128,128]{2,1,0:T(8,128)(2,1)}, bf16[64,128,128]{2,1,0:T(8,128)(2,1)S(1)}, u32[]{:S(2)}) %copy-start) | copy-done | bytes 2097176
  78.4 11.8 %shard_map.74 = bf16[1024,128]{1,0:T(8,128)(2,1)} custom-call(f32[16,32]{1,0:T(8,128)} %pad_maximum_fusion.east_ref, s32[16]{0:T(128)} %and_select_fusion.sub_ref, bf16[64,128,128]{2,1,0:T(8,128)(2,1)} %copy-done, bf16[16,256,512]{2,1,0:T(8,128)(2,1)} %fusion.w_ref, bf16[1024,1024]{1,0:T(8,128)(2,1)} %fusion.4.hot_ref), custom_call_target="tpu_custom_call" | custom-call | flops 2000000000 | bytes 9000000 | tf_op jit(solution)/shard_map/pallas_call | solution.py:217
  90.2 9.7 %all-to-all-start.1 = ((bf16[64,16,128]{2,1,0:T(8,128)(2,1)}), bf16[64,16,128]{2,1,0:T(8,128)(2,1)S(1)}, u32[]{:S(2)}, u32[]{:S(2)}) async-start(bf16[64,16,128]{2,1,0:T(8,128)(2,1)} %bitcast.20), calls=%async_computation.1 | async-start | bytes 524288 | tf_op jit(solution)/shard_map/all_to_all | solution.py:357
  99.9 0.1 select_add_fusion.3
  100.0 0.1 select_add_fusion.2
  100.1 9.7 %all-to-all-done.1 = bf16[64,16,128]{2,1,0:T(8,128)(2,1)S(1)} async-done(((bf16[64,16,128]{2,1,0:T(8,128)(2,1)}), bf16[64,16,128]{2,1,0:T(8,128)(2,1)S(1)}, u32[]{:S(2)}, u32[]{:S(2)}) %all-to-all-start.1) | async-done | bytes 262176 | tf_op jit(solution)/shard_map/all_to_all | solution.py:357
  109.8 0.0 copy-start.2
  109.8 0.3 collective-permute-start.4
  110.2 1.8 %collective-permute-start.5 = (f32[64,128]{1,0:T(8,128)S(1)}, f32[64,128]{1,0:T(8,128)S(1)}, u32[]{:S(2)}, u32[]{:S(2)}) collective-permute-start(f32[64,128]{1,0:T(8,128)S(1)} %bitcast.22), channel_id=1, source_target_pairs={{0,2},{1,3},{2,0},{3,1},{4,6},{5,7},{6,4},{7,5},{8,10},{9,11},{10,... | collective-permute-start | bytes 98312 | tf_op jit(solution)/shard_map/ppermute | solution.py:317
  111.9 1.8 %collective-permute-start.6 = (f32[64,128]{1,0:T(8,128)S(1)}, f32[64,128]{1,0:T(8,128)S(1)}, u32[]{:S(2)}, u32[]{:S(2)}) collective-permute-start(f32[64,128]{1,0:T(8,128)S(1)} %bitcast.23), channel_id=1, source_target_pairs={{0,3},{1,0},{2,1},{3,2},{4,7},{5,4},{6,5},{7,6},{8,11},{9,8},{10,9... | collective-permute-start | bytes 98312 | tf_op jit(solution)/shard_map/ppermute | solution.py:317
  113.7 0.6 pad_add_fusion.delay_ref
  114.3 0.8 collective-permute-done.4.s1_ref
  115.1 0.0 copy-start.6
  115.1 1.8 %collective-permute-done.5.s2_ref = f32[64,128]{1,0:T(8,128)S(1)} collective-permute-done((f32[64,128]{1,0:T(8,128)S(1)}, f32[64,128]{1,0:T(8,128)S(1)}, u32[]{:S(2)}, u32[]{:S(2)}) %collective-permute-start.5) | collective-permute-done | bytes 32800 | tf_op jit(solution)/shard_map/ppermute | solution.py:317
  116.9 0.0 copy-start.7
  116.9 2.2 %collective-permute-done.6.s3_ref = f32[64,128]{1,0:T(8,128)S(1)} collective-permute-done((f32[64,128]{1,0:T(8,128)S(1)}, f32[64,128]{1,0:T(8,128)S(1)}, u32[]{:S(2)}, u32[]{:S(2)}) %collective-permute-start.6) | collective-permute-done | bytes 32800 | tf_op jit(solution)/shard_map/ppermute | solution.py:317
  119.1 0.0 copy-start.8
  119.1 0.0 copy-done.2
  119.1 0.0 copy-done.6
  119.1 0.0 copy-done.7
  119.1 0.6 copy-done.8
  119.7 6.2 %shard_map.75 = f32[64,16,128]{2,1,0:T(8,128)} custom-call(s32[1]{0:T(128)} %bitcast.band_ref, f32[64,128]{1,0:T(8,128)} %bitcast.24, f32[64,128]{1,0:T(8,128)} %copy-done.6, f32[64,128]{1,0:T(8,128)} %copy-done.7, f32[64,128]{1,0:T(8,128)} %copy-done.8, bf16[4,128,256]{2,1,0:T(8,128)(2,1)} %constant.175.clone.tab_ref, s32[16,128]{1,0:T(8,128)} %pad_add_fusion.delay_ref), custom_call_target="tpu_custom_call" | custom-call | flops 600000000 | bytes 1000000 | tf_op jit(solution)/shard_map/pallas_call | solution.py:303
  (12 shorter events, 0.1 us)
Async XLA Ops:
  1.0 42.6 %copy-start.5 = (s32[512,4]{0,1:T(4,128)S(1)}, s32[512,4]{0,1:T(4,128)}, u32[]{:S(2)}) copy-start(s32[512,4]{0,1:T(4,128)} %param.10) | copy-start | bytes 24580
  1.0 42.6 %copy-start.3 = (s32[256]{0:T(256)S(1)}, s32[256]{0:T(256)}, u32[]{:S(2)}) copy-start(s32[256]{0:T(256)} %param.9) | copy-start | bytes 3076
  1.0 53.6 %copy-start.4 = (s32[2,1024]{1,0:T(2,128)S(1)}, s32[2,1024]{1,0:T(2,128)}, u32[]{:S(2)}) copy-start(s32[2,1024]{1,0:T(2,128)} %param.8) | copy-start | bytes 24580
  1.1 13.7 %collective-permute-start.3 = (bf16[3,32,2048]{2,1,0:T(8,128)(2,1)S(1)}, bf16[3,32,2048]{2,1,0:T(8,128)(2,1)S(1)}, u32[]{:S(2)}, u32[]{:S(2)}) collective-permute-start(bf16[3,32,2048]{2,1,0:T(8,128)(2,1)S(1)} %slice.25), channel_id=1, source_target_pairs={{0,1},{1,2},{2,3},{4,5},{5,6},{6,7},{8,9},{9,10},{10,11},{12,13},{... | collective-permute-start | bytes 1179656 | tf_op jit(solution)/shard_map/ppermute | solution.py:325
  14.7 0.7 copy-start.1
  25.2 51.9 %all-to-all-start = ((bf16[64,128,128]{2,1,0:T(8,128)(2,1)}), bf16[64,128,128]{2,1,0:T(8,128)(2,1)S(1)}, u32[]{:S(2)}, u32[]{:S(2)}) async-start(bf16[64,128,128]{2,1,0:T(8,128)(2,1)} %bitcast.19), calls=%async_computation | async-start | bytes 4194304 | tf_op jit(solution)/shard_map/all_to_all | solution.py:350
  43.7 32.4 %collective-permute-start = (s32[8,128]{1,0:T(8,128)S(1)}, s32[8,128]{1,0:T(8,128)S(1)}, u32[]{:S(2)}, u32[]{:S(2)}) collective-permute-start(s32[8,128]{1,0:T(8,128)S(1)} %get-tuple-element.15), channel_id=1, source_target_pairs={{0,1},{1,2},{2,3},{3,0},{4,5},{5,6},{6,7},{7,4},{8,9},{9,10},{10,1... | collective-permute-start | bytes 12296 | tf_op jit(solution)/shard_map/ppermute | solution.py:317
  47.0 29.1 %collective-permute-start.1 = (s32[8,128]{1,0:T(8,128)S(1)}, s32[8,128]{1,0:T(8,128)S(1)}, u32[]{:S(2)}, u32[]{:S(2)}) collective-permute-start(s32[8,128]{1,0:T(8,128)S(1)} %get-tuple-element.16), channel_id=1, source_target_pairs={{0,2},{1,3},{2,0},{3,1},{4,6},{5,7},{6,4},{7,5},{8,10},{9,11},{10,... | collective-permute-start | bytes 12296 | tf_op jit(solution)/shard_map/ppermute | solution.py:317
  51.2 24.9 %collective-permute-start.2 = (s32[8,128]{1,0:T(8,128)S(1)}, s32[8,128]{1,0:T(8,128)S(1)}, u32[]{:S(2)}, u32[]{:S(2)}) collective-permute-start(s32[8,128]{1,0:T(8,128)S(1)} %get-tuple-element.17), channel_id=1, source_target_pairs={{0,3},{1,0},{2,1},{3,2},{4,7},{5,4},{6,5},{7,6},{8,11},{9,8},{10,9... | collective-permute-start | bytes 12296 | tf_op jit(solution)/shard_map/ppermute | solution.py:317
  77.0 1.3 %copy-start = (bf16[64,128,128]{2,1,0:T(8,128)(2,1)}, bf16[64,128,128]{2,1,0:T(8,128)(2,1)S(1)}, u32[]{:S(2)}) copy-start(bf16[64,128,128]{2,1,0:T(8,128)(2,1)S(1)} %all-to-all-done.x_ref) | copy-start | bytes 6291460
  90.2 19.6 %all-to-all-start.1 = ((bf16[64,16,128]{2,1,0:T(8,128)(2,1)}), bf16[64,16,128]{2,1,0:T(8,128)(2,1)S(1)}, u32[]{:S(2)}, u32[]{:S(2)}) async-start(bf16[64,16,128]{2,1,0:T(8,128)(2,1)} %bitcast.20), calls=%async_computation.1 | async-start | bytes 524288 | tf_op jit(solution)/shard_map/all_to_all | solution.py:357
  109.8 9.3 %copy-start.2 = (f32[4,16,128]{2,1,0:T(8,128)}, f32[4,16,128]{2,1,0:T(8,128)S(1)}, u32[]{:S(2)}) copy-start(f32[4,16,128]{2,1,0:T(8,128)S(1)} %convert_reduce_fusion) | copy-start | bytes 98308
  109.8 5.3 %collective-permute-start.4 = (f32[64,128]{1,0:T(8,128)S(1)}, f32[64,128]{1,0:T(8,128)S(1)}, u32[]{:S(2)}, u32[]{:S(2)}) collective-permute-start(f32[64,128]{1,0:T(8,128)S(1)} %bitcast.21), channel_id=1, source_target_pairs={{0,1},{1,2},{2,3},{3,0},{4,5},{5,6},{6,7},{7,4},{8,9},{9,10},{10,1... | collective-permute-start | bytes 98312 | tf_op jit(solution)/shard_map/ppermute | solution.py:317
  110.2 6.8 %collective-permute-start.5 = (f32[64,128]{1,0:T(8,128)S(1)}, f32[64,128]{1,0:T(8,128)S(1)}, u32[]{:S(2)}, u32[]{:S(2)}) collective-permute-start(f32[64,128]{1,0:T(8,128)S(1)} %bitcast.22), channel_id=1, source_target_pairs={{0,2},{1,3},{2,0},{3,1},{4,6},{5,7},{6,4},{7,5},{8,10},{9,11},{10,... | collective-permute-start | bytes 98312 | tf_op jit(solution)/shard_map/ppermute | solution.py:317
  111.9 7.2 %collective-permute-start.6 = (f32[64,128]{1,0:T(8,128)S(1)}, f32[64,128]{1,0:T(8,128)S(1)}, u32[]{:S(2)}, u32[]{:S(2)}) collective-permute-start(f32[64,128]{1,0:T(8,128)S(1)} %bitcast.23), channel_id=1, source_target_pairs={{0,3},{1,0},{2,1},{3,2},{4,7},{5,4},{6,5},{7,6},{8,11},{9,8},{10,9... | collective-permute-start | bytes 98312 | tf_op jit(solution)/shard_map/ppermute | solution.py:317
  115.1 4.0 %copy-start.6 = (f32[64,128]{1,0:T(8,128)}, f32[64,128]{1,0:T(8,128)S(1)}, u32[]{:S(2)}) copy-start(f32[64,128]{1,0:T(8,128)S(1)} %collective-permute-done.4.s1_ref) | copy-start | bytes 98308
  116.9 2.2 %copy-start.7 = (f32[64,128]{1,0:T(8,128)}, f32[64,128]{1,0:T(8,128)S(1)}, u32[]{:S(2)}) copy-start(f32[64,128]{1,0:T(8,128)S(1)} %collective-permute-done.5.s2_ref) | copy-start | bytes 98308
  119.1 0.6 copy-start.8
where the time goes:
time: 126 us
  starting transfers between devices  48.6 us (39%)
  Pallas kernels  27.6 us (22%)
  other arithmetic  22.9 us (18%)
  waiting for transfers between devices  22.4 us (18%)
  local copies, waits for them, and re-layouts  4.16 us (3%)
    all_to_all x1, starting transfers between devices, local(): lax.all_to_all(chunks, 'grp', split_axis=0, concat_axis=0, tiled=True)  18.3 us
    cos x1, other arithmetic, beam_weights(): weights = jnp.concatenate([jnp.cos(phases), jnp.sin(phases)], axis=2) * norm  16.4 us
    ppermute x6, starting transfers between devices, from_band(): lax.ppermute(block, 'band', [(i, (i + back) % count) for i in range(count)])  14.7 us
    pallas_call x1, Pallas kernels, beams(): pl.pallas_call(beam_kernel, out_shape=jax.ShapeDtypeStruct((1024, 128), B...  11.8 us
    all_to_all x1, waiting for transfers between devices, local(): owned = lax.all_to_all(sums, 'grp', split_axis=0, concat_axis=0, tiled=True)  9.74 us
    pallas_call x1, Pallas kernels, spectra(): pl.pallas_call(spectra_kernel, out_shape=jax.ShapeDtypeStruct((4, 16, 128...  9.68 us
    all_to_all x1, starting transfers between devices, local(): owned = lax.all_to_all(sums, 'grp', split_axis=0, concat_axis=0, tiled=True)  9.67 us
    ppermute x1, waiting for transfers between devices, local(): lax.ppermute(voltages[local_frames - 3:], 'band', [(i, i + 1) for i in ra...  7.8 us
  transfers between devices with their start and end apart: 9, of which 5 were waited for; matrix products, arithmetic and copies ran while one was open for 19% of the time, Pallas kernels for 0%

commit v1 on v0

v1 whole, which is shorter than its diff:
```python
import math

import jax
import jax.numpy as jnp
import numpy as np
from jax import lax
from jax.experimental import pallas as pl
from jax.experimental.pallas import tpu as pltpu
from jax.sharding import PartitionSpec as P

A = 2048
FEEDS = 1024
C = 1024
SAMP = 2048
BEAMS = 1024
TRIALS = 512
F32 = jnp.float32
BF16 = jnp.bfloat16
NT = (((1,), (1,)), ((), ()))
NN = (((1,), (0,)), ((), ()))


def window_taps():
    tap_pos = np.arange(4 * SAMP) + 0.5
    taper = 0.5 - 0.5 * np.cos(2.0 * np.pi / (4 * SAMP) * tap_pos)
    window = taper * np.sinc((tap_pos - 2 * SAMP) / SAMP)
    window = window * np.sqrt(SAMP / np.sum(window * window))
    return window.reshape(4, SAMP).astype(np.float32)


def lane_tables():
    k = np.arange(64)[:, None]
    lane = np.arange(128)[None, :]

    def rows(r, part):
        angle = 2.0 * np.pi / SAMP * (((16 * k + r) * lane) % SAMP)
        cos, sin = np.cos(angle) / np.sqrt(SAMP), np.sin(angle) / np.sqrt(SAMP)
        if part is not None:
            none = np.zeros_like(cos)
            pair = lambda x: np.concatenate([x, none] if part == 0 else [none, x], axis=1)
            return np.concatenate([pair(cos), pair(-sin)], axis=0)
        sign = -1.0 if r > 8 else 1.0
        top = np.concatenate([cos, -sin * sign], axis=1)
        return np.concatenate([top, np.concatenate([-sin, -cos * sign], axis=1)], axis=0)

    tables = [np.concatenate([rows(0, 0), rows(8, 1)], axis=0)]
    tables += [np.concatenate([rows(at, None), rows(16 - at, None)], axis=0) for at in range(1, 8)]
    return np.stack(tables).astype(jnp.bfloat16)


def real_dft16(x):
    h, c1, c3 = math.sqrt(0.5), math.cos(math.pi / 8), math.cos(3 * math.pi / 8)
    s = [x[j] + x[j + 8] for j in range(8)]
    d = [x[j] - x[j + 8] for j in range(8)]
    ss = [s[j] + s[j + 4] for j in range(4)]
    sd = [s[j] - s[j + 4] for j in range(4)]
    t0, t1 = ss[0] + ss[2], ss[1] + ss[3]
    out = [None] * 9
    out[0] = (t0 + t1, None)
    out[8] = (t0 - t1, None)
    out[4] = (ss[0] - ss[2], ss[1] - ss[3])
    dif, tot = h * (sd[1] - sd[3]), h * (sd[1] + sd[3])
    out[2] = (sd[0] + dif, sd[2] + tot)
    out[6] = (sd[0] - dif, tot - sd[2])
    p = [None] + [d[j] - d[8 - j] for j in (1, 2, 3)]
    q = [None] + [d[j] + d[8 - j] for j in (1, 2, 3)]
    hp, hq = h * p[2], h * q[2]
    ea, eb = d[0] + hp, d[0] - hp
    u, v = c1 * p[1] + c3 * p[3], c3 * p[1] - c1 * p[3]
    fa, fb = d[4] + hq, hq - d[4]
    y, z = c3 * q[1] + c1 * q[3], c1 * q[1] - c3 * q[3]
    out[1] = (ea + u, y + fa)
    out[7] = (ea - u, y - fa)
    out[3] = (eb + v, z + fb)
    out[5] = (eb - v, z - fb)
    return out


def frame_bins(part_ref, win_ref, row0, a0, frame, keep=None):
    lanes = []
    for jb in range(16):
        cols = slice(128 * jb, 128 * jb + 128)
        total = None
        for p in range(4):
            term = frame(p)[pl.ds(a0, 16), cols].astype(F32) * win_ref[p : p + 1, cols]
            if p == 3 and keep is not None:
                total = total * keep
            total = term if total is None else total + term
        lanes.append(total)
    rows = pl.ds(row0, 16)
    for at, (re, im) in enumerate(real_dft16(lanes)):
        if at % 8 == 0:
            part_ref[0, rows, 16 * at : 16 * at + 128] = re.astype(BF16)
        else:
            part_ref[at, rows, 0:128] = re.astype(BF16)
            part_ref[at, rows, 128:256] = im.astype(BF16)


def inner_kernel(v_ref, win_ref, part_ref):
    def body(step, carry):
        m = step // 2
        a0 = pl.multiple_of(16 * (step % 2), 16)
        frame_bins(part_ref, win_ref, pl.multiple_of(16 * step, 16), a0, lambda p: v_ref.at[m - 2 + p])
        return carry

    lax.fori_loop(4, 30, body, 0)


def spectra_kernel(
    band_ref, part_hbm, v_ref, prev_ref, next_ref, win_ref, tab_ref, out_ref, part_ref, turn_ref, sem
):
    inner = pl.ds(64, 416)
    fetch = pltpu.make_async_copy(part_hbm.at[:, inner, :], part_ref.at[:, inner, :], sem)
    fetch.start()
    keep = jnp.where(band_ref[0] == 3, 0.0, 1.0).astype(F32)

    def edge(half, carry):
        a0 = pl.multiple_of(16 * half, 16)
        for m in (0, 1):
            frame = lambda p, m=m: prev_ref.at[m + p] if m + p < 2 else v_ref.at[m + p - 2]
            frame_bins(part_ref, win_ref, pl.multiple_of(32 * m + a0, 16), a0, frame)
        frame = lambda p: v_ref.at[13 + p] if p < 3 else next_ref.at[0]
        frame_bins(part_ref, win_ref, pl.multiple_of(480 + a0, 16), a0, frame, keep)
        return carry

    lax.fori_loop(0, 2, edge, 0)
    fetch.wait()

    def transform(at, carry):
        rows = lax.dot_general(tab_ref[at], part_ref[at], NT, preferred_element_type=F32)
        for which in range(2):
            for reim in range(2):
                for mb in range(4):
                    r0 = 128 * which + 64 * reim
                    turn_ref[which, pl.ds(reim * 4 + mb, 64, stride=8), :] = rows[
                        r0 : r0 + 64, 128 * mb : 128 * mb + 128
                    ]
        for which in range(2):
            r = at if which == 0 else jnp.where(at == 0, 8, 16 - at)
            for q in range(4):
                out_ref[r, q] = turn_ref[which, 128 * q : 128 * q + 128, :].astype(BF16)
        return carry

    lax.fori_loop(0, 8, transform, 0)


def spectra(voltages, band_at):
    band_count = lax.axis_size("band")
    ahead = lax.ppermute(voltages[14:16], "band", [(i, i + 1) for i in range(band_count - 1)])
    behind = lax.ppermute(voltages[0:1], "band", [(i, (i - 1) % band_count) for i in range(band_count)])
    window, tables = jnp.asarray(window_taps()), jnp.asarray(lane_tables())
    vmem, smem = pl.BlockSpec(memory_space=pltpu.VMEM), pl.BlockSpec(memory_space=pltpu.SMEM)
    parts = pl.pallas_call(
        inner_kernel,
        name="inner_frames",
        out_shape=jax.ShapeDtypeStruct((8, 512, 256), BF16),
        in_specs=[vmem] * 2,
        out_specs=vmem,
        cost_estimate=pl.CostEstimate(flops=20_000_000, bytes_accessed=4_000_000, transcendentals=0),
    )(voltages, window)
    return pl.pallas_call(
        spectra_kernel,
        name="spectra",
        out_shape=jax.ShapeDtypeStruct((16, 4, 128, 128), BF16),
        in_specs=[smem, pl.BlockSpec(memory_space=pl.ANY)] + [vmem] * 5,
        out_specs=vmem,
        scratch_shapes=[
            pltpu.VMEM((8, 512, 256), BF16),
            pltpu.VMEM((2, 512, 128), F32),
            pltpu.SemaphoreType.DMA,
        ],
        cost_estimate=pl.CostEstimate(
            flops=600_000_000, bytes_accessed=6_000_000, transcendentals=0
        ),
    )(band_at.reshape(1), parts, voltages, ahead, behind, window, tables)


def turn_blocks(tiles):
    lane = lax.broadcasted_iota(jnp.int32, tiles[0].shape, 1)
    odd, high = (lane // 32) % 2 == 1, lane // 64 == 1
    one = [None] * 4
    for a, b in ((0, 1), (2, 3)):
        one[a] = jnp.where(odd, pltpu.roll(tiles[b], 32, 1), tiles[a])
        one[b] = jnp.where(odd, tiles[b], pltpu.roll(tiles[a], 96, 1))
    two = [None] * 4
    for a, b in ((0, 2), (1, 3)):
        two[a] = jnp.where(high, pltpu.roll(one[b], 64, 1), one[a])
        two[b] = jnp.where(high, one[b], pltpu.roll(one[a], 64, 1))
    return two


def beam_kernel(
    east_ref, sub_ref, x_ref, w_ref, hot_hbm, out_ref, left_ref, prod_ref, acc_ref, hot_ref, sem
):
    step = pl.program_id(0)
    fetch = pltpu.make_async_copy(hot_hbm, hot_ref, sem)

    @pl.when(step == 0)
    def _():
        fetch.start()
        acc_ref[...] = jnp.zeros_like(acc_ref)

    low = lax.broadcasted_iota(jnp.int32, (8, 128), 0) < 4
    row0 = pl.multiple_of(16 * step, 16)
    for pe in range(8):
        for h in range(2):
            src = pe * 8 + h * 4
            tiles = turn_blocks([x_ref[src + n, pl.ds(row0, 16), :] for n in range(4)])
            tiles = [t.astype(F32) for t in tiles]
            for ch in range(2):
                one = [t[8 * ch : 8 * ch + 8] for t in tiles]
                re = [jnp.where(low, one[a], pltpu.roll(one[a + 1], 4, 0)) for a in (0, 2)]
                im = [jnp.where(low, pltpu.roll(one[a], 4, 0), one[a + 1]) for a in (0, 2)]
                re, im = jnp.concatenate(re, axis=0), jnp.concatenate(im, axis=0)
                rows, cols = slice(16 * pe, 16 * pe + 16), slice(128 * h, 128 * h + 128)
                more = slice(256 + 128 * h, 384 + 128 * h)
                left_ref[ch, 0, rows, cols] = re.astype(BF16)
                left_ref[ch, 0, rows, more] = (-im).astype(BF16)
                left_ref[ch, 1, rows, cols] = re.astype(BF16)
                left_ref[ch, 1, rows, more] = im.astype(BF16)
    for ch in range(2):
        for part in range(2):
            prod_ref[ch, part] = lax.dot_general(
                left_ref[ch, part], w_ref[ch, 256 * part : 256 * part + 512, :], NN, preferred_element_type=F32
            )
    for ch in range(2):
        i = 2 * step + ch
        sub = sub_ref[i]
        cos = [[east_ref[i, s * 4 + e] for e in range(4)] for s in range(4)]
        sin = [[east_ref[i, 16 + s * 4 + e] for e in range(4)] for s in range(4)]
        for t in range(2):
            for h in range(2):
                power = [None] * 4
                for p in range(2):
                    re, im = [], []
                    for e in range(4):
                        r0 = p * 64 + e * 16 + t * 8
                        re.append(prod_ref[ch, 0, r0 : r0 + 8, 128 * h : 128 * h + 128])
                        im.append(prod_ref[ch, 1, r0 : r0 + 8, 128 * h : 128 * h + 128])
                    for s in range(4):
                        beam_re, beam_im = re[0], im[0]
                        for e in range(1, 4):
                            if s == 0:
                                beam_re, beam_im = beam_re + re[e], beam_im + im[e]
                            else:
                                c, d = cos[s][e], sin[s][e]
                                beam_re = beam_re + (c * re[e] - d * im[e])
                                beam_im = beam_im + (c * im[e] + d * re[e])
                        square = beam_re * beam_re + beam_im * beam_im
                        power[s] = square if p == 0 else power[s] + square
                for s in range(4):
                    cols = slice(s * 256 + h * 128, s * 256 + h * 128 + 128)
                    acc_ref[sub, 8 * t : 8 * t + 8, cols] += power[s]

    @pl.when(step == pl.num_programs(0) - 1)
    def _():
        total = acc_ref[...].reshape(64, 1024)
        top = total.astype(BF16)
        rest = (total - top.astype(F32)).astype(BF16)
        parts = jnp.concatenate([top, rest], axis=0)
        fetch.wait()
        out_ref[...] = lax.dot_general(hot_ref[...], parts, NT, preferred_element_type=F32).astype(BF16)


def beams(turned, east, subs, weights, hot):
    smem = pl.BlockSpec(memory_space=pltpu.SMEM)
    return pl.pallas_call(
        beam_kernel,
        name="beams",
        grid=(8,),
        out_shape=jax.ShapeDtypeStruct((1024, 128), BF16),
        in_specs=[
            smem,
            smem,
            pl.BlockSpec((64, 128, 128), lambda i: (0, 0, 0)),
            pl.BlockSpec((2, 768, 256), lambda i: (i, 0, 0)),
            pl.BlockSpec(memory_space=pl.ANY),
        ],
        out_specs=pl.BlockSpec((1024, 128), lambda i: (0, 0)),
        scratch_shapes=[
            pltpu.VMEM((2, 2, 128, 512), BF16),
            pltpu.VMEM((2, 2, 128, 256), F32),
            pltpu.VMEM((4, 16, 1024), F32),
            pltpu.VMEM((1024, 1024), BF16),
            pltpu.SemaphoreType.DMA,
        ],
        cost_estimate=pl.CostEstimate(
            flops=2_000_000_000, bytes_accessed=11_000_000, transcendentals=0
        ),
    )(east, subs, turned, weights, hot)


def beam_weights(channels):
    scale = 2 * C
    steps = scale - channels
    north = jnp.arange(256, dtype=jnp.int32)
    turns = steps[:, None, None] * (north[:, None] * north[None, :])[None] % (scale * 256)
    phases = (2.0 * math.pi / (scale * 256)) * turns.astype(F32)
    norm = 1.0 / math.sqrt(FEEDS)
    cos, sin = (jnp.cos(phases) * norm).astype(BF16), (jnp.sin(phases) * norm).astype(BF16)
    four = jnp.arange(4, dtype=jnp.int32)
    turns = steps[:, None] * (four[:, None] * four[None, :]).reshape(1, 16) % (scale * 4)
    phases = (2.0 * math.pi / (scale * 4)) * turns.astype(F32)
    return jnp.concatenate([cos, sin, cos], axis=1), jnp.concatenate([jnp.cos(phases), jnp.sin(phases)], axis=1)


def gather_kernel(x_ref, out_ref):
    total = x_ref[0].astype(F32)
    for r in range(1, 16):
        total = total + x_ref[r].astype(F32)
    total = total + pltpu.roll(total, 64, 1)
    top = total.astype(BF16)
    rest = (total - top.astype(F32)).astype(BF16)
    lane = lax.broadcasted_iota(jnp.int32, (64, 128), 1)
    both = jnp.where(lane < 64, top, rest)
    for q in range(4):
        for band in range(4):
            out_ref[4 * q + band] = both[16 * q : 16 * q + 16, :]


def gather_residues(pieces):
    vmem = pl.BlockSpec(memory_space=pltpu.VMEM)
    return pl.pallas_call(
        gather_kernel,
        name="residues",
        out_shape=jax.ShapeDtypeStruct((16, 16, 128), BF16),
        in_specs=[vmem],
        out_specs=vmem,
    )(pieces)


def frame_tables():
    table = np.zeros((4, 2, 4, 4, 4, 4, 64), np.float32)
    for band in range(4):
        for m4 in range(4):
            for mb in range(4):
                row = np.full(64, -1.0 / 64.0)
                row[(16 * band + 1 + 4 * mb + m4) % 64] += 1.0
                for sub in range(4):
                    table[band, :, sub, m4, mb, sub, :] = row / math.sqrt(C)
    return table.reshape(4, 128, 256).astype(jnp.bfloat16)


def series_kernel(x_ref, tab_ref, delay_ref, out_ref, hot_ref, left_ref):
    series = None
    for band in range(4):
        rows = jnp.concatenate([x_ref[4 * q + band] for q in range(4)], axis=0)
        term = lax.dot_general(rows, tab_ref[band], NN, preferred_element_type=F32)
        series = term if series is None else series + term
    ahead = lax.broadcasted_iota(jnp.int32, (64, 128), 0)
    for s in range(16):
        hit = (ahead + delay_ref[s : s + 1, :]) % 64 == 0
        hot = jnp.where(hit, 1.0, 0.0).astype(BF16)
        for th in range(4):
            cols = slice(128 * th, 128 * th + 128)
            for tile in range(4):
                to = 64 * s + 16 * tile
                at = 16 * ((tile - th) % 4)
                hot_ref[to : to + 16, cols] = hot[at : at + 16, :]
    lane = lax.broadcasted_iota(jnp.int32, (16, 128), 1) % 64
    for at in range(8):
        rows, cols = slice(16 * (at // 2), 16 * (at // 2) + 16), slice(128 * (at % 2), 128 * (at % 2) + 128)
        block = series[rows, cols]
        for t in range(16):
            x = block
            if t:
                x = jnp.where(lane < 64 - t, pltpu.roll(x, 128 - t, 1), pltpu.roll(x, 64 - t, 1))
            top = x.astype(BF16)
            left_ref[0, 16 * t : 16 * t + 16, 128 * at : 128 * at + 128] = top
            left_ref[1, 16 * t : 16 * t + 16, 128 * at : 128 * at + 128] = (x - top.astype(F32)).astype(BF16)
    hot = hot_ref[...]
    out = lax.dot_general(left_ref[0], hot, NN, preferred_element_type=F32)
    out = out + lax.dot_general(left_ref[1], hot, NN, preferred_element_type=F32)
    for th in range(4):
        out_ref[16 * th : 16 * th + 16] = out[:, 128 * th : 128 * th + 128].reshape(16, 16, 128)


def series(sums, delays):
    vmem = pl.BlockSpec(memory_space=pltpu.VMEM)
    return pl.pallas_call(
        series_kernel,
        name="series",
        out_shape=jax.ShapeDtypeStruct((64, 16, 128), F32),
        in_specs=[vmem] * 3,
        out_specs=vmem,
        scratch_shapes=[pltpu.VMEM((1024, 512), BF16), pltpu.VMEM((2, 256, 1024), BF16)],
        cost_estimate=pl.CostEstimate(
            flops=600_000_000, bytes_accessed=1_000_000, transcendentals=0
        ),
    )(sums, jnp.asarray(frame_tables()), delays)


def from_band(block, back):
    count = lax.axis_size("band")
    return lax.ppermute(block, "band", [(i, (i + back) % count) for i in range(count)])


def local(voltages, steering, chan_sub, delays):
    groups, band_count = lax.axis_size("grp"), lax.axis_size("band")
    grp_at = lax.axis_index("grp")
    band_at = lax.axis_index("band")
    turned_delays = jnp.transpose(delays)
    small = []
    for back in range(band_count):
        trials = lax.dynamic_slice_in_dim(
            turned_delays, (band_at + back) % band_count * 128, 128, axis=1
        )
        note = jnp.concatenate([chan_sub.reshape(2, 128), jnp.zeros((2, 128), jnp.int32), trials])
        small.append(note if back == 0 else from_band(note, back))
    quarter_at = grp_at % 4
    residue = grp_at // 4

    def owned_by(owner):
        found = small[0] * 0
        for back in range(band_count):
            found = found + jnp.where((band_at - back) % band_count == owner, small[back], 0)
        return found

    quarter_subs = owned_by(quarter_at)[0:2].reshape(16, 16)
    subs = lax.dynamic_slice_in_dim(quarter_subs, residue, 1, axis=1).reshape(16) % 4
    all_delays = jnp.concatenate([owned_by(owner)[4:8] for owner in range(band_count)])

    chunks = spectra(voltages, band_at).reshape(64, 128, 128)
    turned = lax.all_to_all(chunks, "grp", split_axis=0, concat_axis=0, tiled=True)

    channels = quarter_at * 256 + 16 * jnp.arange(16, dtype=jnp.int32) + residue
    weights, east = beam_weights(channels)
    grid_at = steering[1] * 256 + steering[0]
    hot = (grid_at[:, None] == jnp.arange(1024, dtype=jnp.int32)[None, :]).astype(BF16)
    sums = beams(turned, east, subs, weights, hot).reshape(16, 64, 128)
    planes = [[4 * r + q for r in range(groups // 4)] for q in range(4)]
    pieces = lax.all_to_all(
        sums, "grp", split_axis=0, concat_axis=0, tiled=True, axis_index_groups=planes
    )
    columns = [
        [(4 * r + q) * band_count + band for q in range(4) for band in range(band_count)]
        for r in range(groups // 4)
    ]
    every = lax.all_to_all(
        gather_residues(pieces),
        ("grp", "band"),
        split_axis=0,
        concat_axis=0,
        tiled=True,
        axis_index_groups=columns,
    )
    return series(every, all_delays)


def solution(mesh):
    in_specs = (P("band", "grp", None), P(), P("band"), P(None, "band"))
    out_specs = P(None, "grp", "band")
    return jax.shard_map(local, mesh=mesh, in_specs=in_specs, out_specs=out_specs, check_vma=False)
```

time: 126 us -> 120 us (0.952)
  starting transfers between devices: 48.6 us -> 40.8 us
  waiting for transfers between devices: 22.4 us -> 17.7 us
  other arithmetic: 22.9 us -> 27.1 us
  local copies, waits for them, and re-layouts: 4.16 us -> 5.76 us
    cos x1 -> x0, other arithmetic: 16.4 us -> none  [beam_weights(): weights = jnp.concatenate([jnp.cos(phases), jnp.sin(phases)], axis=2) * norm]
    convert_element_type x1, other arithmetic: 2.41 us -> 17.2 us  [beam_weights(): (jnp.sin(phases) * norm).astype(BF16)]
    all_to_all x1, starting transfers between devices: 18.3 us -> 9 us  [local(): lax.all_to_all(chunks, 'grp', split_axis=0, concat_axis=0, tiled=True)]
    concatenate x0 -> x1, other arithmetic: none -> 5.84 us  [beam_weights(): jnp.concatenate([cos, sin, cos], axis=1)]
    all_to_all x1 -> x2, waiting for transfers between devices: 9.74 us -> 14.6 us  [the longest x1 7.42 us: local(): lax.all_to_all(sums, 'grp', split_axis=0, concat_axis=0, tiled=True, axis...]
    ppermute x6 -> x3, waiting for transfers between devices: 4.81 us -> 0.01 us  [from_band(): lax.ppermute(block, 'band', [(i, (i + back) % count) for i in range(count)])]
    ppermute x1 -> x2, waiting for transfers between devices: 7.8 us -> 3.14 us  [the longest x1 3.14 us: spectra(): lax.ppermute(voltages[0:1], 'band', [(i, (i - 1) % band_count) for i in r...]
    ppermute x6 -> x3, starting transfers between devices: 14.7 us -> 10.8 us  [from_band(): lax.ppermute(block, 'band', [(i, (i + back) % count) for i in range(count)])]
  transfers between devices with their start and end apart: 9 -> 8, of which waited for: 5 -> 3; matrix products, arithmetic and copies ran while one was open for 19% -> 24% of each run, Pallas kernels for 0% -> 4%
where the time goes in v1:
time: 120 us; the launch traced here: 119 us
  starting transfers between devices  40.8 us (34%)
  Pallas kernels  27.2 us (23%)
  other arithmetic  27.1 us (23%)
  waiting for transfers between devices  17.7 us (15%)
  local copies, waits for them, and re-layouts  5.76 us (5%)
    convert_element_type x1, other arithmetic, beam_weights(): (jnp.sin(phases) * norm).astype(BF16)  17.2 us
    ppermute x3, starting transfers between devices, from_band(): lax.ppermute(block, 'band', [(i, (i + back) % count) for i in range(count)])  10.8 us
    pallas_call x1, Pallas kernels, beams(): pl.pallas_call(beam_kernel, name='beams', grid=(8,), out_shape=jax.ShapeD...  10.2 us
    all_to_all x1, starting transfers between devices, local(): lax.all_to_all(chunks, 'grp', split_axis=0, concat_axis=0, tiled=True)  9 us
    all_to_all x1, waiting for transfers between devices, local(): lax.all_to_all(sums, 'grp', split_axis=0, concat_axis=0, tiled=True, axis...  7.42 us
    pallas_call x1, Pallas kernels, spectra(): pl.pallas_call(spectra_kernel, name='spectra', out_shape=jax.ShapeDtypeSt...  7.25 us
    all_to_all x1, waiting for transfers between devices, local(): lax.all_to_all(gather_residues(pieces), ('grp', 'band'), split_axis=0, co...  7.13 us
    all_to_all x1, starting transfers between devices, local(): lax.all_to_all(sums, 'grp', split_axis=0, concat_axis=0, tiled=True, axis...  6.81 us
  transfers between devices with their start and end apart: 8, of which 3 were waited for; matrix products, arithmetic and copies ran while one was open for 24% of the time, Pallas kernels for 4%

profile of v1, /device:TPU:1, one launch (start us, length us, event | category | flops | bytes accessed | tf_op | source)
XLA Modules:
  0.0 118.9 jit_solution(8774890827246323478)
XLA Ops:
  0.0 1.0 slice.28
  1.0 5.7 %collective-permute-start.3 = (bf16[2,32,2048]{2,1,0:T(8,128)(2,1)S(1)}, bf16[2,32,2048]{2,1,0:T(8,128)(2,1)S(1)}, u32[]{:S(2)}, u32[]{:S(2)}) collective-permute-start(bf16[2,32,2048]{2,1,0:T(8,128)(2,1)S(1)} %slice.28), channel_id=1, source_target_pairs={{0,1},{1,2},{2,3},{4,5},{5,6},{6,7},{8,9},{9,10},{10,11},{12,13},{... | collective-permute-start | bytes 786440 | tf_op jit(solution)/shard_map/ppermute | solution.py:149
  6.7 0.9 slice.29
  7.6 2.5 %collective-permute-start.4 = (bf16[1,32,2048]{2,1,0:T(8,128)(2,1)S(1)}, bf16[1,32,2048]{2,1,0:T(8,128)(2,1)S(1)}, u32[]{:S(2)}, u32[]{:S(2)}) collective-permute-start(bf16[1,32,2048]{2,1,0:T(8,128)(2,1)S(1)} %slice.29), channel_id=1, source_target_pairs={{0,3},{1,0},{2,1},{3,2},{4,7},{5,4},{6,5},{7,6},{8,11},{9,8},{10,9... | collective-permute-start | bytes 393224 | tf_op jit(solution)/shard_map/ppermute | solution.py:150
  10.1 5.0 %inner_frames.1.part_hbm = bf16[8,512,256]{2,1,0:T(8,128)(2,1)} custom-call(bf16[16,32,2048]{2,1,0:T(8,128)(2,1)} %v_ref.3, f32[4,2048]{1,0:T(4,128)} %constant.167.clone.win_ref), custom_call_target="tpu_custom_call" | custom-call | flops 20000000 | bytes 4000000 | tf_op jit(solution)/shard_map/inner_frames/pallas_call | solution.py:153
  15.1 3.1 %collective-permute-done.4.next_ref = bf16[1,32,2048]{2,1,0:T(8,128)(2,1)S(1)} collective-permute-done((bf16[1,32,2048]{2,1,0:T(8,128)(2,1)S(1)}, bf16[1,32,2048]{2,1,0:T(8,128)(2,1)S(1)}, u32[]{:S(2)}, u32[]{:S(2)}) %collective-permute-start.4) | collective-permute-done | bytes 131104 | tf_op jit(solution)/shard_map/ppermute | solution.py:150
  18.2 0.0 copy-start.3
  18.2 0.0 collective-permute-done.3.prev_ref
  18.2 0.0 copy-start.2
  18.2 0.7 copy-done.3
  18.9 0.1 copy-done.2
  19.0 0.0 copy-start.7
  19.0 0.0 copy-start.5
  19.0 7.2 %spectra.1 = bf16[16,4,128,128]{3,2,1,0:T(8,128)(2,1)} custom-call(s32[1]{0:T(128)} %bitcast.6.band_ref, bf16[8,512,256]{2,1,0:T(8,128)(2,1)} %inner_frames.1.part_hbm, bf16[16,32,2048]{2,1,0:T(8,128)(2,1)} %v_ref.3, bf16[2,32,2048]{2,1,0:T(8,128)(2,1)} %copy-done.2, bf16[1,32,2048]{2,1,0:T(8,128)(2,1)} %copy-done.3, f32[4,2048]{1,0:T(4,128)} %constant.167.clone.win_ref, ...), custom_call_target="tpu_custom_call" | custom-call | flops 600000000 | bytes 6000000 | tf_op jit(solution)/shard_map/spectra/pallas_call | solution.py:161
  26.2 0.0 copy-start.6
  26.2 9.0 %all-to-all-start = ((bf16[64,128,128]{2,1,0:T(8,128)(2,1)}), bf16[64,128,128]{2,1,0:T(8,128)(2,1)S(1)}, u32[]{:S(2)}, u32[]{:S(2)}) async-start(bf16[64,128,128]{2,1,0:T(8,128)(2,1)} %bitcast.15), calls=%async_computation | async-start | bytes 4194304 | tf_op jit(solution)/shard_map/all_to_all | solution.py:424
  35.3 0.1 pad.17.clone
  35.4 0.0 copy-done.7
  35.4 0.0 copy-done.5
  35.4 0.1 fusion.9
  35.5 3.2 %collective-permute-start = (s32[8,128]{1,0:T(8,128)S(1)}, s32[8,128]{1,0:T(8,128)S(1)}, u32[]{:S(2)}, u32[]{:S(2)}) collective-permute-start(s32[8,128]{1,0:T(8,128)S(1)} %get-tuple-element.15), channel_id=1, source_target_pairs={{0,1},{1,2},{2,3},{3,0},{4,5},{5,6},{6,7},{7,4},{8,9},{9,10},{10,1... | collective-permute-start | bytes 12296 | tf_op jit(solution)/shard_map/ppermute | solution.py:395
  38.7 4.2 %collective-permute-start.1 = (s32[8,128]{1,0:T(8,128)S(1)}, s32[8,128]{1,0:T(8,128)S(1)}, u32[]{:S(2)}, u32[]{:S(2)}) collective-permute-start(s32[8,128]{1,0:T(8,128)S(1)} %get-tuple-element.16), channel_id=1, source_target_pairs={{0,2},{1,3},{2,0},{3,1},{4,6},{5,7},{6,4},{7,5},{8,10},{9,11},{10,... | collective-permute-start | bytes 12296 | tf_op jit(solution)/shard_map/ppermute | solution.py:395
  42.9 3.4 %collective-permute-start.2 = (s32[8,128]{1,0:T(8,128)S(1)}, s32[8,128]{1,0:T(8,128)S(1)}, u32[]{:S(2)}, u32[]{:S(2)}) collective-permute-start(s32[8,128]{1,0:T(8,128)S(1)} %get-tuple-element.17), channel_id=1, source_target_pairs={{0,3},{1,0},{2,1},{3,2},{4,7},{5,4},{6,5},{7,6},{8,11},{9,8},{10,9... | collective-permute-start | bytes 12296 | tf_op jit(solution)/shard_map/ppermute | solution.py:395
  46.3 0.1 mul.124
  46.4 0.0 copy-done.6
  46.4 0.1 fusion.11
  46.6 1.8 %fusion.3.hot_hbm = bf16[1024,1024]{1,0:T(8,128)(2,1)} fusion(s32[1024]{0:T(1024)S(1)} %bitcast.17), kind=kLoop, calls=%fused_computation.12 | loop fusion | flops 2097152 | bytes 2101248 | tf_op jit(solution)/shard_map/convert_element_type | solution.py:429
  48.4 17.2 %multiply_convert_fusion = (bf16[16,256,256]{2,1,0:T(8,128)(2,1)S(1)}, bf16[16,256,256]{2,1,0:T(8,128)(2,1)S(1)}) fusion(s32[256,256]{1,0:T(8,128)S(1)} %iota_multiply_fusion, s32[16]{0:T(128)S(1)} %add_subtract_fusion), kind=kLoop, calls=%fused_computation.10 | loop fusion | flops 18874368 | bytes 4456512 | tf_op jit(solution)/shard_map/convert_element_type | solution.py:300
  65.5 5.8 %pad_maximum_fusion.w_ref = bf16[16,768,256]{2,1,0:T(8,128)(2,1)} fusion(bf16[16,256,256]{2,1,0:T(8,128)(2,1)S(1)} %get-tuple-element.6, bf16[16,256,256]{2,1,0:T(8,128)(2,1)S(1)} %get-tuple-element.5), kind=kLoop, calls=%fused_computation.3 | loop fusion | flops 18874368 | bytes 10485760 | tf_op jit(solution)/shard_map/concatenate | solution.py:304
  71.4 0.7 pad_maximum_fusion.1.east_ref
  72.0 0.0 collective-permute-done
  72.0 0.0 collective-permute-done.1
  72.0 0.0 collective-permute-done.2
  72.0 0.1 select_add_fusion.4
  72.1 0.1 reshape.76
  72.2 0.1 constant_dynamic-slice_fusion
  72.3 0.1 copy.9
  72.4 0.6 and_select_fusion.sub_ref
  73.0 0.0 all-to-all-done.x_ref
  73.0 0.0 copy-start
  73.0 1.4 %copy-done = bf16[64,128,128]{2,1,0:T(8,128)(2,1)} copy-done((bf16[64,128,128]{2,1,0:T(8,128)(2,1)}, bf16[64,128,128]{2,1,0:T(8,128)(2,1)S(1)}, u32[]{:S(2)}) %copy-start) | copy-done | bytes 2097176
  74.4 10.2 %beams.1 = bf16[1024,128]{1,0:T(8,128)(2,1)} custom-call(f32[16,32]{1,0:T(8,128)} %pad_maximum_fusion.1.east_ref, s32[16]{0:T(128)} %and_select_fusion.sub_ref, bf16[64,128,128]{2,1,0:T(8,128)(2,1)} %copy-done, bf16[16,768,256]{2,1,0:T(8,128)(2,1)} %pad_maximum_fusion.w_ref, bf16[1024,1024]{1,0:T(8,128)(2,1)} %fusion.3.hot_hbm), custom_call_target="tpu_custom_call" | custom-call | flops 2000000000 | bytes 11000000 | tf_op jit(solution)/shard_map/beams/pallas_call | solution.py:267
  84.6 6.8 %all-to-all-start.1 = ((bf16[16,64,128]{2,1,0:T(8,128)(2,1)}), bf16[16,64,128]{2,1,0:T(8,128)(2,1)S(1)}, u32[]{:S(2)}, u32[]{:S(2)}) async-start(bf16[16,64,128]{2,1,0:T(8,128)(2,1)} %bitcast.16), calls=%async_computation.1 | async-start | bytes 524288 | tf_op jit(solution)/shard_map/all_to_all | solution.py:432
  91.4 0.1 select_add_fusion.3
  91.5 7.4 %all-to-all-done.1.x_ref = bf16[16,64,128]{2,1,0:T(8,128)(2,1)S(1)} async-done(((bf16[16,64,128]{2,1,0:T(8,128)(2,1)}), bf16[16,64,128]{2,1,0:T(8,128)(2,1)S(1)}, u32[]{:S(2)}, u32[]{:S(2)}) %all-to-all-start.1) | async-done | bytes 262176 | tf_op jit(solution)/shard_map/all_to_all | solution.py:432
  98.9 0.0 copy-start.1
  98.9 0.7 copy-done.1
  99.6 1.7 %residues.1 = bf16[16,16,128]{2,1,0:T(8,128)(2,1)} custom-call(bf16[16,64,128]{2,1,0:T(8,128)(2,1)} %copy-done.1), custom_call_target="tpu_custom_call" | custom-call | tf_op jit(solution)/shard_map/residues/pallas_call | solution.py:323
  101.3 5.9 %all-to-all-start.2 = ((bf16[16,16,128]{2,1,0:T(8,128)(2,1)}), bf16[16,16,128]{2,1,0:T(8,128)(2,1)S(1)}, u32[]{:S(2)}, u32[]{:S(2)}) async-start(bf16[16,16,128]{2,1,0:T(8,128)(2,1)} %residues.1), calls=%async_computation.2 | async-start | bytes 131072 | tf_op jit(solution)/shard_map/all_to_all | solution.py:439
  107.3 0.1 select_add_fusion.2
  107.4 0.6 pad_add_fusion.delay_ref
  108.0 7.1 %all-to-all-done.2.x_ref = bf16[16,16,128]{2,1,0:T(8,128)(2,1)S(1)} async-done(((bf16[16,16,128]{2,1,0:T(8,128)(2,1)}), bf16[16,16,128]{2,1,0:T(8,128)(2,1)S(1)}, u32[]{:S(2)}, u32[]{:S(2)}) %all-to-all-start.2) | async-done | bytes 65568 | tf_op jit(solution)/shard_map/all_to_all | solution.py:439
  115.1 0.0 copy-start.4
  115.1 0.6 copy-done.4
  115.7 3.1 %series.1 = f32[64,16,128]{2,1,0:T(8,128)} custom-call(bf16[16,16,128]{2,1,0:T(8,128)(2,1)} %copy-done.4, bf16[4,128,256]{2,1,0:T(8,128)(2,1)} %constant.169.clone.tab_ref, s32[16,128]{1,0:T(8,128)} %pad_add_fusion.delay_ref), custom_call_target="tpu_custom_call" | custom-call | flops 600000000 | bytes 1000000 | tf_op jit(solution)/shard_map/series/pallas_call | solution.py:380
  (11 shorter events, 0.1 us)
Async XLA Ops:
  1.0 17.2 %collective-permute-start.3 = (bf16[2,32,2048]{2,1,0:T(8,128)(2,1)S(1)}, bf16[2,32,2048]{2,1,0:T(8,128)(2,1)S(1)}, u32[]{:S(2)}, u32[]{:S(2)}) collective-permute-start(bf16[2,32,2048]{2,1,0:T(8,128)(2,1)S(1)} %slice.28), channel_id=1, source_target_pairs={{0,1},{1,2},{2,3},{4,5},{5,6},{6,7},{8,9},{9,10},{10,11},{12,13},{... | collective-permute-start | bytes 786440 | tf_op jit(solution)/shard_map/ppermute | solution.py:149
  7.6 10.6 %collective-permute-start.4 = (bf16[1,32,2048]{2,1,0:T(8,128)(2,1)S(1)}, bf16[1,32,2048]{2,1,0:T(8,128)(2,1)S(1)}, u32[]{:S(2)}, u32[]{:S(2)}) collective-permute-start(bf16[1,32,2048]{2,1,0:T(8,128)(2,1)S(1)} %slice.29), channel_id=1, source_target_pairs={{0,3},{1,0},{2,1},{3,2},{4,7},{5,4},{6,5},{7,6},{8,11},{9,8},{10,9... | collective-permute-start | bytes 393224 | tf_op jit(solution)/shard_map/ppermute | solution.py:150
  18.2 0.7 copy-start.3
  18.2 0.7 copy-start.2
  19.0 16.4 %copy-start.7 = (s32[512,4]{0,1:T(4,128)S(1)}, s32[512,4]{0,1:T(4,128)}, u32[]{:S(2)}) copy-start(s32[512,4]{0,1:T(4,128)} %param.10) | copy-start | bytes 24580
  19.0 16.4 %copy-start.5 = (s32[256]{0:T(256)S(1)}, s32[256]{0:T(256)}, u32[]{:S(2)}) copy-start(s32[256]{0:T(256)} %param.9) | copy-start | bytes 3076
  26.2 20.2 %copy-start.6 = (s32[2,1024]{1,0:T(2,128)S(1)}, s32[2,1024]{1,0:T(2,128)}, u32[]{:S(2)}) copy-start(s32[2,1024]{1,0:T(2,128)} %param.8) | copy-start | bytes 24580
  26.2 46.8 %all-to-all-start = ((bf16[64,128,128]{2,1,0:T(8,128)(2,1)}), bf16[64,128,128]{2,1,0:T(8,128)(2,1)S(1)}, u32[]{:S(2)}, u32[]{:S(2)}) async-start(bf16[64,128,128]{2,1,0:T(8,128)(2,1)} %bitcast.15), calls=%async_computation | async-start | bytes 4194304 | tf_op jit(solution)/shard_map/all_to_all | solution.py:424
  35.5 36.6 %collective-permute-start = (s32[8,128]{1,0:T(8,128)S(1)}, s32[8,128]{1,0:T(8,128)S(1)}, u32[]{:S(2)}, u32[]{:S(2)}) collective-permute-start(s32[8,128]{1,0:T(8,128)S(1)} %get-tuple-element.15), channel_id=1, source_target_pairs={{0,1},{1,2},{2,3},{3,0},{4,5},{5,6},{6,7},{7,4},{8,9},{9,10},{10,1... | collective-permute-start | bytes 12296 | tf_op jit(solution)/shard_map/ppermute | solution.py:395
  38.7 33.4 %collective-permute-start.1 = (s32[8,128]{1,0:T(8,128)S(1)}, s32[8,128]{1,0:T(8,128)S(1)}, u32[]{:S(2)}, u32[]{:S(2)}) collective-permute-start(s32[8,128]{1,0:T(8,128)S(1)} %get-tuple-element.16), channel_id=1, source_target_pairs={{0,2},{1,3},{2,0},{3,1},{4,6},{5,7},{6,4},{7,5},{8,10},{9,11},{10,... | collective-permute-start | bytes 12296 | tf_op jit(solution)/shard_map/ppermute | solution.py:395
  42.9 29.1 %collective-permute-start.2 = (s32[8,128]{1,0:T(8,128)S(1)}, s32[8,128]{1,0:T(8,128)S(1)}, u32[]{:S(2)}, u32[]{:S(2)}) collective-permute-start(s32[8,128]{1,0:T(8,128)S(1)} %get-tuple-element.17), channel_id=1, source_target_pairs={{0,3},{1,0},{2,1},{3,2},{4,7},{5,4},{6,5},{7,6},{8,11},{9,8},{10,9... | collective-permute-start | bytes 12296 | tf_op jit(solution)/shard_map/ppermute | solution.py:395
  73.0 1.4 %copy-start = (bf16[64,128,128]{2,1,0:T(8,128)(2,1)}, bf16[64,128,128]{2,1,0:T(8,128)(2,1)S(1)}, u32[]{:S(2)}) copy-start(bf16[64,128,128]{2,1,0:T(8,128)(2,1)S(1)} %all-to-all-done.x_ref) | copy-start | bytes 6291460
  84.6 14.4 %all-to-all-start.1 = ((bf16[16,64,128]{2,1,0:T(8,128)(2,1)}), bf16[16,64,128]{2,1,0:T(8,128)(2,1)S(1)}, u32[]{:S(2)}, u32[]{:S(2)}) async-start(bf16[16,64,128]{2,1,0:T(8,128)(2,1)} %bitcast.16), calls=%async_computation.1 | async-start | bytes 524288 | tf_op jit(solution)/shard_map/all_to_all | solution.py:432
  98.9 0.7 copy-start.1
  101.3 13.8 %all-to-all-start.2 = ((bf16[16,16,128]{2,1,0:T(8,128)(2,1)}), bf16[16,16,128]{2,1,0:T(8,128)(2,1)S(1)}, u32[]{:S(2)}, u32[]{:S(2)}) async-start(bf16[16,16,128]{2,1,0:T(8,128)(2,1)} %residues.1), calls=%async_computation.2 | async-start | bytes 131072 | tf_op jit(solution)/shard_map/all_to_all | solution.py:439
  115.1 0.6 copy-start.4

commit v2 on v1

--- a/solution.py
+++ b/solution.py
@@ -16,6 +16,7 @@
 TRIALS = 512
 F32 = jnp.float32
 BF16 = jnp.bfloat16
+MIB = 1 << 20
 NT = (((1,), (1,)), ((), ()))
 NN = (((1,), (0,)), ((), ()))
 
@@ -107,41 +108,53 @@
 
 
 def spectra_kernel(
-    band_ref, part_hbm, v_ref, prev_ref, next_ref, win_ref, tab_ref, out_ref, part_ref, turn_ref, sem
+    band_ref, part_hbm, v_hbm, prev_ref, next_ref, win_ref, tab_hbm, out_hbm,
+    part_ref, edge_ref, tab_ref, stage_ref, turn_ref, in_sem, out_sem
 ):
     inner = pl.ds(64, 416)
-    fetch = pltpu.make_async_copy(part_hbm.at[:, inner, :], part_ref.at[:, inner, :], sem)
-    fetch.start()
+    first = pltpu.make_async_copy(v_hbm.at[0:3], edge_ref.at[0:3], in_sem.at[0])
+    last = pltpu.make_async_copy(v_hbm.at[13:16], edge_ref.at[3:6], in_sem.at[1])
+    parts = pltpu.make_async_copy(part_hbm.at[:, inner, :], part_ref.at[:, inner, :], in_sem.at[2])
+    tables = pltpu.make_async_copy(tab_hbm, tab_ref, in_sem.at[3])
+    for copy in (first, last, parts, tables):
+        copy.start()
     keep = jnp.where(band_ref[0] == 3, 0.0, 1.0).astype(F32)
+    first.wait()
+    last.wait()
 
     def edge(half, carry):
         a0 = pl.multiple_of(16 * half, 16)
         for m in (0, 1):
-            frame = lambda p, m=m: prev_ref.at[m + p] if m + p < 2 else v_ref.at[m + p - 2]
+            frame = lambda p, m=m: prev_ref.at[m + p] if m + p < 2 else edge_ref.at[m + p - 2]
             frame_bins(part_ref, win_ref, pl.multiple_of(32 * m + a0, 16), a0, frame)
-        frame = lambda p: v_ref.at[13 + p] if p < 3 else next_ref.at[0]
+        frame = lambda p: edge_ref.at[3 + p] if p < 3 else next_ref.at[0]
         frame_bins(part_ref, win_ref, pl.multiple_of(480 + a0, 16), a0, frame, keep)
         return carry
 
     lax.fori_loop(0, 2, edge, 0)
-    fetch.wait()
-
-    def transform(at, carry):
+    parts.wait()
+    tables.wait()
+    sent = []
+    for at in range(8):
         rows = lax.dot_general(tab_ref[at], part_ref[at], NT, preferred_element_type=F32)
         for which in range(2):
+            slot = 2 * (at % 2) + which
             for reim in range(2):
                 for mb in range(4):
                     r0 = 128 * which + 64 * reim
-                    turn_ref[which, pl.ds(reim * 4 + mb, 64, stride=8), :] = rows[
+                    turn_ref[slot, pl.ds(reim * 4 + mb, 64, stride=8), :] = rows[
                         r0 : r0 + 64, 128 * mb : 128 * mb + 128
                     ]
         for which in range(2):
-            r = at if which == 0 else jnp.where(at == 0, 8, 16 - at)
+            slot = 2 * (at % 2) + which
+            r = at if which == 0 else (8 if at == 0 else 16 - at)
             for q in range(4):
-                out_ref[r, q] = turn_ref[which, 128 * q : 128 * q + 128, :].astype(BF16)
-        return carry
-
-    lax.fori_loop(0, 8, transform, 0)
+                stage_ref[r, q] = turn_ref[slot, 128 * q : 128 * q + 128, :].astype(BF16)
+            copy = pltpu.make_async_copy(stage_ref.at[r], out_hbm.at[r], out_sem.at[r])
+            copy.start()
+            sent.append(copy)
+    for copy in sent:
+        copy.wait()
 
 
 def spectra(voltages, band_at):
@@ -150,25 +163,32 @@
     behind = lax.ppermute(voltages[0:1], "band", [(i, (i - 1) % band_count) for i in range(band_count)])
     window, tables = jnp.asarray(window_taps()), jnp.asarray(lane_tables())
     vmem, smem = pl.BlockSpec(memory_space=pltpu.VMEM), pl.BlockSpec(memory_space=pltpu.SMEM)
+    anywhere = pl.BlockSpec(memory_space=pl.ANY)
     parts = pl.pallas_call(
         inner_kernel,
         name="inner_frames",
         out_shape=jax.ShapeDtypeStruct((8, 512, 256), BF16),
         in_specs=[vmem] * 2,
         out_specs=vmem,
+        compiler_params=pltpu.CompilerParams(vmem_limit_bytes=58 * MIB),
         cost_estimate=pl.CostEstimate(flops=20_000_000, bytes_accessed=4_000_000, transcendentals=0),
     )(voltages, window)
     return pl.pallas_call(
         spectra_kernel,
         name="spectra",
         out_shape=jax.ShapeDtypeStruct((16, 4, 128, 128), BF16),
-        in_specs=[smem, pl.BlockSpec(memory_space=pl.ANY)] + [vmem] * 5,
-        out_specs=vmem,
+        in_specs=[smem, anywhere, anywhere, vmem, vmem, vmem, anywhere],
+        out_specs=pl.BlockSpec(memory_space=pltpu.HBM),
         scratch_shapes=[
             pltpu.VMEM((8, 512, 256), BF16),
-            pltpu.VMEM((2, 512, 128), F32),
-            pltpu.SemaphoreType.DMA,
+            pltpu.VMEM((6, 32, 2048), BF16),
+            pltpu.VMEM((8, 256, 256), BF16),
+            pltpu.VMEM((16, 4, 128, 128), BF16),
+            pltpu.VMEM((4, 512, 128), F32),
+            pltpu.SemaphoreType.DMA((4,)),
+            pltpu.SemaphoreType.DMA((16,)),
         ],
+        compiler_params=pltpu.CompilerParams(vmem_limit_bytes=52 * MIB),
         cost_estimate=pl.CostEstimate(
             flops=600_000_000, bytes_accessed=6_000_000, transcendentals=0
         ),
@@ -189,42 +209,30 @@
     return two
 
 
-def beam_kernel(
-    east_ref, sub_ref, x_ref, w_ref, hot_hbm, out_ref, left_ref, prod_ref, acc_ref, hot_ref, sem
-):
-    step = pl.program_id(0)
-    fetch = pltpu.make_async_copy(hot_hbm, hot_ref, sem)
-
-    @pl.when(step == 0)
-    def _():
-        fetch.start()
-        acc_ref[...] = jnp.zeros_like(acc_ref)
-
+def place_channels(x_ref, left_ref):
     low = lax.broadcasted_iota(jnp.int32, (8, 128), 0) < 4
-    row0 = pl.multiple_of(16 * step, 16)
     for pe in range(8):
         for h in range(2):
             src = pe * 8 + h * 4
-            tiles = turn_blocks([x_ref[src + n, pl.ds(row0, 16), :] for n in range(4)])
+            tiles = turn_blocks([x_ref[src + n] for n in range(4)])
             tiles = [t.astype(F32) for t in tiles]
             for ch in range(2):
                 one = [t[8 * ch : 8 * ch + 8] for t in tiles]
                 re = [jnp.where(low, one[a], pltpu.roll(one[a + 1], 4, 0)) for a in (0, 2)]
                 im = [jnp.where(low, pltpu.roll(one[a], 4, 0), one[a + 1]) for a in (0, 2)]
-                re, im = jnp.concatenate(re, axis=0), jnp.concatenate(im, axis=0)
+                re = jnp.concatenate(re, axis=0).astype(BF16)
+                im = jnp.concatenate(im, axis=0).astype(BF16)
                 rows, cols = slice(16 * pe, 16 * pe + 16), slice(128 * h, 128 * h + 128)
                 more = slice(256 + 128 * h, 384 + 128 * h)
-                left_ref[ch, 0, rows, cols] = re.astype(BF16)
-                left_ref[ch, 0, rows, more] = (-im).astype(BF16)
-                left_ref[ch, 1, rows, cols] = re.astype(BF16)
-                left_ref[ch, 1, rows, more] = im.astype(BF16)
+                left_ref[ch, 0, rows, cols] = re
+                left_ref[ch, 0, rows, more] = -im
+                left_ref[ch, 1, rows, cols] = re
+                left_ref[ch, 1, rows, more] = im
+
+
+def add_powers(pair, east_ref, sub_ref, prod_ref, acc_ref):
     for ch in range(2):
-        for part in range(2):
-            prod_ref[ch, part] = lax.dot_general(
-                left_ref[ch, part], w_ref[ch, 256 * part : 256 * part + 512, :], NN, preferred_element_type=F32
-            )
-    for ch in range(2):
-        i = 2 * step + ch
+        i = 2 * pair + ch
         sub = sub_ref[i]
         cos = [[east_ref[i, s * 4 + e] for e in range(4)] for s in range(4)]
         sin = [[east_ref[i, 16 + s * 4 + e] for e in range(4)] for s in range(4)]
@@ -252,8 +260,31 @@
                     cols = slice(s * 256 + h * 128, s * 256 + h * 128 + 128)
                     acc_ref[sub, 8 * t : 8 * t + 8, cols] += power[s]
 
+
+def beam_kernel(
+    east_ref, sub_ref, first_ref, next_ref, w_ref, hot_hbm, out_ref, left_ref, prod_ref, acc_ref, hot_ref, sem
+):
+    step = pl.program_id(0)
+    fetch = pltpu.make_async_copy(hot_hbm, hot_ref, sem)
+
+    @pl.when(step == 0)
+    def _():
+        fetch.start()
+        acc_ref[...] = jnp.zeros_like(acc_ref)
+        prod_ref[...] = jnp.zeros_like(prod_ref)
+        place_channels(first_ref, left_ref)
+
+    add_powers(jnp.maximum(step - 1, 0), east_ref, sub_ref, prod_ref, acc_ref)
+    for ch in range(2):
+        for part in range(2):
+            prod_ref[ch, part] = lax.dot_general(
+                left_ref[ch, part], w_ref[ch, 256 * part : 256 * part + 512, :], NN, preferred_element_type=F32
+            )
+    place_channels(next_ref, left_ref)
+
     @pl.when(step == pl.num_programs(0) - 1)
     def _():
+        add_powers(step, east_ref, sub_ref, prod_ref, acc_ref)
         total = acc_ref[...].reshape(64, 1024)
         top = total.astype(BF16)
         rest = (total - top.astype(F32)).astype(BF16)
@@ -272,7 +303,8 @@
         in_specs=[
             smem,
             smem,
-            pl.BlockSpec((64, 128, 128), lambda i: (0, 0, 0)),
+            pl.BlockSpec((64, 16, 128), lambda i: (0, 0, 0)),
+            pl.BlockSpec((64, 16, 128), lambda i: (0, jnp.minimum(i + 1, 7), 0)),
             pl.BlockSpec((2, 768, 256), lambda i: (i, 0, 0)),
             pl.BlockSpec(memory_space=pl.ANY),
         ],
@@ -284,24 +316,54 @@
             pltpu.VMEM((1024, 1024), BF16),
             pltpu.SemaphoreType.DMA,
         ],
+        compiler_params=pltpu.CompilerParams(vmem_limit_bytes=51 * MIB),
         cost_estimate=pl.CostEstimate(
             flops=2_000_000_000, bytes_accessed=11_000_000, transcendentals=0
         ),
-    )(east, subs, turned, weights, hot)
+    )(east, subs, turned, turned, weights, hot)
+
+
+def weight_kernel(step_ref, out_ref):
+    scale = 2 * C * 256
+    row = lax.broadcasted_iota(jnp.int32, (16, 256), 0)
+    north = lax.broadcasted_iota(jnp.int32, (16, 256), 1)
+    for ch in range(2):
+        rate = step_ref[2 * pl.program_id(0) + ch]
+
+        def turn(feeds):
+            phases = (2.0 * math.pi / scale) * ((rate * (feeds * north)) % scale).astype(F32)
+            return jnp.cos(phases), jnp.sin(phases)
+
+        norm = 1.0 / math.sqrt(FEEDS)
+        cos, sin = turn(row)
+        cos, sin = cos * norm, sin * norm
+        more_cos, more_sin = turn(16 + 0 * row)
+        for tile in range(16):
+            if tile:
+                cos, sin = cos * more_cos - sin * more_sin, sin * more_cos + cos * more_sin
+            r0 = 16 * tile
+            out_ref[ch, r0 : r0 + 16, :] = cos.astype(BF16)
+            out_ref[ch, 256 + r0 : 272 + r0, :] = sin.astype(BF16)
+            out_ref[ch, 512 + r0 : 528 + r0, :] = cos.astype(BF16)
 
 
 def beam_weights(channels):
     scale = 2 * C
     steps = scale - channels
-    north = jnp.arange(256, dtype=jnp.int32)
-    turns = steps[:, None, None] * (north[:, None] * north[None, :])[None] % (scale * 256)
-    phases = (2.0 * math.pi / (scale * 256)) * turns.astype(F32)
-    norm = 1.0 / math.sqrt(FEEDS)
-    cos, sin = (jnp.cos(phases) * norm).astype(BF16), (jnp.sin(phases) * norm).astype(BF16)
+    weights = pl.pallas_call(
+        weight_kernel,
+        name="weights",
+        grid=(8,),
+        out_shape=jax.ShapeDtypeStruct((16, 768, 256), BF16),
+        in_specs=[pl.BlockSpec(memory_space=pltpu.SMEM)],
+        out_specs=pl.BlockSpec((2, 768, 256), lambda i: (i, 0, 0)),
+        compiler_params=pltpu.CompilerParams(vmem_limit_bytes=56 * MIB),
+        cost_estimate=pl.CostEstimate(flops=20_000_000, bytes_accessed=6_000_000, transcendentals=500_000),
+    )(steps)
     four = jnp.arange(4, dtype=jnp.int32)
     turns = steps[:, None] * (four[:, None] * four[None, :]).reshape(1, 16) % (scale * 4)
     phases = (2.0 * math.pi / (scale * 4)) * turns.astype(F32)
-    return jnp.concatenate([cos, sin, cos], axis=1), jnp.concatenate([jnp.cos(phases), jnp.sin(phases)], axis=1)
+    return weights, jnp.concatenate([jnp.cos(phases), jnp.sin(phases)], axis=1)
 
 
 def gather_kernel(x_ref, out_ref):
@@ -326,6 +388,7 @@
         out_shape=jax.ShapeDtypeStruct((16, 16, 128), BF16),
         in_specs=[vmem],
         out_specs=vmem,
+        compiler_params=pltpu.CompilerParams(vmem_limit_bytes=4 * MIB),
     )(pieces)
 
 
@@ -384,6 +447,7 @@
         in_specs=[vmem] * 3,
         out_specs=vmem,
         scratch_shapes=[pltpu.VMEM((1024, 512), BF16), pltpu.VMEM((2, 256, 1024), BF16)],
+        compiler_params=pltpu.CompilerParams(vmem_limit_bytes=8 * MIB),
         cost_estimate=pl.CostEstimate(
             flops=600_000_000, bytes_accessed=1_000_000, transcendentals=0
         ),

time: 120 us -> 104 us (0.87)
  other arithmetic: 27.1 us -> 2.35 us
  waiting for transfers between devices: 17.7 us -> 29.5 us
  local copies, waits for them, and re-layouts: 5.76 us -> 2.34 us
    convert_element_type x1 -> x0, other arithmetic: 17.2 us -> none  [beam_weights(): (jnp.sin(phases) * norm).astype(BF16)]
    ppermute x3, waiting for transfers between devices: 0.01 us -> 11.3 us  [from_band(): lax.ppermute(block, 'band', [(i, (i + back) % count) for i in range(count)])]
    pallas_call x0 -> x1, Pallas kernels: none -> 5.89 us  [beam_weights(): pl.pallas_call(weight_kernel, name='weights', grid=(8,), out_shape=jax.Sh...]
    concatenate x1 -> x0, other arithmetic: 5.84 us -> none  [beam_weights(): jnp.concatenate([cos, sin, cos], axis=1)]
    pallas_call x1, Pallas kernels: 7.25 us -> 3.67 us  [spectra(): pl.pallas_call(spectra_kernel, name='spectra', out_shape=jax.ShapeDtypeSt...]
    unnamed x17 -> x15, local copies, waits for them, and re-layouts: 3.53 us -> 0.12 us
  transfers between devices with their start and end apart: 8 -> 8, of which waited for: 3 -> 5; matrix products, arithmetic and copies ran while one was open for 24% -> 4% of each run, Pallas kernels for 4% -> 11%
where the time goes in v2:
time: 104 us; the launch traced here: 103 us
  starting transfers between devices  41.6 us (40%)
  waiting for transfers between devices  29.5 us (28%)
  Pallas kernels  27.4 us (26%)
  other arithmetic  2.35 us (2%)
  local copies, waits for them, and re-layouts  2.34 us (2%)
    ppermute x3, waiting for transfers between devices, from_band(): lax.ppermute(block, 'band', [(i, (i + back) % count) for i in range(count)])  11.3 us
    ppermute x3, starting transfers between devices, from_band(): lax.ppermute(block, 'band', [(i, (i + back) % count) for i in range(count)])  10.8 us
    pallas_call x1, Pallas kernels, beams(): pl.pallas_call(beam_kernel, name='beams', grid=(8,), out_shape=jax.ShapeD...  9.83 us
    all_to_all x1, starting transfers between devices, local(): lax.all_to_all(chunks, 'grp', split_axis=0, concat_axis=0, tiled=True)  9.17 us
    all_to_all x1, waiting for transfers between devices, local(): lax.all_to_all(gather_residues(pieces), ('grp', 'band'), split_axis=0, co...  7.69 us
    all_to_all x1, waiting for transfers between devices, local(): lax.all_to_all(sums, 'grp', split_axis=0, concat_axis=0, tiled=True, axis...  7.42 us
    all_to_all x1, starting transfers between devices, local(): lax.all_to_all(sums, 'grp', split_axis=0, concat_axis=0, tiled=True, axis...  6.73 us
    all_to_all x1, starting transfers between devices, local(): lax.all_to_all(gather_residues(pieces), ('grp', 'band'), split_axis=0, co...  6.65 us
  transfers between devices with their start and end apart: 8, of which 5 were waited for; matrix products, arithmetic and copies ran while one was open for 4% of the time, Pallas kernels for 11%

profile of v2, /device:TPU:1, one launch (start us, length us, event | category | flops | bytes accessed | tf_op | source)
XLA Modules:
  0.0 103.3 jit_solution(11038895331222922740)
XLA Ops:
  0.0 1.0 slice.28
  1.0 5.7 %collective-permute-start.3 = (bf16[2,32,2048]{2,1,0:T(8,128)(2,1)S(1)}, bf16[2,32,2048]{2,1,0:T(8,128)(2,1)S(1)}, u32[]{:S(2)}, u32[]{:S(2)}) collective-permute-start(bf16[2,32,2048]{2,1,0:T(8,128)(2,1)S(1)} %slice.28), channel_id=1, source_target_pairs={{0,1},{1,2},{2,3},{4,5},{5,6},{6,7},{8,9},{9,10},{10,11},{12,13},{... | collective-permute-start | bytes 786440 | tf_op jit(solution)/shard_map/ppermute | solution.py:162
  6.7 0.9 slice.29
  7.6 2.5 %collective-permute-start.4 = (bf16[1,32,2048]{2,1,0:T(8,128)(2,1)S(1)}, bf16[1,32,2048]{2,1,0:T(8,128)(2,1)S(1)}, u32[]{:S(2)}, u32[]{:S(2)}) collective-permute-start(bf16[1,32,2048]{2,1,0:T(8,128)(2,1)S(1)} %slice.29), channel_id=1, source_target_pairs={{0,3},{1,0},{2,1},{3,2},{4,7},{5,4},{6,5},{7,6},{8,11},{9,8},{10,9... | collective-permute-start | bytes 393224 | tf_op jit(solution)/shard_map/ppermute | solution.py:163
  10.1 0.0 copy-start
  10.1 0.0 copy-start.1
  10.1 5.0 %inner_frames.1.part_hbm = bf16[8,512,256]{2,1,0:T(8,128)(2,1)} custom-call(bf16[16,32,2048]{2,1,0:T(8,128)(2,1)} %v_hbm.1, f32[4,2048]{1,0:T(4,128)} %constant.149.clone.win_ref), custom_call_target="tpu_custom_call" | custom-call | flops 20000000 | bytes 4000000 | tf_op jit(solution)/shard_map/inner_frames/pallas_call | solution.py:167
  15.1 3.1 %collective-permute-done.4.next_ref = bf16[1,32,2048]{2,1,0:T(8,128)(2,1)S(1)} collective-permute-done((bf16[1,32,2048]{2,1,0:T(8,128)(2,1)S(1)}, bf16[1,32,2048]{2,1,0:T(8,128)(2,1)S(1)}, u32[]{:S(2)}, u32[]{:S(2)}) %collective-permute-start.4) | collective-permute-done | bytes 131104 | tf_op jit(solution)/shard_map/ppermute | solution.py:163
  18.2 0.0 collective-permute-done.3.prev_ref
  18.2 0.0 copy-done
  18.2 0.0 copy-done.1
  18.2 3.7 %spectra.1 = bf16[16,4,128,128]{3,2,1,0:T(8,128)(2,1)} custom-call(s32[1]{0:T(128)} %bitcast.6.band_ref, bf16[8,512,256]{2,1,0:T(8,128)(2,1)} %inner_frames.1.part_hbm, bf16[16,32,2048]{2,1,0:T(8,128)(2,1)} %v_hbm.1, bf16[2,32,2048]{2,1,0:T(8,128)(2,1)S(1)} %collective-permute-done.3.prev_ref, bf16[1,32,2048]{2,1,0:T(8,128)(2,1)S(1)} %collective-permute-done.4.next_ref, ...), custom_call_target="tpu_custom_call" | custom-call | flops 600000000 | bytes 6000000 | tf_op jit(solution)/shard_map/spectra/pallas_call | solution.py:176
  21.9 0.0 copy-start.5
  21.9 0.0 copy-start.3
  21.9 0.0 copy-start.4
  21.9 9.2 %all-to-all-start = ((bf16[64,128,128]{2,1,0:T(8,128)(2,1)}), bf16[64,128,128]{2,1,0:T(8,128)(2,1)S(1)}, u32[]{:S(2)}, u32[]{:S(2)}) async-start(bf16[64,128,128]{2,1,0:T(8,128)(2,1)} %bitcast.15), calls=%async_computation | async-start | bytes 4194304 | tf_op jit(solution)/shard_map/all_to_all | solution.py:488
  31.2 0.1 pad.14.clone
  31.2 0.0 copy-done.5
  31.3 0.0 copy-done.3
  31.3 0.1 fusion.6
  31.3 3.2 %collective-permute-start = (s32[8,128]{1,0:T(8,128)S(1)}, s32[8,128]{1,0:T(8,128)S(1)}, u32[]{:S(2)}, u32[]{:S(2)}) collective-permute-start(s32[8,128]{1,0:T(8,128)S(1)} %get-tuple-element.13), channel_id=1, source_target_pairs={{0,1},{1,2},{2,3},{3,0},{4,5},{5,6},{6,7},{7,4},{8,9},{9,10},{10,1... | collective-permute-start | bytes 12296 | tf_op jit(solution)/shard_map/ppermute | solution.py:459
  34.6 4.2 %collective-permute-start.1 = (s32[8,128]{1,0:T(8,128)S(1)}, s32[8,128]{1,0:T(8,128)S(1)}, u32[]{:S(2)}, u32[]{:S(2)}) collective-permute-start(s32[8,128]{1,0:T(8,128)S(1)} %get-tuple-element.14), channel_id=1, source_target_pairs={{0,2},{1,3},{2,0},{3,1},{4,6},{5,7},{6,4},{7,5},{8,10},{9,11},{10,... | collective-permute-start | bytes 12296 | tf_op jit(solution)/shard_map/ppermute | solution.py:459
  38.8 3.4 %collective-permute-start.2 = (s32[8,128]{1,0:T(8,128)S(1)}, s32[8,128]{1,0:T(8,128)S(1)}, u32[]{:S(2)}, u32[]{:S(2)}) collective-permute-start(s32[8,128]{1,0:T(8,128)S(1)} %get-tuple-element.15), channel_id=1, source_target_pairs={{0,3},{1,0},{2,1},{3,2},{4,7},{5,4},{6,5},{7,6},{8,11},{9,8},{10,9... | collective-permute-start | bytes 12296 | tf_op jit(solution)/shard_map/ppermute | solution.py:459
  42.2 0.1 mul.78
  42.3 0.0 copy-start.6
  42.3 0.1 fusion.8
  42.4 0.1 pad_maximum_fusion.east_ref
  42.5 0.0 copy-done.4
  42.5 1.8 %fusion.hot_hbm = bf16[1024,1024]{1,0:T(8,128)(2,1)} fusion(s32[1024]{0:T(1024)S(1)} %bitcast.16), kind=kLoop, calls=%fused_computation.1 | loop fusion | flops 2097152 | bytes 2101248 | tf_op jit(solution)/shard_map/convert_element_type | solution.py:493
  44.3 0.0 copy-done.6
  44.3 5.9 %weights.1.w_ref = bf16[16,768,256]{2,1,0:T(8,128)(2,1)} custom-call(s32[16]{0:T(128)} %copy-done.6), custom_call_target="tpu_custom_call" | custom-call | flops 20000000 | bytes 6000000 | tf_op jit(solution)/shard_map/weights/pallas_call | solution.py:353
  50.2 9.6 %collective-permute-done = s32[8,128]{1,0:T(8,128)S(1)} collective-permute-done((s32[8,128]{1,0:T(8,128)S(1)}, s32[8,128]{1,0:T(8,128)S(1)}, u32[]{:S(2)}, u32[]{:S(2)}) %collective-permute-start) | collective-permute-done | bytes 4128 | tf_op jit(solution)/shard_map/ppermute | solution.py:459
  59.7 1.7 %collective-permute-done.1 = s32[8,128]{1,0:T(8,128)S(1)} collective-permute-done((s32[8,128]{1,0:T(8,128)S(1)}, s32[8,128]{1,0:T(8,128)S(1)}, u32[]{:S(2)}, u32[]{:S(2)}) %collective-permute-start.1) | collective-permute-done | bytes 4128 | tf_op jit(solution)/shard_map/ppermute | solution.py:459
  61.5 0.0 collective-permute-done.2
  61.5 0.1 select_add_fusion.4
  61.6 0.1 reshape.57
  61.6 0.1 constant_dynamic-slice_fusion
  61.7 0.1 copy.9
  61.8 0.0 copy-start.2
  61.8 0.0 all-to-all-done.first_ref.next_ref
  61.8 9.8 %beams.1 = bf16[1024,128]{1,0:T(8,128)(2,1)} custom-call(f32[16,32]{1,0:T(8,128)S(1)} %pad_maximum_fusion.east_ref, s32[16]{0:T(128)S(1)} %and_select_fusion.sub_ref, bf16[64,128,128]{2,1,0:T(8,128)(2,1)S(1)} %all-to-all-done.first_ref.next_ref, bf16[64,128,128]{2,1,0:T(8,128)(2,1)S(1)} %all-to-all-done.first_ref.next_ref, ...), custom_call_target="tpu_custom_call" | custom-call | flops 2000000000 | bytes 11000000 | tf_op jit(solution)/shard_map/beams/pallas_call | solution.py:298
  71.7 6.7 %all-to-all-start.1 = ((bf16[16,64,128]{2,1,0:T(8,128)(2,1)}), bf16[16,64,128]{2,1,0:T(8,128)(2,1)S(1)}, u32[]{:S(2)}, u32[]{:S(2)}) async-start(bf16[16,64,128]{2,1,0:T(8,128)(2,1)} %bitcast.9), calls=%async_computation.1 | async-start | bytes 524288 | tf_op jit(solution)/shard_map/all_to_all | solution.py:496
  78.4 0.1 select_add_fusion.2
  78.5 7.4 %all-to-all-done.1.x_ref = bf16[16,64,128]{2,1,0:T(8,128)(2,1)S(1)} async-done(((bf16[16,64,128]{2,1,0:T(8,128)(2,1)}), bf16[16,64,128]{2,1,0:T(8,128)(2,1)S(1)}, u32[]{:S(2)}, u32[]{:S(2)}) %all-to-all-start.1) | async-done | bytes 262176 | tf_op jit(solution)/shard_map/all_to_all | solution.py:496
  85.9 0.8 residues.1
  86.7 6.7 %all-to-all-start.2 = ((bf16[16,16,128]{2,1,0:T(8,128)(2,1)}), bf16[16,16,128]{2,1,0:T(8,128)(2,1)S(1)}, u32[]{:S(2)}, u32[]{:S(2)}) async-start(bf16[16,16,128]{2,1,0:T(8,128)(2,1)} %residues.1), calls=%async_computation.2 | async-start | bytes 131072 | tf_op jit(solution)/shard_map/all_to_all | solution.py:503
  93.3 0.1 select_add_fusion.3
  93.5 7.7 %all-to-all-done.2.x_ref = bf16[16,16,128]{2,1,0:T(8,128)(2,1)S(1)} async-done(((bf16[16,16,128]{2,1,0:T(8,128)(2,1)}), bf16[16,16,128]{2,1,0:T(8,128)(2,1)S(1)}, u32[]{:S(2)}, u32[]{:S(2)}) %all-to-all-start.2) | async-done | bytes 65568 | tf_op jit(solution)/shard_map/all_to_all | solution.py:503
  101.2 0.0 copy-done.2
  101.2 2.2 %series.1 = f32[64,16,128]{2,1,0:T(8,128)} custom-call(bf16[16,16,128]{2,1,0:T(8,128)(2,1)S(1)} %all-to-all-done.2.x_ref, bf16[4,128,256]{2,1,0:T(8,128)(2,1)S(1)} %copy-done.2, s32[16,128]{1,0:T(8,128)S(1)} %pad_add_fusion.delay_ref), custom_call_target="tpu_custom_call" | custom-call | flops 600000000 | bytes 1000000 | tf_op jit(solution)/shard_map/series/pallas_call | solution.py:443
  (12 shorter events, 0.1 us)
Async XLA Ops:
  1.0 17.2 %collective-permute-start.3 = (bf16[2,32,2048]{2,1,0:T(8,128)(2,1)S(1)}, bf16[2,32,2048]{2,1,0:T(8,128)(2,1)S(1)}, u32[]{:S(2)}, u32[]{:S(2)}) collective-permute-start(bf16[2,32,2048]{2,1,0:T(8,128)(2,1)S(1)} %slice.28), channel_id=1, source_target_pairs={{0,1},{1,2},{2,3},{4,5},{5,6},{6,7},{8,9},{9,10},{10,11},{12,13},{... | collective-permute-start | bytes 786440 | tf_op jit(solution)/shard_map/ppermute | solution.py:162
  7.6 10.6 %collective-permute-start.4 = (bf16[1,32,2048]{2,1,0:T(8,128)(2,1)S(1)}, bf16[1,32,2048]{2,1,0:T(8,128)(2,1)S(1)}, u32[]{:S(2)}, u32[]{:S(2)}) collective-permute-start(bf16[1,32,2048]{2,1,0:T(8,128)(2,1)S(1)} %slice.29), channel_id=1, source_target_pairs={{0,3},{1,0},{2,1},{3,2},{4,7},{5,4},{6,5},{7,6},{8,11},{9,8},{10,9... | collective-permute-start | bytes 393224 | tf_op jit(solution)/shard_map/ppermute | solution.py:163
  10.1 8.1 %copy-start = (bf16[8,256,256]{2,1,0:T(8,128)(2,1)S(1)}, bf16[8,256,256]{2,1,0:T(8,128)(2,1)}, u32[]{:S(2)}) copy-start(bf16[8,256,256]{2,1,0:T(8,128)(2,1)} %constant.150.clone.tab_hbm) | copy-start | bytes 3145732
  10.1 8.1 %copy-start.1 = (f32[4,2048]{1,0:T(4,128)S(1)}, f32[4,2048]{1,0:T(4,128)}, u32[]{:S(2)}) copy-start(f32[4,2048]{1,0:T(4,128)} %constant.149.clone.win_ref) | copy-start | bytes 98308
  21.9 9.4 %copy-start.5 = (s32[512,4]{0,1:T(4,128)S(1)}, s32[512,4]{0,1:T(4,128)}, u32[]{:S(2)}) copy-start(s32[512,4]{0,1:T(4,128)} %param.10) | copy-start | bytes 24580
  21.9 9.3 %copy-start.3 = (s32[256]{0:T(256)S(1)}, s32[256]{0:T(256)}, u32[]{:S(2)}) copy-start(s32[256]{0:T(256)} %param.9) | copy-start | bytes 3076
  21.9 20.6 %copy-start.4 = (s32[2,1024]{1,0:T(2,128)S(1)}, s32[2,1024]{1,0:T(2,128)}, u32[]{:S(2)}) copy-start(s32[2,1024]{1,0:T(2,128)} %param.8) | copy-start | bytes 24580
  21.9 39.9 %all-to-all-start = ((bf16[64,128,128]{2,1,0:T(8,128)(2,1)}), bf16[64,128,128]{2,1,0:T(8,128)(2,1)S(1)}, u32[]{:S(2)}, u32[]{:S(2)}) async-start(bf16[64,128,128]{2,1,0:T(8,128)(2,1)} %bitcast.15), calls=%async_computation | async-start | bytes 4194304 | tf_op jit(solution)/shard_map/all_to_all | solution.py:488
  31.3 28.4 %collective-permute-start = (s32[8,128]{1,0:T(8,128)S(1)}, s32[8,128]{1,0:T(8,128)S(1)}, u32[]{:S(2)}, u32[]{:S(2)}) collective-permute-start(s32[8,128]{1,0:T(8,128)S(1)} %get-tuple-element.13), channel_id=1, source_target_pairs={{0,1},{1,2},{2,3},{3,0},{4,5},{5,6},{6,7},{7,4},{8,9},{9,10},{10,1... | collective-permute-start | bytes 12296 | tf_op jit(solution)/shard_map/ppermute | solution.py:459
  34.6 26.9 %collective-permute-start.1 = (s32[8,128]{1,0:T(8,128)S(1)}, s32[8,128]{1,0:T(8,128)S(1)}, u32[]{:S(2)}, u32[]{:S(2)}) collective-permute-start(s32[8,128]{1,0:T(8,128)S(1)} %get-tuple-element.14), channel_id=1, source_target_pairs={{0,2},{1,3},{2,0},{3,1},{4,6},{5,7},{6,4},{7,5},{8,10},{9,11},{10,... | collective-permute-start | bytes 12296 | tf_op jit(solution)/shard_map/ppermute | solution.py:459
  38.8 22.7 %collective-permute-start.2 = (s32[8,128]{1,0:T(8,128)S(1)}, s32[8,128]{1,0:T(8,128)S(1)}, u32[]{:S(2)}, u32[]{:S(2)}) collective-permute-start(s32[8,128]{1,0:T(8,128)S(1)} %get-tuple-element.15), channel_id=1, source_target_pairs={{0,3},{1,0},{2,1},{3,2},{4,7},{5,4},{6,5},{7,6},{8,11},{9,8},{10,9... | collective-permute-start | bytes 12296 | tf_op jit(solution)/shard_map/ppermute | solution.py:459
  42.3 2.0 %copy-start.6 = (s32[16]{0:T(128)}, s32[16]{0:T(128)S(1)}, u32[]{:S(2)}) copy-start(s32[16]{0:T(128)S(1)} %add_subtract_fusion.step_ref) | copy-start | bytes 196
  61.8 39.4 %copy-start.2 = (bf16[4,128,256]{2,1,0:T(8,128)(2,1)S(1)}, bf16[4,128,256]{2,1,0:T(8,128)(2,1)}, u32[]{:S(2)}) copy-start(bf16[4,128,256]{2,1,0:T(8,128)(2,1)} %constant.151.clone.tab_ref) | copy-start | bytes 786436
  71.7 14.3 %all-to-all-start.1 = ((bf16[16,64,128]{2,1,0:T(8,128)(2,1)}), bf16[16,64,128]{2,1,0:T(8,128)(2,1)S(1)}, u32[]{:S(2)}, u32[]{:S(2)}) async-start(bf16[16,64,128]{2,1,0:T(8,128)(2,1)} %bitcast.9), calls=%async_computation.1 | async-start | bytes 524288 | tf_op jit(solution)/shard_map/all_to_all | solution.py:496
  86.7 14.5 %all-to-all-start.2 = ((bf16[16,16,128]{2,1,0:T(8,128)(2,1)}), bf16[16,16,128]{2,1,0:T(8,128)(2,1)S(1)}, u32[]{:S(2)}, u32[]{:S(2)}) async-start(bf16[16,16,128]{2,1,0:T(8,128)(2,1)} %residues.1), calls=%async_computation.2 | async-start | bytes 131072 | tf_op jit(solution)/shard_map/all_to_all | solution.py:503

commit v3 on v2

--- a/solution.py
+++ b/solution.py
@@ -195,96 +195,119 @@
     )(band_at.reshape(1), parts, voltages, ahead, behind, window, tables)
 
 
-def turn_blocks(tiles):
-    lane = lax.broadcasted_iota(jnp.int32, tiles[0].shape, 1)
-    odd, high = (lane // 32) % 2 == 1, lane // 64 == 1
+def turn_blocks(tiles, axis, size):
+    shape = tiles[0].shape
+    at = lax.broadcasted_iota(jnp.int32, shape, axis) // size
+    odd, high = at % 2 == 1, at // 2 == 1
     one = [None] * 4
     for a, b in ((0, 1), (2, 3)):
-        one[a] = jnp.where(odd, pltpu.roll(tiles[b], 32, 1), tiles[a])
-        one[b] = jnp.where(odd, tiles[b], pltpu.roll(tiles[a], 96, 1))
+        one[a] = jnp.where(odd, pltpu.roll(tiles[b], size, axis), tiles[a])
+        one[b] = jnp.where(odd, tiles[b], pltpu.roll(tiles[a], shape[axis] - size, axis))
     two = [None] * 4
     for a, b in ((0, 2), (1, 3)):
-        two[a] = jnp.where(high, pltpu.roll(one[b], 64, 1), one[a])
-        two[b] = jnp.where(high, one[b], pltpu.roll(one[a], 64, 1))
+        two[a] = jnp.where(high, pltpu.roll(one[b], 2 * size, axis), one[a])
+        two[b] = jnp.where(high, one[b], pltpu.roll(one[a], 2 * size, axis))
     return two
 
 
 def place_channels(x_ref, left_ref):
-    low = lax.broadcasted_iota(jnp.int32, (8, 128), 0) < 4
     for pe in range(8):
         for h in range(2):
             src = pe * 8 + h * 4
-            tiles = turn_blocks([x_ref[src + n] for n in range(4)])
-            tiles = [t.astype(F32) for t in tiles]
-            for ch in range(2):
-                one = [t[8 * ch : 8 * ch + 8] for t in tiles]
-                re = [jnp.where(low, one[a], pltpu.roll(one[a + 1], 4, 0)) for a in (0, 2)]
-                im = [jnp.where(low, pltpu.roll(one[a], 4, 0), one[a + 1]) for a in (0, 2)]
-                re = jnp.concatenate(re, axis=0).astype(BF16)
-                im = jnp.concatenate(im, axis=0).astype(BF16)
-                rows, cols = slice(16 * pe, 16 * pe + 16), slice(128 * h, 128 * h + 128)
-                more = slice(256 + 128 * h, 384 + 128 * h)
-                left_ref[ch, 0, rows, cols] = re
-                left_ref[ch, 0, rows, more] = -im
-                left_ref[ch, 1, rows, cols] = re
-                left_ref[ch, 1, rows, more] = im
-
-
-def add_powers(pair, east_ref, sub_ref, prod_ref, acc_ref):
-    for ch in range(2):
+            tiles = turn_blocks([x_ref[src + n] for n in range(4)], 1, 32)
+            for m4 in range(4):
+                rows = slice(16 * pe + 4 * m4, 16 * pe + 4 * m4 + 4)
+                for ch in range(2):
+                    for part in range(2):
+                        cols = slice(256 * part + 128 * h, 256 * part + 128 * h + 128)
+                        at = 8 * ch + 4 * part
+                        left_ref[ch, rows, cols] = tiles[m4][at : at + 4]
+
+
+def add_powers(channels, pair, east_ref, sub_ref, prod_ref, acc_ref):
+    for ch in channels:
         i = 2 * pair + ch
         sub = sub_ref[i]
-        cos = [[east_ref[i, s * 4 + e] for e in range(4)] for s in range(4)]
-        sin = [[east_ref[i, 16 + s * 4 + e] for e in range(4)] for s in range(4)]
+        cos = [[east_ref[i, s * 4 + k] for k in range(4)] for s in range(4)]
+        sin = [[east_ref[i, 16 + s * 4 + k] for k in range(4)] for s in range(4)]
         for t in range(2):
             for h in range(2):
-                power = [None] * 4
+                total, corr_re, corr_im = None, [None] * 4, [None] * 4
                 for p in range(2):
                     re, im = [], []
                     for e in range(4):
-                        r0 = p * 64 + e * 16 + t * 8
-                        re.append(prod_ref[ch, 0, r0 : r0 + 8, 128 * h : 128 * h + 128])
-                        im.append(prod_ref[ch, 1, r0 : r0 + 8, 128 * h : 128 * h + 128])
-                    for s in range(4):
-                        beam_re, beam_im = re[0], im[0]
-                        for e in range(1, 4):
-                            if s == 0:
-                                beam_re, beam_im = beam_re + re[e], beam_im + im[e]
-                            else:
-                                c, d = cos[s][e], sin[s][e]
-                                beam_re = beam_re + (c * re[e] - d * im[e])
-                                beam_im = beam_im + (c * im[e] + d * re[e])
-                        square = beam_re * beam_re + beam_im * beam_im
-                        power[s] = square if p == 0 else power[s] + square
+                        rows = slice(p * 64 + e * 16 + t * 8, p * 64 + e * 16 + t * 8 + 8)
+                        re.append(prod_ref[ch, rows, 128 * h : 128 * h + 128])
+                        im.append(prod_ref[ch, rows, 256 + 128 * h : 384 + 128 * h])
+                    for e in range(4):
+                        square = re[e] * re[e] + im[e] * im[e]
+                        total = square if total is None else total + square
+                    for k in range(1, 4):
+                        for f in range(4 - k):
+                            a = re[f + k] * re[f] + im[f + k] * im[f]
+                            b = im[f + k] * re[f] - re[f + k] * im[f]
+                            corr_re[k] = a if corr_re[k] is None else corr_re[k] + a
+                            corr_im[k] = b if corr_im[k] is None else corr_im[k] + b
                 for s in range(4):
+                    if s == 0:
+                        twice = corr_re[1] + corr_re[2] + corr_re[3]
+                        power = total + (twice + twice)
+                    else:
+                        power = total
+                        for k in range(1, 4):
+                            power = power + (cos[s][k] * corr_re[k] - sin[s][k] * corr_im[k])
                     cols = slice(s * 256 + h * 128, s * 256 + h * 128 + 128)
-                    acc_ref[sub, 8 * t : 8 * t + 8, cols] += power[s]
+                    acc_ref[sub, 8 * t : 8 * t + 8, cols] += power
 
 
 def beam_kernel(
-    east_ref, sub_ref, first_ref, next_ref, w_ref, hot_hbm, out_ref, left_ref, prod_ref, acc_ref, hot_ref, sem
+    east_ref, sub_ref, first_ref, odd_ref, next_ref, w_ref, hot_hbm, out_ref,
+    left_ref, prod_ref, acc_ref, hot_ref, sem
 ):
     step = pl.program_id(0)
     fetch = pltpu.make_async_copy(hot_hbm, hot_ref, sem)
+    block = [pl.when(sub_ref[0] >= 0) for at in range(4)]
 
     @pl.when(step == 0)
     def _():
         fetch.start()
         acc_ref[...] = jnp.zeros_like(acc_ref)
         prod_ref[...] = jnp.zeros_like(prod_ref)
-        place_channels(first_ref, left_ref)
-
-    add_powers(jnp.maximum(step - 1, 0), east_ref, sub_ref, prod_ref, acc_ref)
-    for ch in range(2):
-        for part in range(2):
-            prod_ref[ch, part] = lax.dot_general(
-                left_ref[ch, part], w_ref[ch, 256 * part : 256 * part + 512, :], NN, preferred_element_type=F32
+        place_channels(first_ref, left_ref.at[0])
+
+    def multiply(slot):
+        for ch in range(2):
+            prod_ref[slot, ch] = lax.dot_general(
+                left_ref[slot, ch], w_ref[2 * slot + ch], NN, preferred_element_type=F32
             )
-    place_channels(next_ref, left_ref)
+
+    def powers(channel, slot, pair):
+        add_powers((channel,), pair, east_ref, sub_ref, prod_ref.at[slot], acc_ref)
+
+    @block[0]
+    def _():
+        powers(0, 1, jnp.maximum(2 * step - 1, 0))
+        multiply(0)
+
+    @block[1]
+    def _():
+        powers(1, 1, jnp.maximum(2 * step - 1, 0))
+        place_channels(odd_ref, left_ref.at[1])
+
+    @block[2]
+    def _():
+        powers(0, 0, 2 * step)
+        multiply(1)
+
+    @block[3]
+    def _():
+        powers(1, 0, 2 * step)
+        place_channels(next_ref, left_ref.at[0])
 
     @pl.when(step == pl.num_programs(0) - 1)
     def _():
-        add_powers(step, east_ref, sub_ref, prod_ref, acc_ref)
+        powers(0, 1, 2 * step + 1)
+        powers(1, 1, 2 * step + 1)
         total = acc_ref[...].reshape(64, 1024)
         top = total.astype(BF16)
         rest = (total - top.astype(F32)).astype(BF16)
@@ -298,29 +321,30 @@
     return pl.pallas_call(
         beam_kernel,
         name="beams",
-        grid=(8,),
+        grid=(4,),
         out_shape=jax.ShapeDtypeStruct((1024, 128), BF16),
         in_specs=[
             smem,
             smem,
             pl.BlockSpec((64, 16, 128), lambda i: (0, 0, 0)),
-            pl.BlockSpec((64, 16, 128), lambda i: (0, jnp.minimum(i + 1, 7), 0)),
-            pl.BlockSpec((2, 768, 256), lambda i: (i, 0, 0)),
+            pl.BlockSpec((64, 16, 128), lambda i: (0, 2 * i + 1, 0)),
+            pl.BlockSpec((64, 16, 128), lambda i: (0, jnp.minimum(2 * i + 2, 7), 0)),
+            pl.BlockSpec((4, 512, 512), lambda i: (i, 0, 0)),
             pl.BlockSpec(memory_space=pl.ANY),
         ],
         out_specs=pl.BlockSpec((1024, 128), lambda i: (0, 0)),
         scratch_shapes=[
             pltpu.VMEM((2, 2, 128, 512), BF16),
-            pltpu.VMEM((2, 2, 128, 256), F32),
+            pltpu.VMEM((2, 2, 128, 512), F32),
             pltpu.VMEM((4, 16, 1024), F32),
             pltpu.VMEM((1024, 1024), BF16),
             pltpu.SemaphoreType.DMA,
         ],
         compiler_params=pltpu.CompilerParams(vmem_limit_bytes=51 * MIB),
         cost_estimate=pl.CostEstimate(
-            flops=2_000_000_000, bytes_accessed=11_000_000, transcendentals=0
+            flops=2_000_000_000, bytes_accessed=13_000_000, transcendentals=0
         ),
-    )(east, subs, turned, turned, weights, hot)
+    )(east, subs, turned, turned, turned, weights, hot)
 
 
 def weight_kernel(step_ref, out_ref):
@@ -341,10 +365,11 @@
         for tile in range(16):
             if tile:
                 cos, sin = cos * more_cos - sin * more_sin, sin * more_cos + cos * more_sin
-            r0 = 16 * tile
-            out_ref[ch, r0 : r0 + 16, :] = cos.astype(BF16)
-            out_ref[ch, 256 + r0 : 272 + r0, :] = sin.astype(BF16)
-            out_ref[ch, 512 + r0 : 528 + r0, :] = cos.astype(BF16)
+            top, low = slice(16 * tile, 16 * tile + 16), slice(256 + 16 * tile, 272 + 16 * tile)
+            out_ref[ch, top, 0:256] = cos.astype(BF16)
+            out_ref[ch, top, 256:512] = sin.astype(BF16)
+            out_ref[ch, low, 0:256] = (-sin).astype(BF16)
+            out_ref[ch, low, 256:512] = cos.astype(BF16)
 
 
 def beam_weights(channels):
@@ -354,16 +379,16 @@
         weight_kernel,
         name="weights",
         grid=(8,),
-        out_shape=jax.ShapeDtypeStruct((16, 768, 256), BF16),
+        out_shape=jax.ShapeDtypeStruct((16, 512, 512), BF16),
         in_specs=[pl.BlockSpec(memory_space=pltpu.SMEM)],
-        out_specs=pl.BlockSpec((2, 768, 256), lambda i: (i, 0, 0)),
+        out_specs=pl.BlockSpec((2, 512, 512), lambda i: (i, 0, 0)),
         compiler_params=pltpu.CompilerParams(vmem_limit_bytes=56 * MIB),
         cost_estimate=pl.CostEstimate(flops=20_000_000, bytes_accessed=6_000_000, transcendentals=500_000),
     )(steps)
     four = jnp.arange(4, dtype=jnp.int32)
     turns = steps[:, None] * (four[:, None] * four[None, :]).reshape(1, 16) % (scale * 4)
     phases = (2.0 * math.pi / (scale * 4)) * turns.astype(F32)
-    return weights, jnp.concatenate([jnp.cos(phases), jnp.sin(phases)], axis=1)
+    return weights, 2.0 * jnp.concatenate([jnp.cos(phases), jnp.sin(phases)], axis=1)
 
 
 def gather_kernel(x_ref, out_ref):

time: 104 us -> 103 us (level)
  no operation moved by 1% of the time
where the time goes in v3:
time: 103 us; the launch traced here: 102 us
  starting transfers between devices  41.6 us (40%)
  waiting for transfers between devices  29 us (28%)
  Pallas kernels  27.1 us (26%)
  local copies, waits for them, and re-layouts  2.34 us (2%)
  other arithmetic  2.28 us (2%)
    ppermute x3, starting transfers between devices, from_band(): lax.ppermute(block, 'band', [(i, (i + back) % count) for i in range(count)])  10.8 us
    ppermute x3, waiting for transfers between devices, from_band(): lax.ppermute(block, 'band', [(i, (i + back) % count) for i in range(count)])  10.8 us
    all_to_all x1, starting transfers between devices, local(): lax.all_to_all(chunks, 'grp', split_axis=0, concat_axis=0, tiled=True)  9.17 us
    pallas_call x1, Pallas kernels, beams(): pl.pallas_call(beam_kernel, name='beams', grid=(4,), out_shape=jax.ShapeD...  8.93 us
    all_to_all x1, waiting for transfers between devices, local(): lax.all_to_all(gather_residues(pieces), ('grp', 'band'), split_axis=0, co...  7.69 us
    all_to_all x1, waiting for transfers between devices, local(): lax.all_to_all(sums, 'grp', split_axis=0, concat_axis=0, tiled=True, axis...  7.42 us
    all_to_all x1, starting transfers between devices, local(): lax.all_to_all(sums, 'grp', split_axis=0, concat_axis=0, tiled=True, axis...  6.72 us
    all_to_all x1, starting transfers between devices, local(): lax.all_to_all(gather_residues(pieces), ('grp', 'band'), split_axis=0, co...  6.66 us
  transfers between devices with their start and end apart: 8, of which 5 were waited for; matrix products, arithmetic and copies ran while one was open for 4% of the time, Pallas kernels for 11%

profile of v3, /device:TPU:1, one launch (start us, length us, event | category | flops | bytes accessed | tf_op | source)
XLA Modules:
  0.0 102.5 jit_solution(3030095738728722921)
XLA Ops:
  0.0 1.0 slice.28
  1.0 5.7 %collective-permute-start.3 = (bf16[2,32,2048]{2,1,0:T(8,128)(2,1)S(1)}, bf16[2,32,2048]{2,1,0:T(8,128)(2,1)S(1)}, u32[]{:S(2)}, u32[]{:S(2)}) collective-permute-start(bf16[2,32,2048]{2,1,0:T(8,128)(2,1)S(1)} %slice.28), channel_id=1, source_target_pairs={{0,1},{1,2},{2,3},{4,5},{5,6},{6,7},{8,9},{9,10},{10,11},{12,13},{... | collective-permute-start | bytes 786440 | tf_op jit(solution)/shard_map/ppermute | solution.py:162
  6.7 0.9 slice.29
  7.6 2.5 %collective-permute-start.4 = (bf16[1,32,2048]{2,1,0:T(8,128)(2,1)S(1)}, bf16[1,32,2048]{2,1,0:T(8,128)(2,1)S(1)}, u32[]{:S(2)}, u32[]{:S(2)}) collective-permute-start(bf16[1,32,2048]{2,1,0:T(8,128)(2,1)S(1)} %slice.29), channel_id=1, source_target_pairs={{0,3},{1,0},{2,1},{3,2},{4,7},{5,4},{6,5},{7,6},{8,11},{9,8},{10,9... | collective-permute-start | bytes 393224 | tf_op jit(solution)/shard_map/ppermute | solution.py:163
  10.1 0.0 copy-start
  10.1 0.0 copy-start.1
  10.1 5.0 %inner_frames.1.part_hbm = bf16[8,512,256]{2,1,0:T(8,128)(2,1)} custom-call(bf16[16,32,2048]{2,1,0:T(8,128)(2,1)} %v_hbm.1, f32[4,2048]{1,0:T(4,128)} %constant.151.clone.win_ref), custom_call_target="tpu_custom_call" | custom-call | flops 20000000 | bytes 4000000 | tf_op jit(solution)/shard_map/inner_frames/pallas_call | solution.py:167
  15.1 3.1 %collective-permute-done.4.next_ref = bf16[1,32,2048]{2,1,0:T(8,128)(2,1)S(1)} collective-permute-done((bf16[1,32,2048]{2,1,0:T(8,128)(2,1)S(1)}, bf16[1,32,2048]{2,1,0:T(8,128)(2,1)S(1)}, u32[]{:S(2)}, u32[]{:S(2)}) %collective-permute-start.4) | collective-permute-done | bytes 131104 | tf_op jit(solution)/shard_map/ppermute | solution.py:163
  18.2 0.0 collective-permute-done.3.prev_ref
  18.2 0.0 copy-done
  18.2 0.0 copy-done.1
  18.2 3.7 %spectra.1 = bf16[16,4,128,128]{3,2,1,0:T(8,128)(2,1)} custom-call(s32[1]{0:T(128)} %bitcast.6.band_ref, bf16[8,512,256]{2,1,0:T(8,128)(2,1)} %inner_frames.1.part_hbm, bf16[16,32,2048]{2,1,0:T(8,128)(2,1)} %v_hbm.1, bf16[2,32,2048]{2,1,0:T(8,128)(2,1)S(1)} %collective-permute-done.3.prev_ref, bf16[1,32,2048]{2,1,0:T(8,128)(2,1)S(1)} %collective-permute-done.4.next_ref, ...), custom_call_target="tpu_custom_call" | custom-call | flops 600000000 | bytes 6000000 | tf_op jit(solution)/shard_map/spectra/pallas_call | solution.py:176
  21.9 0.0 copy-start.5
  21.9 0.0 copy-start.3
  22.0 0.0 copy-start.4
  22.0 9.2 %all-to-all-start = ((bf16[64,128,128]{2,1,0:T(8,128)(2,1)}), bf16[64,128,128]{2,1,0:T(8,128)(2,1)S(1)}, u32[]{:S(2)}, u32[]{:S(2)}) async-start(bf16[64,128,128]{2,1,0:T(8,128)(2,1)} %bitcast.15), calls=%async_computation | async-start | bytes 4194304 | tf_op jit(solution)/shard_map/all_to_all | solution.py:513
  31.2 0.1 pad.14.clone
  31.3 0.0 copy-done.5
  31.3 0.0 copy-done.3
  31.3 0.1 fusion.6
  31.4 3.2 %collective-permute-start = (s32[8,128]{1,0:T(8,128)S(1)}, s32[8,128]{1,0:T(8,128)S(1)}, u32[]{:S(2)}, u32[]{:S(2)}) collective-permute-start(s32[8,128]{1,0:T(8,128)S(1)} %get-tuple-element.13), channel_id=1, source_target_pairs={{0,1},{1,2},{2,3},{3,0},{4,5},{5,6},{6,7},{7,4},{8,9},{9,10},{10,1... | collective-permute-start | bytes 12296 | tf_op jit(solution)/shard_map/ppermute | solution.py:484
  34.6 4.2 %collective-permute-start.1 = (s32[8,128]{1,0:T(8,128)S(1)}, s32[8,128]{1,0:T(8,128)S(1)}, u32[]{:S(2)}, u32[]{:S(2)}) collective-permute-start(s32[8,128]{1,0:T(8,128)S(1)} %get-tuple-element.14), channel_id=1, source_target_pairs={{0,2},{1,3},{2,0},{3,1},{4,6},{5,7},{6,4},{7,5},{8,10},{9,11},{10,... | collective-permute-start | bytes 12296 | tf_op jit(solution)/shard_map/ppermute | solution.py:484
  38.8 3.4 %collective-permute-start.2 = (s32[8,128]{1,0:T(8,128)S(1)}, s32[8,128]{1,0:T(8,128)S(1)}, u32[]{:S(2)}, u32[]{:S(2)}) collective-permute-start(s32[8,128]{1,0:T(8,128)S(1)} %get-tuple-element.15), channel_id=1, source_target_pairs={{0,3},{1,0},{2,1},{3,2},{4,7},{5,4},{6,5},{7,6},{8,11},{9,8},{10,9... | collective-permute-start | bytes 12296 | tf_op jit(solution)/shard_map/ppermute | solution.py:484
  42.2 0.1 mul.84
  42.3 0.0 copy-start.6
  42.3 0.1 fusion.8
  42.4 0.1 maximum_multiply_fusion.east_ref
  42.5 0.0 copy-done.4
  42.5 1.7 %fusion.hot_hbm = bf16[1024,1024]{1,0:T(8,128)(2,1)} fusion(s32[1024]{0:T(1024)S(1)} %bitcast.16), kind=kLoop, calls=%fused_computation.1 | loop fusion | flops 2097152 | bytes 2101248 | tf_op jit(solution)/shard_map/convert_element_type | solution.py:518
  44.3 0.0 copy-done.6
  44.3 6.5 %weights.1.w_ref = bf16[16,512,512]{2,1,0:T(8,128)(2,1)} custom-call(s32[16]{0:T(128)} %copy-done.6), custom_call_target="tpu_custom_call" | custom-call | flops 20000000 | bytes 6000000 | tf_op jit(solution)/shard_map/weights/pallas_call | solution.py:378
  50.7 9.1 %collective-permute-done = s32[8,128]{1,0:T(8,128)S(1)} collective-permute-done((s32[8,128]{1,0:T(8,128)S(1)}, s32[8,128]{1,0:T(8,128)S(1)}, u32[]{:S(2)}, u32[]{:S(2)}) %collective-permute-start) | collective-permute-done | bytes 4128 | tf_op jit(solution)/shard_map/ppermute | solution.py:484
  59.8 1.7 %collective-permute-done.1 = s32[8,128]{1,0:T(8,128)S(1)} collective-permute-done((s32[8,128]{1,0:T(8,128)S(1)}, s32[8,128]{1,0:T(8,128)S(1)}, u32[]{:S(2)}, u32[]{:S(2)}) %collective-permute-start.1) | collective-permute-done | bytes 4128 | tf_op jit(solution)/shard_map/ppermute | solution.py:484
  61.5 0.0 collective-permute-done.2
  61.5 0.1 select_add_fusion.4
  61.6 0.1 reshape.57
  61.7 0.1 constant_dynamic-slice_fusion
  61.7 0.1 copy.9
  61.8 0.0 copy-start.2
  61.8 0.0 all-to-all-done.first_ref.odd_ref.next_ref
  61.9 8.9 %beams.1 = bf16[1024,128]{1,0:T(8,128)(2,1)} custom-call(f32[16,32]{1,0:T(8,128)S(1)} %maximum_multiply_fusion.east_ref, s32[16]{0:T(128)S(1)} %and_select_fusion.sub_ref, bf16[64,128,128]{2,1,0:T(8,128)(2,1)S(1)} %all-to-all-done.first_ref.odd_ref.next_ref, bf16[64,128,128]{2,1,0:T(8,128)(2,1)S(1)} %all-to-all-done.first_ref.odd_ref.next_ref, ...), custom_call_target="tpu_custom_call" | custom-call | flops 2000000000 | bytes 13000000 | tf_op jit(solution)/shard_map/beams/pallas_call | solution.py:321
  70.8 6.7 %all-to-all-start.1 = ((bf16[16,64,128]{2,1,0:T(8,128)(2,1)}), bf16[16,64,128]{2,1,0:T(8,128)(2,1)S(1)}, u32[]{:S(2)}, u32[]{:S(2)}) async-start(bf16[16,64,128]{2,1,0:T(8,128)(2,1)} %bitcast.9), calls=%async_computation.1 | async-start | bytes 524288 | tf_op jit(solution)/shard_map/all_to_all | solution.py:521
  77.6 0.1 select_add_fusion.2
  77.6 7.4 %all-to-all-done.1.x_ref = bf16[16,64,128]{2,1,0:T(8,128)(2,1)S(1)} async-done(((bf16[16,64,128]{2,1,0:T(8,128)(2,1)}), bf16[16,64,128]{2,1,0:T(8,128)(2,1)S(1)}, u32[]{:S(2)}, u32[]{:S(2)}) %all-to-all-start.1) | async-done | bytes 262176 | tf_op jit(solution)/shard_map/all_to_all | solution.py:521
  85.1 0.8 residues.1
  85.8 6.7 %all-to-all-start.2 = ((bf16[16,16,128]{2,1,0:T(8,128)(2,1)}), bf16[16,16,128]{2,1,0:T(8,128)(2,1)S(1)}, u32[]{:S(2)}, u32[]{:S(2)}) async-start(bf16[16,16,128]{2,1,0:T(8,128)(2,1)} %residues.1), calls=%async_computation.2 | async-start | bytes 131072 | tf_op jit(solution)/shard_map/all_to_all | solution.py:528
  92.5 0.1 select_add_fusion.3
  92.6 7.7 %all-to-all-done.2.x_ref = bf16[16,16,128]{2,1,0:T(8,128)(2,1)S(1)} async-done(((bf16[16,16,128]{2,1,0:T(8,128)(2,1)}), bf16[16,16,128]{2,1,0:T(8,128)(2,1)S(1)}, u32[]{:S(2)}, u32[]{:S(2)}) %all-to-all-start.2) | async-done | bytes 65568 | tf_op jit(solution)/shard_map/all_to_all | solution.py:528
  100.3 0.0 copy-done.2
  100.3 2.2 %series.1 = f32[64,16,128]{2,1,0:T(8,128)} custom-call(bf16[16,16,128]{2,1,0:T(8,128)(2,1)S(1)} %all-to-all-done.2.x_ref, bf16[4,128,256]{2,1,0:T(8,128)(2,1)S(1)} %copy-done.2, s32[16,128]{1,0:T(8,128)S(1)} %pad_add_fusion.delay_ref), custom_call_target="tpu_custom_call" | custom-call | flops 600000000 | bytes 1000000 | tf_op jit(solution)/shard_map/series/pallas_call | solution.py:468
  (12 shorter events, 0.1 us)
Async XLA Ops:
  1.0 17.2 %collective-permute-start.3 = (bf16[2,32,2048]{2,1,0:T(8,128)(2,1)S(1)}, bf16[2,32,2048]{2,1,0:T(8,128)(2,1)S(1)}, u32[]{:S(2)}, u32[]{:S(2)}) collective-permute-start(bf16[2,32,2048]{2,1,0:T(8,128)(2,1)S(1)} %slice.28), channel_id=1, source_target_pairs={{0,1},{1,2},{2,3},{4,5},{5,6},{6,7},{8,9},{9,10},{10,11},{12,13},{... | collective-permute-start | bytes 786440 | tf_op jit(solution)/shard_map/ppermute | solution.py:162
  7.6 10.6 %collective-permute-start.4 = (bf16[1,32,2048]{2,1,0:T(8,128)(2,1)S(1)}, bf16[1,32,2048]{2,1,0:T(8,128)(2,1)S(1)}, u32[]{:S(2)}, u32[]{:S(2)}) collective-permute-start(bf16[1,32,2048]{2,1,0:T(8,128)(2,1)S(1)} %slice.29), channel_id=1, source_target_pairs={{0,3},{1,0},{2,1},{3,2},{4,7},{5,4},{6,5},{7,6},{8,11},{9,8},{10,9... | collective-permute-start | bytes 393224 | tf_op jit(solution)/shard_map/ppermute | solution.py:163
  10.1 8.1 %copy-start = (bf16[8,256,256]{2,1,0:T(8,128)(2,1)S(1)}, bf16[8,256,256]{2,1,0:T(8,128)(2,1)}, u32[]{:S(2)}) copy-start(bf16[8,256,256]{2,1,0:T(8,128)(2,1)} %constant.152.clone.tab_hbm) | copy-start | bytes 3145732
  10.1 8.1 %copy-start.1 = (f32[4,2048]{1,0:T(4,128)S(1)}, f32[4,2048]{1,0:T(4,128)}, u32[]{:S(2)}) copy-start(f32[4,2048]{1,0:T(4,128)} %constant.151.clone.win_ref) | copy-start | bytes 98308
  21.9 9.4 %copy-start.5 = (s32[512,4]{0,1:T(4,128)S(1)}, s32[512,4]{0,1:T(4,128)}, u32[]{:S(2)}) copy-start(s32[512,4]{0,1:T(4,128)} %param.10) | copy-start | bytes 24580
  21.9 9.3 %copy-start.3 = (s32[256]{0:T(256)S(1)}, s32[256]{0:T(256)}, u32[]{:S(2)}) copy-start(s32[256]{0:T(256)} %param.9) | copy-start | bytes 3076
  22.0 20.6 %copy-start.4 = (s32[2,1024]{1,0:T(2,128)S(1)}, s32[2,1024]{1,0:T(2,128)}, u32[]{:S(2)}) copy-start(s32[2,1024]{1,0:T(2,128)} %param.8) | copy-start | bytes 24580
  22.0 39.9 %all-to-all-start = ((bf16[64,128,128]{2,1,0:T(8,128)(2,1)}), bf16[64,128,128]{2,1,0:T(8,128)(2,1)S(1)}, u32[]{:S(2)}, u32[]{:S(2)}) async-start(bf16[64,128,128]{2,1,0:T(8,128)(2,1)} %bitcast.15), calls=%async_computation | async-start | bytes 4194304 | tf_op jit(solution)/shard_map/all_to_all | solution.py:513
  31.4 28.4 %collective-permute-start = (s32[8,128]{1,0:T(8,128)S(1)}, s32[8,128]{1,0:T(8,128)S(1)}, u32[]{:S(2)}, u32[]{:S(2)}) collective-permute-start(s32[8,128]{1,0:T(8,128)S(1)} %get-tuple-element.13), channel_id=1, source_target_pairs={{0,1},{1,2},{2,3},{3,0},{4,5},{5,6},{6,7},{7,4},{8,9},{9,10},{10,1... | collective-permute-start | bytes 12296 | tf_op jit(solution)/shard_map/ppermute | solution.py:484
  34.6 26.9 %collective-permute-start.1 = (s32[8,128]{1,0:T(8,128)S(1)}, s32[8,128]{1,0:T(8,128)S(1)}, u32[]{:S(2)}, u32[]{:S(2)}) collective-permute-start(s32[8,128]{1,0:T(8,128)S(1)} %get-tuple-element.14), channel_id=1, source_target_pairs={{0,2},{1,3},{2,0},{3,1},{4,6},{5,7},{6,4},{7,5},{8,10},{9,11},{10,... | collective-permute-start | bytes 12296 | tf_op jit(solution)/shard_map/ppermute | solution.py:484
  38.8 22.7 %collective-permute-start.2 = (s32[8,128]{1,0:T(8,128)S(1)}, s32[8,128]{1,0:T(8,128)S(1)}, u32[]{:S(2)}, u32[]{:S(2)}) collective-permute-start(s32[8,128]{1,0:T(8,128)S(1)} %get-tuple-element.15), channel_id=1, source_target_pairs={{0,3},{1,0},{2,1},{3,2},{4,7},{5,4},{6,5},{7,6},{8,11},{9,8},{10,9... | collective-permute-start | bytes 12296 | tf_op jit(solution)/shard_map/ppermute | solution.py:484
  42.3 2.0 %copy-start.6 = (s32[16]{0:T(128)}, s32[16]{0:T(128)S(1)}, u32[]{:S(2)}) copy-start(s32[16]{0:T(128)S(1)} %add_subtract_fusion.step_ref) | copy-start | bytes 196
  61.8 38.4 %copy-start.2 = (bf16[4,128,256]{2,1,0:T(8,128)(2,1)S(1)}, bf16[4,128,256]{2,1,0:T(8,128)(2,1)}, u32[]{:S(2)}) copy-start(bf16[4,128,256]{2,1,0:T(8,128)(2,1)} %constant.153.clone.tab_ref) | copy-start | bytes 786436
  70.8 14.3 %all-to-all-start.1 = ((bf16[16,64,128]{2,1,0:T(8,128)(2,1)}), bf16[16,64,128]{2,1,0:T(8,128)(2,1)S(1)}, u32[]{:S(2)}, u32[]{:S(2)}) async-start(bf16[16,64,128]{2,1,0:T(8,128)(2,1)} %bitcast.9), calls=%async_computation.1 | async-start | bytes 524288 | tf_op jit(solution)/shard_map/all_to_all | solution.py:521
  85.8 14.5 %all-to-all-start.2 = ((bf16[16,16,128]{2,1,0:T(8,128)(2,1)}), bf16[16,16,128]{2,1,0:T(8,128)(2,1)S(1)}, u32[]{:S(2)}, u32[]{:S(2)}) async-start(bf16[16,16,128]{2,1,0:T(8,128)(2,1)} %residues.1), calls=%async_computation.2 | async-start | bytes 131072 | tf_op jit(solution)/shard_map/all_to_all | solution.py:528

commit v4 on v3

--- a/solution.py
+++ b/solution.py
@@ -224,10 +224,10 @@
                         left_ref[ch, rows, cols] = tiles[m4][at : at + 4]
 
 
-def add_powers(channels, pair, east_ref, sub_ref, prod_ref, acc_ref):
+def add_powers(channels, pair, east_ref, chan_ref, residue_ref, prod_ref, acc_ref):
     for ch in channels:
         i = 2 * pair + ch
-        sub = sub_ref[i]
+        sub = chan_ref[16 * i + residue_ref[0]] % 4
         cos = [[east_ref[i, s * 4 + k] for k in range(4)] for s in range(4)]
         sin = [[east_ref[i, 16 + s * 4 + k] for k in range(4)] for s in range(4)]
         for t in range(2):
@@ -261,28 +261,37 @@
 
 
 def beam_kernel(
-    east_ref, sub_ref, first_ref, odd_ref, next_ref, w_ref, hot_hbm, out_ref,
-    left_ref, prod_ref, acc_ref, hot_ref, sem
+    east_ref, chan_ref, residue_ref, first_ref, odd_ref, next_ref, w_hbm, hot_hbm, out_ref,
+    left_ref, prod_ref, acc_ref, w_ref, hot_ref, w_sem, sem
 ):
     step = pl.program_id(0)
     fetch = pltpu.make_async_copy(hot_hbm, hot_ref, sem)
-    block = [pl.when(sub_ref[0] >= 0) for at in range(4)]
+
+    def weights(at):
+        four = pl.ds(4 * at, 4)
+        return pltpu.make_async_copy(w_hbm.at[four], w_ref.at[four], w_sem.at[at])
+
+    block = [pl.when(chan_ref[0] >= 0) for at in range(4)]
 
     @pl.when(step == 0)
     def _():
+        for at in range(4):
+            weights(at).start()
         fetch.start()
         acc_ref[...] = jnp.zeros_like(acc_ref)
         prod_ref[...] = jnp.zeros_like(prod_ref)
         place_channels(first_ref, left_ref.at[0])
 
+    weights(step).wait()
+
     def multiply(slot):
         for ch in range(2):
             prod_ref[slot, ch] = lax.dot_general(
-                left_ref[slot, ch], w_ref[2 * slot + ch], NN, preferred_element_type=F32
+                left_ref[slot, ch], w_ref[4 * step + 2 * slot + ch], NN, preferred_element_type=F32
             )
 
     def powers(channel, slot, pair):
-        add_powers((channel,), pair, east_ref, sub_ref, prod_ref.at[slot], acc_ref)
+        add_powers((channel,), pair, east_ref, chan_ref, residue_ref, prod_ref.at[slot], acc_ref)
 
     @block[0]
     def _():
@@ -316,7 +325,7 @@
         out_ref[...] = lax.dot_general(hot_ref[...], parts, NT, preferred_element_type=F32).astype(BF16)
 
 
-def beams(turned, east, subs, weights, hot):
+def beams(turned, east, chan_sub, residue, weights, hot):
     smem = pl.BlockSpec(memory_space=pltpu.SMEM)
     return pl.pallas_call(
         beam_kernel,
@@ -326,10 +335,11 @@
         in_specs=[
             smem,
             smem,
+            smem,
             pl.BlockSpec((64, 16, 128), lambda i: (0, 0, 0)),
             pl.BlockSpec((64, 16, 128), lambda i: (0, 2 * i + 1, 0)),
             pl.BlockSpec((64, 16, 128), lambda i: (0, jnp.minimum(2 * i + 2, 7), 0)),
-            pl.BlockSpec((4, 512, 512), lambda i: (i, 0, 0)),
+            pl.BlockSpec(memory_space=pl.ANY),
             pl.BlockSpec(memory_space=pl.ANY),
         ],
         out_specs=pl.BlockSpec((1024, 128), lambda i: (0, 0)),
@@ -337,14 +347,16 @@
             pltpu.VMEM((2, 2, 128, 512), BF16),
             pltpu.VMEM((2, 2, 128, 512), F32),
             pltpu.VMEM((4, 16, 1024), F32),
+            pltpu.VMEM((16, 512, 512), BF16),
             pltpu.VMEM((1024, 1024), BF16),
+            pltpu.SemaphoreType.DMA((4,)),
             pltpu.SemaphoreType.DMA,
         ],
         compiler_params=pltpu.CompilerParams(vmem_limit_bytes=51 * MIB),
         cost_estimate=pl.CostEstimate(
             flops=2_000_000_000, bytes_accessed=13_000_000, transcendentals=0
         ),
-    )(east, subs, turned, turned, turned, weights, hot)
+    )(east, chan_sub, residue.reshape(1), turned, turned, turned, weights, hot)
 
 
 def weight_kernel(step_ref, out_ref):
@@ -391,7 +403,7 @@
     return weights, 2.0 * jnp.concatenate([jnp.cos(phases), jnp.sin(phases)], axis=1)
 
 
-def gather_kernel(x_ref, out_ref):
+def gather_kernel(x_ref, delay_ref, out_ref):
     total = x_ref[0].astype(F32)
     for r in range(1, 16):
         total = total + x_ref[r].astype(F32)
@@ -402,19 +414,20 @@
     both = jnp.where(lane < 64, top, rest)
     for q in range(4):
         for band in range(4):
-            out_ref[4 * q + band] = both[16 * q : 16 * q + 16, :]
-
-
-def gather_residues(pieces):
+            out_ref[4 * q + band, 0:16] = both[16 * q : 16 * q + 16, :]
+            out_ref[4 * q + band, 16:24] = delay_ref[band]
+
+
+def gather_residues(pieces, delays):
     vmem = pl.BlockSpec(memory_space=pltpu.VMEM)
     return pl.pallas_call(
         gather_kernel,
         name="residues",
-        out_shape=jax.ShapeDtypeStruct((16, 16, 128), BF16),
-        in_specs=[vmem],
+        out_shape=jax.ShapeDtypeStruct((16, 24, 128), BF16),
+        in_specs=[vmem] * 2,
         out_specs=vmem,
         compiler_params=pltpu.CompilerParams(vmem_limit_bytes=4 * MIB),
-    )(pieces)
+    )(pieces, delays)
 
 
 def frame_tables():
@@ -429,15 +442,16 @@
     return table.reshape(4, 128, 256).astype(jnp.bfloat16)
 
 
-def series_kernel(x_ref, tab_ref, delay_ref, out_ref, hot_ref, left_ref):
+def series_kernel(x_ref, tab_ref, out_ref, hot_ref, left_ref):
     series = None
     for band in range(4):
-        rows = jnp.concatenate([x_ref[4 * q + band] for q in range(4)], axis=0)
+        rows = jnp.concatenate([x_ref[4 * q + band, 0:16] for q in range(4)], axis=0)
         term = lax.dot_general(rows, tab_ref[band], NN, preferred_element_type=F32)
         series = term if series is None else series + term
     ahead = lax.broadcasted_iota(jnp.int32, (64, 128), 0)
+    delays = [x_ref[band, 16:24].astype(F32).astype(jnp.int32) for band in range(4)]
     for s in range(16):
-        hit = (ahead + delay_ref[s : s + 1, :]) % 64 == 0
+        hit = (ahead + delays[s // 4][s % 4 : s % 4 + 1, :]) % 64 == 0
         hot = jnp.where(hit, 1.0, 0.0).astype(BF16)
         for th in range(4):
             cols = slice(128 * th, 128 * th + 128)
@@ -463,77 +477,63 @@
         out_ref[16 * th : 16 * th + 16] = out[:, 128 * th : 128 * th + 128].reshape(16, 16, 128)
 
 
-def series(sums, delays):
+def series(sums):
     vmem = pl.BlockSpec(memory_space=pltpu.VMEM)
     return pl.pallas_call(
         series_kernel,
         name="series",
         out_shape=jax.ShapeDtypeStruct((64, 16, 128), F32),
-        in_specs=[vmem] * 3,
+        in_specs=[vmem] * 2,
         out_specs=vmem,
         scratch_shapes=[pltpu.VMEM((1024, 512), BF16), pltpu.VMEM((2, 256, 1024), BF16)],
         compiler_params=pltpu.CompilerParams(vmem_limit_bytes=8 * MIB),
         cost_estimate=pl.CostEstimate(
             flops=600_000_000, bytes_accessed=1_000_000, transcendentals=0
         ),
-    )(sums, jnp.asarray(frame_tables()), delays)
-
-
-def from_band(block, back):
-    count = lax.axis_size("band")
-    return lax.ppermute(block, "band", [(i, (i + back) % count) for i in range(count)])
+    )(sums, jnp.asarray(frame_tables()))
 
 
 def local(voltages, steering, chan_sub, delays):
     groups, band_count = lax.axis_size("grp"), lax.axis_size("band")
     grp_at = lax.axis_index("grp")
     band_at = lax.axis_index("band")
-    turned_delays = jnp.transpose(delays)
-    small = []
-    for back in range(band_count):
-        trials = lax.dynamic_slice_in_dim(
-            turned_delays, (band_at + back) % band_count * 128, 128, axis=1
-        )
-        note = jnp.concatenate([chan_sub.reshape(2, 128), jnp.zeros((2, 128), jnp.int32), trials])
-        small.append(note if back == 0 else from_band(note, back))
     quarter_at = grp_at % 4
     residue = grp_at // 4
 
-    def owned_by(owner):
-        found = small[0] * 0
-        for back in range(band_count):
-            found = found + jnp.where((band_at - back) % band_count == owner, small[back], 0)
-        return found
-
-    quarter_subs = owned_by(quarter_at)[0:2].reshape(16, 16)
-    subs = lax.dynamic_slice_in_dim(quarter_subs, residue, 1, axis=1).reshape(16) % 4
-    all_delays = jnp.concatenate([owned_by(owner)[4:8] for owner in range(band_count)])
-
     chunks = spectra(voltages, band_at).reshape(64, 128, 128)
     turned = lax.all_to_all(chunks, "grp", split_axis=0, concat_axis=0, tiled=True)
 
+    place = lambda r, q, b: (4 * r + q) * band_count + b
+    swap = [
+        (place(r, q, b), place(r, b, q))
+        for r in range(groups // 4)
+        for q in range(4)
+        for b in range(band_count)
+    ]
+    quarter_subs = lax.ppermute(chan_sub, ("grp", "band"), swap)
     channels = quarter_at * 256 + 16 * jnp.arange(16, dtype=jnp.int32) + residue
     weights, east = beam_weights(channels)
     grid_at = steering[1] * 256 + steering[0]
     hot = (grid_at[:, None] == jnp.arange(1024, dtype=jnp.int32)[None, :]).astype(BF16)
-    sums = beams(turned, east, subs, weights, hot).reshape(16, 64, 128)
+    notes = jnp.transpose(delays.reshape(band_count, 128, 4), (0, 2, 1)).astype(BF16)
+    notes = jnp.pad(notes, ((0, 0), (0, 4), (0, 0)))
+    sums = beams(turned, east, quarter_subs, residue, weights, hot).reshape(16, 64, 128)
     planes = [[4 * r + q for r in range(groups // 4)] for q in range(4)]
     pieces = lax.all_to_all(
         sums, "grp", split_axis=0, concat_axis=0, tiled=True, axis_index_groups=planes
     )
     columns = [
-        [(4 * r + q) * band_count + band for q in range(4) for band in range(band_count)]
-        for r in range(groups // 4)
+        [place(r, q, b) for q in range(4) for b in range(band_count)] for r in range(groups // 4)
     ]
     every = lax.all_to_all(
-        gather_residues(pieces),
+        gather_residues(pieces, notes),
         ("grp", "band"),
         split_axis=0,
         concat_axis=0,
         tiled=True,
         axis_index_groups=columns,
     )
-    return series(every, all_delays)
+    return series(every)
 
 
 def solution(mesh):

time: 103 us -> 102 us (level)
  blocking collectives: 0 us -> 18.4 us
  starting transfers between devices: 41.6 us -> 26.2 us
  waiting for transfers between devices: 29 us -> 26.9 us
    all_to_all x0 -> x1, blocking collectives: none -> 18.4 us  [local(): lax.all_to_all(gather_residues(pieces, notes), ('grp', 'band'), split_axi...]
    all_to_all x1 -> x0, waiting for transfers between devices: 7.69 us -> none  [local(): lax.all_to_all(gather_residues(pieces), ('grp', 'band'), split_axis=0, co...]
    all_to_all x1, waiting for transfers between devices: 0.01 us -> 7.11 us  [local(): lax.all_to_all(chunks, 'grp', split_axis=0, concat_axis=0, tiled=True)]
    all_to_all x1 -> x0, starting transfers between devices: 6.66 us -> none  [local(): lax.all_to_all(gather_residues(pieces), ('grp', 'band'), split_axis=0, co...]
    ppermute x3 -> x1, starting transfers between devices: 10.8 us -> 5.45 us  [local(): quarter_subs = lax.ppermute(chan_sub, ('grp', 'band'), swap)]
    all_to_all x1, starting transfers between devices: 6.72 us -> 3.55 us  [local(): lax.all_to_all(sums, 'grp', split_axis=0, concat_axis=0, tiled=True, axis...]
    ppermute x3 -> x1, waiting for transfers between devices: 10.8 us -> 8.48 us  [local(): quarter_subs = lax.ppermute(chan_sub, ('grp', 'band'), swap)]
  transfers between devices with their start and end apart: 8 -> 5, of which waited for: 5 -> 4; matrix products, arithmetic and copies ran while one was open for 4% -> 3% of each run, Pallas kernels for 11% -> 11%
where the time goes in v4:
time: 102 us
  waiting for transfers between devices  26.9 us (26%)
  starting transfers between devices  26.2 us (26%)
  Pallas kernels  26.2 us (26%)
  blocking collectives  18.4 us (18%)
  local copies, waits for them, and re-layouts  2 us (2%)
  other arithmetic  1.96 us (2%)
    all_to_all x1, blocking collectives, local(): lax.all_to_all(gather_residues(pieces, notes), ('grp', 'band'), split_axi...  18.4 us
    all_to_all x1, starting transfers between devices, local(): lax.all_to_all(chunks, 'grp', split_axis=0, concat_axis=0, tiled=True)  9.03 us
    pallas_call x1, Pallas kernels, beams(): pl.pallas_call(beam_kernel, name='beams', grid=(4,), out_shape=jax.ShapeD...  8.77 us
    ppermute x1, waiting for transfers between devices, local(): quarter_subs = lax.ppermute(chan_sub, ('grp', 'band'), swap)  8.48 us
    all_to_all x1, waiting for transfers between devices, local(): lax.all_to_all(sums, 'grp', split_axis=0, concat_axis=0, tiled=True, axis...  8.28 us
    all_to_all x1, waiting for transfers between devices, local(): lax.all_to_all(chunks, 'grp', split_axis=0, concat_axis=0, tiled=True)  7.11 us
    pallas_call x1, Pallas kernels, beam_weights(): pl.pallas_call(weight_kernel, name='weights', grid=(8,), out_shape=jax.Sh...  6.44 us
    ppermute x1, starting transfers between devices, spectra(): lax.ppermute(voltages[14:16], 'band', [(i, i + 1) for i in range(band_cou...  5.73 us
  transfers between devices with their start and end apart: 5, of which 4 were waited for; matrix products, arithmetic and copies ran while one was open for 3% of the time, Pallas kernels for 11%

profile of v4, /device:TPU:1, one launch (start us, length us, event | category | flops | bytes accessed | tf_op | source)
XLA Modules:
  0.0 101.9 jit_solution(16195561412808344270)
XLA Ops:
  0.0 1.0 slice.12
  1.0 5.7 %collective-permute-start.1 = (bf16[2,32,2048]{2,1,0:T(8,128)(2,1)S(1)}, bf16[2,32,2048]{2,1,0:T(8,128)(2,1)S(1)}, u32[]{:S(2)}, u32[]{:S(2)}) collective-permute-start(bf16[2,32,2048]{2,1,0:T(8,128)(2,1)S(1)} %slice.12), channel_id=1, source_target_pairs={{0,1},{1,2},{2,3},{4,5},{5,6},{6,7},{8,9},{9,10},{10,11},{12,13},{... | collective-permute-start | bytes 786440 | tf_op jit(solution)/shard_map/ppermute | solution.py:162
  6.7 0.9 slice.13
  7.6 2.5 %collective-permute-start.2 = (bf16[1,32,2048]{2,1,0:T(8,128)(2,1)S(1)}, bf16[1,32,2048]{2,1,0:T(8,128)(2,1)S(1)}, u32[]{:S(2)}, u32[]{:S(2)}) collective-permute-start(bf16[1,32,2048]{2,1,0:T(8,128)(2,1)S(1)} %slice.13), channel_id=1, source_target_pairs={{0,3},{1,0},{2,1},{3,2},{4,7},{5,4},{6,5},{7,6},{8,11},{9,8},{10,9... | collective-permute-start | bytes 393224 | tf_op jit(solution)/shard_map/ppermute | solution.py:163
  10.1 0.0 copy-start
  10.1 0.0 copy-start.1
  10.1 5.1 %inner_frames.1.part_hbm = bf16[8,512,256]{2,1,0:T(8,128)(2,1)} custom-call(bf16[16,32,2048]{2,1,0:T(8,128)(2,1)} %v_hbm.1, f32[4,2048]{1,0:T(4,128)} %constant.69.clone.win_ref), custom_call_target="tpu_custom_call" | custom-call | flops 20000000 | bytes 4000000 | tf_op jit(solution)/shard_map/inner_frames/pallas_call | solution.py:167
  15.2 3.0 %collective-permute-done.2.next_ref = bf16[1,32,2048]{2,1,0:T(8,128)(2,1)S(1)} collective-permute-done((bf16[1,32,2048]{2,1,0:T(8,128)(2,1)S(1)}, bf16[1,32,2048]{2,1,0:T(8,128)(2,1)S(1)}, u32[]{:S(2)}, u32[]{:S(2)}) %collective-permute-start.2) | collective-permute-done | bytes 131104 | tf_op jit(solution)/shard_map/ppermute | solution.py:163
  18.2 0.0 collective-permute-done.1.prev_ref
  18.2 0.0 copy-done
  18.2 0.0 copy-done.1
  18.2 3.7 %spectra.1 = bf16[16,4,128,128]{3,2,1,0:T(8,128)(2,1)} custom-call(s32[1]{0:T(128)} %bitcast.1.band_ref, bf16[8,512,256]{2,1,0:T(8,128)(2,1)} %inner_frames.1.part_hbm, bf16[16,32,2048]{2,1,0:T(8,128)(2,1)} %v_hbm.1, bf16[2,32,2048]{2,1,0:T(8,128)(2,1)S(1)} %collective-permute-done.1.prev_ref, bf16[1,32,2048]{2,1,0:T(8,128)(2,1)S(1)} %collective-permute-done.2.next_ref, ...), custom_call_target="tpu_custom_call" | custom-call | flops 600000000 | bytes 6000000 | tf_op jit(solution)/shard_map/spectra/pallas_call | solution.py:176
  21.9 0.0 copy-start.6
  21.9 0.0 copy-start.3
  21.9 9.0 %all-to-all-start = ((bf16[64,128,128]{2,1,0:T(8,128)(2,1)}), bf16[64,128,128]{2,1,0:T(8,128)(2,1)S(1)}, u32[]{:S(2)}, u32[]{:S(2)}) async-start(bf16[64,128,128]{2,1,0:T(8,128)(2,1)} %bitcast.9), calls=%async_computation | async-start | bytes 4194304 | tf_op jit(solution)/shard_map/all_to_all | solution.py:504
  31.0 0.0 copy-done.6
  31.0 5.5 %collective-permute-start = (s32[256]{0:T(256)S(1)}, s32[256]{0:T(256)S(1)}, u32[]{:S(2)}, u32[]{:S(2)}) collective-permute-start(s32[256]{0:T(256)S(1)} %copy-done.6), channel_id=1, source_target_pairs={{0,0},{1,4},{2,8},{3,12},{4,1},{5,5},{6,9},{7,13},{8,2},{9,6},{10,... | collective-permute-start | bytes 3080 | tf_op jit(solution)/shard_map/ppermute | solution.py:513
  36.5 0.1 mul.72
  36.6 0.0 copy-start.5
  36.6 0.1 fusion.5
  36.7 0.1 maximum_multiply_fusion.east_ref
  36.8 0.0 copy-done.3
  36.8 1.7 %fusion.hot_hbm = bf16[1024,1024]{1,0:T(8,128)(2,1)} fusion(s32[1024]{0:T(1024)S(1)} %bitcast.10), kind=kLoop, calls=%fused_computation.1 | loop fusion | flops 2097152 | bytes 2101248 | tf_op jit(solution)/shard_map/convert_element_type | solution.py:517
  38.5 0.0 copy-done.5
  38.5 6.4 %weights.1.w_hbm = bf16[16,512,512]{2,1,0:T(8,128)(2,1)} custom-call(s32[16]{0:T(128)} %copy-done.5), custom_call_target="tpu_custom_call" | custom-call | flops 20000000 | bytes 6000000 | tf_op jit(solution)/shard_map/weights/pallas_call | solution.py:390
  45.0 8.5 %collective-permute-done.chan_ref = s32[256]{0:T(256)S(1)} collective-permute-done((s32[256]{0:T(256)S(1)}, s32[256]{0:T(256)S(1)}, u32[]{:S(2)}, u32[]{:S(2)}) %collective-permute-start) | collective-permute-done | bytes 1056 | tf_op jit(solution)/shard_map/ppermute | solution.py:513
  53.5 7.1 %all-to-all-done.first_ref.odd_ref.next_ref = bf16[64,128,128]{2,1,0:T(8,128)(2,1)S(1)} async-done(((bf16[64,128,128]{2,1,0:T(8,128)(2,1)}), bf16[64,128,128]{2,1,0:T(8,128)(2,1)S(1)}, u32[]{:S(2)}, u32[]{:S(2)}) %all-to-all-start) | async-done | bytes 2097184 | tf_op jit(solution)/shard_map/all_to_all | solution.py:504
  60.6 0.0 copy-start.4
  60.6 0.0 copy-start.2
  60.6 8.8 %beams.1 = bf16[1024,128]{1,0:T(8,128)(2,1)} custom-call(f32[16,32]{1,0:T(8,128)S(1)} %maximum_multiply_fusion.east_ref, s32[256]{0:T(256)S(1)} %collective-permute-done.chan_ref, s32[1]{0:T(128)} %bitcast.residue_ref, bf16[64,128,128]{2,1,0:T(8,128)(2,1)S(1)} %all-to-all-done.first_ref.odd_ref.next_ref, ...), custom_call_target="tpu_custom_call" | custom-call | flops 2000000000 | bytes 13000000 | tf_op jit(solution)/shard_map/beams/pallas_call | solution.py:330
  69.4 3.5 %all-to-all-start.1 = ((bf16[16,64,128]{2,1,0:T(8,128)(2,1)}), bf16[16,64,128]{2,1,0:T(8,128)(2,1)S(1)}, u32[]{:S(2)}, u32[]{:S(2)}) async-start(bf16[16,64,128]{2,1,0:T(8,128)(2,1)} %bitcast.4), calls=%async_computation.1 | async-start | bytes 524288 | tf_op jit(solution)/shard_map/all_to_all | solution.py:522
  72.9 0.0 copy-done.4
  72.9 8.3 %all-to-all-done.1.x_ref = bf16[16,64,128]{2,1,0:T(8,128)(2,1)S(1)} async-done(((bf16[16,64,128]{2,1,0:T(8,128)(2,1)}), bf16[16,64,128]{2,1,0:T(8,128)(2,1)S(1)}, u32[]{:S(2)}, u32[]{:S(2)}) %all-to-all-start.1) | async-done | bytes 262176 | tf_op jit(solution)/shard_map/all_to_all | solution.py:522
  81.2 0.1 residues.1
  81.3 18.4 %all_to_all.15.x_ref = bf16[16,24,128]{2,1,0:T(8,128)(2,1)S(1)} all-to-all(bf16[16,24,128]{2,1,0:T(8,128)(2,1)S(1)} %residues.1), channel_id=1, replica_groups={{0,1,2,3,4,5,6,7,8,9,10,11,12,13,14,15},{16,17,18,19,20,21,22,23,24,25,..., dimensions={0} | all-to-all | bytes 196608 | tf_op jit(solution)/shard_map/all_to_all | solution.py:528
  99.7 0.0 copy-done.2
  99.7 2.2 %series.1 = f32[64,16,128]{2,1,0:T(8,128)} custom-call(bf16[16,24,128]{2,1,0:T(8,128)(2,1)S(1)} %all_to_all.15.x_ref, bf16[4,128,256]{2,1,0:T(8,128)(2,1)S(1)} %copy-done.2), custom_call_target="tpu_custom_call" | custom-call | flops 600000000 | bytes 1000000 | tf_op jit(solution)/shard_map/series/pallas_call | solution.py:482
  (5 shorter events, 0.0 us)
Async XLA Ops:
  1.0 17.2 %collective-permute-start.1 = (bf16[2,32,2048]{2,1,0:T(8,128)(2,1)S(1)}, bf16[2,32,2048]{2,1,0:T(8,128)(2,1)S(1)}, u32[]{:S(2)}, u32[]{:S(2)}) collective-permute-start(bf16[2,32,2048]{2,1,0:T(8,128)(2,1)S(1)} %slice.12), channel_id=1, source_target_pairs={{0,1},{1,2},{2,3},{4,5},{5,6},{6,7},{8,9},{9,10},{10,11},{12,13},{... | collective-permute-start | bytes 786440 | tf_op jit(solution)/shard_map/ppermute | solution.py:162
  7.6 10.6 %collective-permute-start.2 = (bf16[1,32,2048]{2,1,0:T(8,128)(2,1)S(1)}, bf16[1,32,2048]{2,1,0:T(8,128)(2,1)S(1)}, u32[]{:S(2)}, u32[]{:S(2)}) collective-permute-start(bf16[1,32,2048]{2,1,0:T(8,128)(2,1)S(1)} %slice.13), channel_id=1, source_target_pairs={{0,3},{1,0},{2,1},{3,2},{4,7},{5,4},{6,5},{7,6},{8,11},{9,8},{10,9... | collective-permute-start | bytes 393224 | tf_op jit(solution)/shard_map/ppermute | solution.py:163
  10.1 8.1 %copy-start = (bf16[8,256,256]{2,1,0:T(8,128)(2,1)S(1)}, bf16[8,256,256]{2,1,0:T(8,128)(2,1)}, u32[]{:S(2)}) copy-start(bf16[8,256,256]{2,1,0:T(8,128)(2,1)} %constant.70.clone.tab_hbm) | copy-start | bytes 3145732
  10.1 8.1 %copy-start.1 = (f32[4,2048]{1,0:T(4,128)S(1)}, f32[4,2048]{1,0:T(4,128)}, u32[]{:S(2)}) copy-start(f32[4,2048]{1,0:T(4,128)} %constant.69.clone.win_ref) | copy-start | bytes 98308
  21.9 9.1 %copy-start.6 = (s32[256]{0:T(256)S(1)}, s32[256]{0:T(256)}, u32[]{:S(2)}) copy-start(s32[256]{0:T(256)} %param.9) | copy-start | bytes 3076
  21.9 14.9 %copy-start.3 = (s32[2,1024]{1,0:T(2,128)S(1)}, s32[2,1024]{1,0:T(2,128)}, u32[]{:S(2)}) copy-start(s32[2,1024]{1,0:T(2,128)} %param.8) | copy-start | bytes 24580
  21.9 38.6 %all-to-all-start = ((bf16[64,128,128]{2,1,0:T(8,128)(2,1)}), bf16[64,128,128]{2,1,0:T(8,128)(2,1)S(1)}, u32[]{:S(2)}, u32[]{:S(2)}) async-start(bf16[64,128,128]{2,1,0:T(8,128)(2,1)} %bitcast.9), calls=%async_computation | async-start | bytes 4194304 | tf_op jit(solution)/shard_map/all_to_all | solution.py:504
  31.0 22.5 %collective-permute-start = (s32[256]{0:T(256)S(1)}, s32[256]{0:T(256)S(1)}, u32[]{:S(2)}, u32[]{:S(2)}) collective-permute-start(s32[256]{0:T(256)S(1)} %copy-done.6), channel_id=1, source_target_pairs={{0,0},{1,4},{2,8},{3,12},{4,1},{5,5},{6,9},{7,13},{8,2},{9,6},{10,... | collective-permute-start | bytes 3080 | tf_op jit(solution)/shard_map/ppermute | solution.py:513
  36.6 2.0 %copy-start.5 = (s32[16]{0:T(128)}, s32[16]{0:T(128)S(1)}, u32[]{:S(2)}) copy-start(s32[16]{0:T(128)S(1)} %add_subtract_fusion.step_ref) | copy-start | bytes 196
  60.6 12.3 %copy-start.4 = (s32[512,4]{0,1:T(4,128)S(1)}, s32[512,4]{0,1:T(4,128)}, u32[]{:S(2)}) copy-start(s32[512,4]{0,1:T(4,128)} %param.10) | copy-start | bytes 24580
  60.6 39.2 %copy-start.2 = (bf16[4,128,256]{2,1,0:T(8,128)(2,1)S(1)}, bf16[4,128,256]{2,1,0:T(8,128)(2,1)}, u32[]{:S(2)}) copy-start(bf16[4,128,256]{2,1,0:T(8,128)(2,1)} %constant.71.clone.tab_ref) | copy-start | bytes 786436
  69.4 11.9 %all-to-all-start.1 = ((bf16[16,64,128]{2,1,0:T(8,128)(2,1)}), bf16[16,64,128]{2,1,0:T(8,128)(2,1)S(1)}, u32[]{:S(2)}, u32[]{:S(2)}) async-start(bf16[16,64,128]{2,1,0:T(8,128)(2,1)} %bitcast.4), calls=%async_computation.1 | async-start | bytes 524288 | tf_op jit(solution)/shard_map/all_to_all | solution.py:522

commit v5 on v4

--- a/solution.py
+++ b/solution.py
@@ -8,12 +8,10 @@
 from jax.experimental.pallas import tpu as pltpu
 from jax.sharding import PartitionSpec as P
 
-A = 2048
+
 FEEDS = 1024
 C = 1024
 SAMP = 2048
-BEAMS = 1024
-TRIALS = 512
 F32 = jnp.float32
 BF16 = jnp.bfloat16
 MIB = 1 << 20
@@ -271,7 +269,7 @@
         four = pl.ds(4 * at, 4)
         return pltpu.make_async_copy(w_hbm.at[four], w_ref.at[four], w_sem.at[at])
 
-    block = [pl.when(chan_ref[0] >= 0) for at in range(4)]
+    block = [pl.when(chan_ref[0] >= 0) for _ in range(4)]
 
     @pl.when(step == 0)
     def _():
@@ -431,15 +429,11 @@
 
 
 def frame_tables():
-    table = np.zeros((4, 2, 4, 4, 4, 4, 64), np.float32)
-    for band in range(4):
-        for m4 in range(4):
-            for mb in range(4):
-                row = np.full(64, -1.0 / 64.0)
-                row[(16 * band + 1 + 4 * mb + m4) % 64] += 1.0
-                for sub in range(4):
-                    table[band, :, sub, m4, mb, sub, :] = row / math.sqrt(C)
-    return table.reshape(4, 128, 256).astype(jnp.bfloat16)
+    shape = (4, 128, 256)
+    band, lane, to = (lax.broadcasted_iota(jnp.int32, shape, axis) for axis in range(3))
+    frame = (16 * band + 1 + 4 * (lane % 4) + lane // 4 % 4) % 64
+    value = jnp.where(frame == to % 64, 63.0 / 64.0, -1.0 / 64.0) / math.sqrt(C)
+    return jnp.where(lane // 16 % 4 == to // 64, value, 0.0).astype(BF16)
 
 
 def series_kernel(x_ref, tab_ref, out_ref, hot_ref, left_ref):
@@ -477,7 +471,7 @@
         out_ref[16 * th : 16 * th + 16] = out[:, 128 * th : 128 * th + 128].reshape(16, 16, 128)
 
 
-def series(sums):
+def series(sums, tables):
     vmem = pl.BlockSpec(memory_space=pltpu.VMEM)
     return pl.pallas_call(
         series_kernel,
@@ -490,7 +484,7 @@
         cost_estimate=pl.CostEstimate(
             flops=600_000_000, bytes_accessed=1_000_000, transcendentals=0
         ),
-    )(sums, jnp.asarray(frame_tables()))
+    )(sums, tables)
 
 
 def local(voltages, steering, chan_sub, delays):
@@ -525,15 +519,17 @@
     columns = [
         [place(r, q, b) for q in range(4) for b in range(band_count)] for r in range(groups // 4)
     ]
+    residues = gather_residues(pieces, notes)
     every = lax.all_to_all(
-        gather_residues(pieces, notes),
+        residues,
         ("grp", "band"),
         split_axis=0,
         concat_axis=0,
         tiled=True,
         axis_index_groups=columns,
     )
-    return series(every)
+    tables = frame_tables()
+    return series(every, tables)
 
 
 def solution(mesh):

time: 102 us -> 103 us (level)
  blocking collectives: 18.4 us -> 0 us
  starting transfers between devices: 26.2 us -> 36.4 us
  waiting for transfers between devices: 26.9 us -> 34.9 us
    all_to_all x1 -> x0, blocking collectives: 18.4 us -> none  [local(): lax.all_to_all(gather_residues(pieces, notes), ('grp', 'band'), split_axi...]
    all_to_all x0 -> x1, starting transfers between devices: none -> 10.1 us  [local(): lax.all_to_all(residues, ('grp', 'band'), split_axis=0, concat_axis=0, ti...]
    all_to_all x0 -> x1, waiting for transfers between devices: none -> 8.12 us  [local(): lax.all_to_all(residues, ('grp', 'band'), split_axis=0, concat_axis=0, ti...]
  transfers between devices with their start and end apart: 5 -> 6, of which waited for: 4 -> 5; matrix products, arithmetic and copies ran while one was open for 3% -> 3% of each run, Pallas kernels for 11% -> 11%
where the time goes in v5:
time: 103 us
  starting transfers between devices  36.4 us (35%)
  waiting for transfers between devices  34.9 us (34%)
  Pallas kernels  26.9 us (26%)
  other arithmetic  2.4 us (2%)
  local copies, waits for them, and re-layouts  2 us (2%)
    all_to_all x1, starting transfers between devices, local(): lax.all_to_all(residues, ('grp', 'band'), split_axis=0, concat_axis=0, ti...  10.1 us
    all_to_all x1, starting transfers between devices, local(): lax.all_to_all(chunks, 'grp', split_axis=0, concat_axis=0, tiled=True)  9.16 us
    pallas_call x1, Pallas kernels, beams(): pl.pallas_call(beam_kernel, name='beams', grid=(4,), out_shape=jax.ShapeD...  8.77 us
    ppermute x1, waiting for transfers between devices, local(): quarter_subs = lax.ppermute(chan_sub, ('grp', 'band'), swap)  8.36 us
    all_to_all x1, waiting for transfers between devices, local(): lax.all_to_all(sums, 'grp', split_axis=0, concat_axis=0, tiled=True, axis...  8.27 us
    all_to_all x1, waiting for transfers between devices, local(): lax.all_to_all(residues, ('grp', 'band'), split_axis=0, concat_axis=0, ti...  8.12 us
    all_to_all x1, waiting for transfers between devices, local(): lax.all_to_all(chunks, 'grp', split_axis=0, concat_axis=0, tiled=True)  7.11 us
    pallas_call x1, Pallas kernels, beam_weights(): pl.pallas_call(weight_kernel, name='weights', grid=(8,), out_shape=jax.Sh...  6.46 us
  transfers between devices with their start and end apart: 6, of which 5 were waited for; matrix products, arithmetic and copies ran while one was open for 3% of the time, Pallas kernels for 11%

profile of v5, /device:TPU:1, one launch (start us, length us, event | category | flops | bytes accessed | tf_op | source)
XLA Modules:
  0.0 102.9 jit_solution(13786812760174958238)
XLA Ops:
  0.0 1.0 slice.12
  1.0 5.7 %collective-permute-start.1 = (bf16[2,32,2048]{2,1,0:T(8,128)(2,1)S(1)}, bf16[2,32,2048]{2,1,0:T(8,128)(2,1)S(1)}, u32[]{:S(2)}, u32[]{:S(2)}) collective-permute-start(bf16[2,32,2048]{2,1,0:T(8,128)(2,1)S(1)} %slice.12), channel_id=1, source_target_pairs={{0,1},{1,2},{2,3},{4,5},{5,6},{6,7},{8,9},{9,10},{10,11},{12,13},{... | collective-permute-start | bytes 786440 | tf_op jit(solution)/shard_map/ppermute | solution.py:160
  6.7 0.9 slice.13
  7.6 2.5 %collective-permute-start.2 = (bf16[1,32,2048]{2,1,0:T(8,128)(2,1)S(1)}, bf16[1,32,2048]{2,1,0:T(8,128)(2,1)S(1)}, u32[]{:S(2)}, u32[]{:S(2)}) collective-permute-start(bf16[1,32,2048]{2,1,0:T(8,128)(2,1)S(1)} %slice.13), channel_id=1, source_target_pairs={{0,3},{1,0},{2,1},{3,2},{4,7},{5,4},{6,5},{7,6},{8,11},{9,8},{10,9... | collective-permute-start | bytes 393224 | tf_op jit(solution)/shard_map/ppermute | solution.py:161
  10.1 0.0 copy-start
  10.1 0.0 copy-start.1
  10.1 5.0 %inner_frames.1.part_hbm = bf16[8,512,256]{2,1,0:T(8,128)(2,1)} custom-call(bf16[16,32,2048]{2,1,0:T(8,128)(2,1)} %v_hbm.1, f32[4,2048]{1,0:T(4,128)} %constant.153.clone.win_ref), custom_call_target="tpu_custom_call" | custom-call | flops 20000000 | bytes 4000000 | tf_op jit(solution)/shard_map/inner_frames/pallas_call | solution.py:165
  15.1 3.1 %collective-permute-done.2.next_ref = bf16[1,32,2048]{2,1,0:T(8,128)(2,1)S(1)} collective-permute-done((bf16[1,32,2048]{2,1,0:T(8,128)(2,1)S(1)}, bf16[1,32,2048]{2,1,0:T(8,128)(2,1)S(1)}, u32[]{:S(2)}, u32[]{:S(2)}) %collective-permute-start.2) | collective-permute-done | bytes 131104 | tf_op jit(solution)/shard_map/ppermute | solution.py:161
  18.2 0.0 collective-permute-done.1.prev_ref
  18.2 0.0 copy-done
  18.2 0.0 copy-done.1
  18.2 3.7 %spectra.1 = bf16[16,4,128,128]{3,2,1,0:T(8,128)(2,1)} custom-call(s32[1]{0:T(128)} %bitcast.1.band_ref, bf16[8,512,256]{2,1,0:T(8,128)(2,1)} %inner_frames.1.part_hbm, bf16[16,32,2048]{2,1,0:T(8,128)(2,1)} %v_hbm.1, bf16[2,32,2048]{2,1,0:T(8,128)(2,1)S(1)} %collective-permute-done.1.prev_ref, bf16[1,32,2048]{2,1,0:T(8,128)(2,1)S(1)} %collective-permute-done.2.next_ref, ...), custom_call_target="tpu_custom_call" | custom-call | flops 600000000 | bytes 6000000 | tf_op jit(solution)/shard_map/spectra/pallas_call | solution.py:174
  21.9 0.0 copy-start.5
  21.9 0.0 copy-start.2
  22.0 0.0 copy-start.3
  22.0 9.2 %all-to-all-start = ((bf16[64,128,128]{2,1,0:T(8,128)(2,1)}), bf16[64,128,128]{2,1,0:T(8,128)(2,1)S(1)}, u32[]{:S(2)}, u32[]{:S(2)}) async-start(bf16[64,128,128]{2,1,0:T(8,128)(2,1)} %bitcast.9), calls=%async_computation | async-start | bytes 4194304 | tf_op jit(solution)/shard_map/all_to_all | solution.py:498
  31.1 0.0 copy-done.5
  31.1 5.5 %collective-permute-start = (s32[256]{0:T(256)S(1)}, s32[256]{0:T(256)S(1)}, u32[]{:S(2)}, u32[]{:S(2)}) collective-permute-start(s32[256]{0:T(256)S(1)} %copy-done.5), channel_id=1, source_target_pairs={{0,0},{1,4},{2,8},{3,12},{4,1},{5,5},{6,9},{7,13},{8,2},{9,6},{10,... | collective-permute-start | bytes 3080 | tf_op jit(solution)/shard_map/ppermute | solution.py:507
  36.6 0.1 mul.81
  36.7 0.0 copy-start.4
  36.8 0.1 fusion.11
  36.9 0.1 maximum_multiply_fusion.east_ref
  37.0 0.0 copy-done.2
  37.0 0.0 copy-done.3
  37.0 1.7 %fusion.hot_hbm = bf16[1024,1024]{1,0:T(8,128)(2,1)} fusion(s32[1024]{0:T(1024)S(1)} %bitcast.10), kind=kLoop, calls=%fused_computation.1 | loop fusion | flops 2097152 | bytes 2101248 | tf_op jit(solution)/shard_map/convert_element_type | solution.py:511
  38.8 0.0 copy-done.4
  38.8 6.5 %weights.1.w_hbm = bf16[16,512,512]{2,1,0:T(8,128)(2,1)} custom-call(s32[16]{0:T(128)} %copy-done.4), custom_call_target="tpu_custom_call" | custom-call | flops 20000000 | bytes 6000000 | tf_op jit(solution)/shard_map/weights/pallas_call | solution.py:388
  45.2 8.4 %collective-permute-done.chan_ref = s32[256]{0:T(256)S(1)} collective-permute-done((s32[256]{0:T(256)S(1)}, s32[256]{0:T(256)S(1)}, u32[]{:S(2)}, u32[]{:S(2)}) %collective-permute-start) | collective-permute-done | bytes 1056 | tf_op jit(solution)/shard_map/ppermute | solution.py:507
  53.6 7.1 %all-to-all-done.first_ref.odd_ref.next_ref = bf16[64,128,128]{2,1,0:T(8,128)(2,1)S(1)} async-done(((bf16[64,128,128]{2,1,0:T(8,128)(2,1)}), bf16[64,128,128]{2,1,0:T(8,128)(2,1)S(1)}, u32[]{:S(2)}, u32[]{:S(2)}) %all-to-all-start) | async-done | bytes 2097184 | tf_op jit(solution)/shard_map/all_to_all | solution.py:498
  60.7 8.8 %beams.1 = bf16[1024,128]{1,0:T(8,128)(2,1)} custom-call(f32[16,32]{1,0:T(8,128)S(1)} %maximum_multiply_fusion.east_ref, s32[256]{0:T(256)S(1)} %collective-permute-done.chan_ref, s32[1]{0:T(128)} %bitcast.residue_ref, bf16[64,128,128]{2,1,0:T(8,128)(2,1)S(1)} %all-to-all-done.first_ref.odd_ref.next_ref, ...), custom_call_target="tpu_custom_call" | custom-call | flops 2000000000 | bytes 13000000 | tf_op jit(solution)/shard_map/beams/pallas_call | solution.py:328
  69.5 3.5 %all-to-all-start.1 = ((bf16[16,64,128]{2,1,0:T(8,128)(2,1)}), bf16[16,64,128]{2,1,0:T(8,128)(2,1)S(1)}, u32[]{:S(2)}, u32[]{:S(2)}) async-start(bf16[16,64,128]{2,1,0:T(8,128)(2,1)} %bitcast.4), calls=%async_computation.1 | async-start | bytes 524288 | tf_op jit(solution)/shard_map/all_to_all | solution.py:516
  73.1 8.3 %all-to-all-done.1.x_ref = bf16[16,64,128]{2,1,0:T(8,128)(2,1)S(1)} async-done(((bf16[16,64,128]{2,1,0:T(8,128)(2,1)}), bf16[16,64,128]{2,1,0:T(8,128)(2,1)S(1)}, u32[]{:S(2)}, u32[]{:S(2)}) %all-to-all-start.1) | async-done | bytes 262176 | tf_op jit(solution)/shard_map/all_to_all | solution.py:516
  81.4 0.8 residues.1
  82.1 10.1 %all-to-all-start.2 = ((bf16[16,24,128]{2,1,0:T(8,128)(2,1)}), bf16[16,24,128]{2,1,0:T(8,128)(2,1)S(1)}, u32[]{:S(2)}, u32[]{:S(2)}) async-start(bf16[16,24,128]{2,1,0:T(8,128)(2,1)} %residues.1), calls=%async_computation.2 | async-start | bytes 196608 | tf_op jit(solution)/shard_map/all_to_all | solution.py:523
  92.2 0.4 select_convert_fusion.tab_ref
  92.6 8.1 %all-to-all-done.2.x_ref = bf16[16,24,128]{2,1,0:T(8,128)(2,1)S(1)} async-done(((bf16[16,24,128]{2,1,0:T(8,128)(2,1)}), bf16[16,24,128]{2,1,0:T(8,128)(2,1)S(1)}, u32[]{:S(2)}, u32[]{:S(2)}) %all-to-all-start.2) | async-done | bytes 98336 | tf_op jit(solution)/shard_map/all_to_all | solution.py:523
  100.7 2.2 %series.1 = f32[64,16,128]{2,1,0:T(8,128)} custom-call(bf16[16,24,128]{2,1,0:T(8,128)(2,1)S(1)} %all-to-all-done.2.x_ref, bf16[4,128,256]{2,1,0:T(8,128)(2,1)S(1)} %select_convert_fusion.tab_ref), custom_call_target="tpu_custom_call" | custom-call | flops 600000000 | bytes 1000000 | tf_op jit(solution)/shard_map/series/pallas_call | solution.py:476
  (14 shorter events, 0.1 us)
Async XLA Ops:
  1.0 17.2 %collective-permute-start.1 = (bf16[2,32,2048]{2,1,0:T(8,128)(2,1)S(1)}, bf16[2,32,2048]{2,1,0:T(8,128)(2,1)S(1)}, u32[]{:S(2)}, u32[]{:S(2)}) collective-permute-start(bf16[2,32,2048]{2,1,0:T(8,128)(2,1)S(1)} %slice.12), channel_id=1, source_target_pairs={{0,1},{1,2},{2,3},{4,5},{5,6},{6,7},{8,9},{9,10},{10,11},{12,13},{... | collective-permute-start | bytes 786440 | tf_op jit(solution)/shard_map/ppermute | solution.py:160
  7.6 10.6 %collective-permute-start.2 = (bf16[1,32,2048]{2,1,0:T(8,128)(2,1)S(1)}, bf16[1,32,2048]{2,1,0:T(8,128)(2,1)S(1)}, u32[]{:S(2)}, u32[]{:S(2)}) collective-permute-start(bf16[1,32,2048]{2,1,0:T(8,128)(2,1)S(1)} %slice.13), channel_id=1, source_target_pairs={{0,3},{1,0},{2,1},{3,2},{4,7},{5,4},{6,5},{7,6},{8,11},{9,8},{10,9... | collective-permute-start | bytes 393224 | tf_op jit(solution)/shard_map/ppermute | solution.py:161
  10.1 8.1 %copy-start = (bf16[8,256,256]{2,1,0:T(8,128)(2,1)S(1)}, bf16[8,256,256]{2,1,0:T(8,128)(2,1)}, u32[]{:S(2)}) copy-start(bf16[8,256,256]{2,1,0:T(8,128)(2,1)} %constant.154.clone.tab_hbm) | copy-start | bytes 3145732
  10.1 8.1 %copy-start.1 = (f32[4,2048]{1,0:T(4,128)S(1)}, f32[4,2048]{1,0:T(4,128)}, u32[]{:S(2)}) copy-start(f32[4,2048]{1,0:T(4,128)} %constant.153.clone.win_ref) | copy-start | bytes 98308
  21.9 9.2 %copy-start.5 = (s32[256]{0:T(256)S(1)}, s32[256]{0:T(256)}, u32[]{:S(2)}) copy-start(s32[256]{0:T(256)} %param.8) | copy-start | bytes 3076
  21.9 15.1 %copy-start.2 = (s32[2,1024]{1,0:T(2,128)S(1)}, s32[2,1024]{1,0:T(2,128)}, u32[]{:S(2)}) copy-start(s32[2,1024]{1,0:T(2,128)} %param.7) | copy-start | bytes 24580
  22.0 15.1 %copy-start.3 = (s32[512,4]{0,1:T(4,128)S(1)}, s32[512,4]{0,1:T(4,128)}, u32[]{:S(2)}) copy-start(s32[512,4]{0,1:T(4,128)} %param.9) | copy-start | bytes 24580
  22.0 38.8 %all-to-all-start = ((bf16[64,128,128]{2,1,0:T(8,128)(2,1)}), bf16[64,128,128]{2,1,0:T(8,128)(2,1)S(1)}, u32[]{:S(2)}, u32[]{:S(2)}) async-start(bf16[64,128,128]{2,1,0:T(8,128)(2,1)} %bitcast.9), calls=%async_computation | async-start | bytes 4194304 | tf_op jit(solution)/shard_map/all_to_all | solution.py:498
  31.1 22.5 %collective-permute-start = (s32[256]{0:T(256)S(1)}, s32[256]{0:T(256)S(1)}, u32[]{:S(2)}, u32[]{:S(2)}) collective-permute-start(s32[256]{0:T(256)S(1)} %copy-done.5), channel_id=1, source_target_pairs={{0,0},{1,4},{2,8},{3,12},{4,1},{5,5},{6,9},{7,13},{8,2},{9,6},{10,... | collective-permute-start | bytes 3080 | tf_op jit(solution)/shard_map/ppermute | solution.py:507
  36.7 2.1 %copy-start.4 = (s32[16]{0:T(128)}, s32[16]{0:T(128)S(1)}, u32[]{:S(2)}) copy-start(s32[16]{0:T(128)S(1)} %add_subtract_fusion.step_ref) | copy-start | bytes 196
  69.5 11.9 %all-to-all-start.1 = ((bf16[16,64,128]{2,1,0:T(8,128)(2,1)}), bf16[16,64,128]{2,1,0:T(8,128)(2,1)S(1)}, u32[]{:S(2)}, u32[]{:S(2)}) async-start(bf16[16,64,128]{2,1,0:T(8,128)(2,1)} %bitcast.4), calls=%async_computation.1 | async-start | bytes 524288 | tf_op jit(solution)/shard_map/all_to_all | solution.py:516
  82.1 18.6 %all-to-all-start.2 = ((bf16[16,24,128]{2,1,0:T(8,128)(2,1)}), bf16[16,24,128]{2,1,0:T(8,128)(2,1)S(1)}, u32[]{:S(2)}, u32[]{:S(2)}) async-start(bf16[16,24,128]{2,1,0:T(8,128)(2,1)} %residues.1), calls=%async_computation.2 | async-start | bytes 196608 | tf_op jit(solution)/shard_map/all_to_all | solution.py:523

commit v6 on v4

--- a/solution.py
+++ b/solution.py
@@ -108,26 +108,22 @@
 
 
 def spectra_kernel(
-    band_ref, part_hbm, v_hbm, prev_ref, next_ref, win_ref, tab_hbm, out_hbm,
-    part_ref, edge_ref, tab_ref, stage_ref, turn_ref, in_sem, out_sem
+    band_ref, part_hbm, first_ref, last_ref, prev_ref, next_ref, win_ref, tab_hbm, out_hbm,
+    part_ref, tab_ref, stage_ref, turn_ref, in_sem, out_sem
 ):
     inner = pl.ds(64, 416)
-    first = pltpu.make_async_copy(v_hbm.at[0:3], edge_ref.at[0:3], in_sem.at[0])
-    last = pltpu.make_async_copy(v_hbm.at[13:16], edge_ref.at[3:6], in_sem.at[1])
-    parts = pltpu.make_async_copy(part_hbm.at[:, inner, :], part_ref.at[:, inner, :], in_sem.at[2])
-    tables = pltpu.make_async_copy(tab_hbm, tab_ref, in_sem.at[3])
-    for copy in (first, last, parts, tables):
+    parts = pltpu.make_async_copy(part_hbm.at[:, inner, :], part_ref.at[:, inner, :], in_sem.at[0])
+    tables = pltpu.make_async_copy(tab_hbm, tab_ref, in_sem.at[1])
+    for copy in (parts, tables):
         copy.start()
     keep = jnp.where(band_ref[0] == 3, 0.0, 1.0).astype(F32)
-    first.wait()
-    last.wait()
 
     def edge(half, carry):
         a0 = pl.multiple_of(16 * half, 16)
         for m in (0, 1):
-            frame = lambda p, m=m: prev_ref.at[m + p] if m + p < 2 else edge_ref.at[m + p - 2]
+            frame = lambda p, m=m: prev_ref.at[m + p] if m + p < 2 else first_ref.at[m + p - 2]
             frame_bins(part_ref, win_ref, pl.multiple_of(32 * m + a0, 16), a0, frame)
-        frame = lambda p: edge_ref.at[3 + p] if p < 3 else next_ref.at[0]
+        frame = lambda p: last_ref.at[p] if p < 3 else next_ref.at[0]
         frame_bins(part_ref, win_ref, pl.multiple_of(480 + a0, 16), a0, frame, keep)
         return carry
 
@@ -177,22 +173,21 @@
         spectra_kernel,
         name="spectra",
         out_shape=jax.ShapeDtypeStruct((16, 4, 128, 128), BF16),
-        in_specs=[smem, anywhere, anywhere, vmem, vmem, vmem, anywhere],
+        in_specs=[smem, anywhere, vmem, vmem, vmem, vmem, vmem, anywhere],
         out_specs=pl.BlockSpec(memory_space=pltpu.HBM),
         scratch_shapes=[
             pltpu.VMEM((8, 512, 256), BF16),
-            pltpu.VMEM((6, 32, 2048), BF16),
             pltpu.VMEM((8, 256, 256), BF16),
             pltpu.VMEM((16, 4, 128, 128), BF16),
             pltpu.VMEM((4, 512, 128), F32),
-            pltpu.SemaphoreType.DMA((4,)),
+            pltpu.SemaphoreType.DMA((2,)),
             pltpu.SemaphoreType.DMA((16,)),
         ],
         compiler_params=pltpu.CompilerParams(vmem_limit_bytes=52 * MIB),
         cost_estimate=pl.CostEstimate(
             flops=600_000_000, bytes_accessed=6_000_000, transcendentals=0
         ),
-    )(band_at.reshape(1), parts, voltages, ahead, behind, window, tables)
+    )(band_at.reshape(1), parts, voltages[0:3], voltages[13:16], ahead, behind, window, tables)
 
 
 def turn_blocks(tiles, axis, size):

time: 102 us -> 102 us (level)
  local copies, waits for them, and re-layouts: 2 us -> 3.17 us
  waiting for transfers between devices: 26.9 us -> 25.8 us
    slice x0 -> x1, local copies, waits for them, and re-layouts: none -> 1.17 us  [spectra(): voltages[13:16]]
    ppermute x1, waiting for transfers between devices: 3.04 us -> 1.95 us  [spectra(): lax.ppermute(voltages[0:1], 'band', [(i, (i - 1) % band_count) for i in r...]
  transfers between devices with their start and end apart: 5 -> 5, of which waited for: 4 -> 4; matrix products, arithmetic and copies ran while one was open for 3% -> 4% of each run, Pallas kernels for 11% -> 11%
where the time goes in v6:
time: 102 us
  starting transfers between devices  26.2 us (26%)
  Pallas kernels  26.2 us (26%)
  waiting for transfers between devices  25.8 us (25%)
  blocking collectives  18.4 us (18%)
  local copies, waits for them, and re-layouts  3.17 us (3%)
  other arithmetic  1.96 us (2%)
    all_to_all x1, blocking collectives, local(): lax.all_to_all(gather_residues(pieces, notes), ('grp', 'band'), split_axi...  18.4 us
    all_to_all x1, starting transfers between devices, local(): lax.all_to_all(chunks, 'grp', split_axis=0, concat_axis=0, tiled=True)  9.04 us
    pallas_call x1, Pallas kernels, beams(): pl.pallas_call(beam_kernel, name='beams', grid=(4,), out_shape=jax.ShapeD...  8.77 us
    ppermute x1, waiting for transfers between devices, local(): quarter_subs = lax.ppermute(chan_sub, ('grp', 'band'), swap)  8.48 us
    all_to_all x1, waiting for transfers between devices, local(): lax.all_to_all(sums, 'grp', split_axis=0, concat_axis=0, tiled=True, axis...  8.28 us
    all_to_all x1, waiting for transfers between devices, local(): lax.all_to_all(chunks, 'grp', split_axis=0, concat_axis=0, tiled=True)  7.11 us
    pallas_call x1, Pallas kernels, beam_weights(): pl.pallas_call(weight_kernel, name='weights', grid=(8,), out_shape=jax.Sh...  6.44 us
    ppermute x1, starting transfers between devices, spectra(): lax.ppermute(voltages[14:16], 'band', [(i, i + 1) for i in range(band_cou...  5.73 us
  transfers between devices with their start and end apart: 5, of which 4 were waited for; matrix products, arithmetic and copies ran while one was open for 4% of the time, Pallas kernels for 11%

profile of v6, /device:TPU:1, one launch (start us, length us, event | category | flops | bytes accessed | tf_op | source)
XLA Modules:
  0.0 101.9 jit_solution(17028666689056360555)
XLA Ops:
  0.0 1.0 slice.20
  1.0 5.7 %collective-permute-start.1 = (bf16[2,32,2048]{2,1,0:T(8,128)(2,1)S(1)}, bf16[2,32,2048]{2,1,0:T(8,128)(2,1)S(1)}, u32[]{:S(2)}, u32[]{:S(2)}) collective-permute-start(bf16[2,32,2048]{2,1,0:T(8,128)(2,1)S(1)} %slice.20), channel_id=1, source_target_pairs={{0,1},{1,2},{2,3},{4,5},{5,6},{6,7},{8,9},{9,10},{10,11},{12,13},{... | collective-permute-start | bytes 786440 | tf_op jit(solution)/shard_map/ppermute | solution.py:158
  6.7 0.9 slice.21
  7.6 2.5 %collective-permute-start.2 = (bf16[1,32,2048]{2,1,0:T(8,128)(2,1)S(1)}, bf16[1,32,2048]{2,1,0:T(8,128)(2,1)S(1)}, u32[]{:S(2)}, u32[]{:S(2)}) collective-permute-start(bf16[1,32,2048]{2,1,0:T(8,128)(2,1)S(1)} %slice.21), channel_id=1, source_target_pairs={{0,3},{1,0},{2,1},{3,2},{4,7},{5,4},{6,5},{7,6},{8,11},{9,8},{10,9... | collective-permute-start | bytes 393224 | tf_op jit(solution)/shard_map/ppermute | solution.py:159
  10.1 1.2 %fusion.6 = (bf16[3,32,2048]{2,1,0:T(8,128)(2,1)S(1)}, bf16[3,32,2048]{2,1,0:T(8,128)(2,1)S(1)}) fusion(bf16[16,32,2048]{2,1,0:T(8,128)(2,1)} %v_ref.1), kind=kLoop, calls=%fused_computation.17 | loop fusion | bytes 1572864 | tf_op jit(solution)/shard_map/slice | solution.py:190
  11.3 0.0 copy-start
  11.3 5.0 %inner_frames.1.part_hbm = bf16[8,512,256]{2,1,0:T(8,128)(2,1)} custom-call(bf16[16,32,2048]{2,1,0:T(8,128)(2,1)} %v_ref.1, f32[4,2048]{1,0:T(4,128)} %constant.69.clone.win_ref), custom_call_target="tpu_custom_call" | custom-call | flops 20000000 | bytes 4000000 | tf_op jit(solution)/shard_map/inner_frames/pallas_call | solution.py:163
  16.3 1.9 %collective-permute-done.2.next_ref = bf16[1,32,2048]{2,1,0:T(8,128)(2,1)S(1)} collective-permute-done((bf16[1,32,2048]{2,1,0:T(8,128)(2,1)S(1)}, bf16[1,32,2048]{2,1,0:T(8,128)(2,1)S(1)}, u32[]{:S(2)}, u32[]{:S(2)}) %collective-permute-start.2) | collective-permute-done | bytes 131104 | tf_op jit(solution)/shard_map/ppermute | solution.py:159
  18.2 0.0 collective-permute-done.1.prev_ref
  18.2 0.0 copy-done
  18.2 3.7 %spectra.1 = bf16[16,4,128,128]{3,2,1,0:T(8,128)(2,1)} custom-call(s32[1]{0:T(128)} %bitcast.1.band_ref, bf16[8,512,256]{2,1,0:T(8,128)(2,1)} %inner_frames.1.part_hbm, bf16[3,32,2048]{2,1,0:T(8,128)(2,1)S(1)} %get-tuple-element.6.first_ref, bf16[3,32,2048]{2,1,0:T(8,128)(2,1)S(1)} %get-tuple-element.5.last_ref, ...), custom_call_target="tpu_custom_call" | custom-call | flops 600000000 | bytes 6000000 | tf_op jit(solution)/shard_map/spectra/pallas_call | solution.py:172
  21.9 0.0 copy-start.5
  21.9 0.0 copy-start.2
  21.9 9.0 %all-to-all-start = ((bf16[64,128,128]{2,1,0:T(8,128)(2,1)}), bf16[64,128,128]{2,1,0:T(8,128)(2,1)S(1)}, u32[]{:S(2)}, u32[]{:S(2)}) async-start(bf16[64,128,128]{2,1,0:T(8,128)(2,1)} %bitcast.9), calls=%async_computation | async-start | bytes 4194304 | tf_op jit(solution)/shard_map/all_to_all | solution.py:499
  31.0 0.0 copy-done.5
  31.0 5.5 %collective-permute-start = (s32[256]{0:T(256)S(1)}, s32[256]{0:T(256)S(1)}, u32[]{:S(2)}, u32[]{:S(2)}) collective-permute-start(s32[256]{0:T(256)S(1)} %copy-done.5), channel_id=1, source_target_pairs={{0,0},{1,4},{2,8},{3,12},{4,1},{5,5},{6,9},{7,13},{8,2},{9,6},{10,... | collective-permute-start | bytes 3080 | tf_op jit(solution)/shard_map/ppermute | solution.py:508
  36.5 0.1 mul.72
  36.6 0.0 copy-start.4
  36.6 0.1 fusion.5
  36.7 0.1 maximum_multiply_fusion.east_ref
  36.8 0.0 copy-done.2
  36.8 1.7 %fusion.hot_hbm = bf16[1024,1024]{1,0:T(8,128)(2,1)} fusion(s32[1024]{0:T(1024)S(1)} %bitcast.10), kind=kLoop, calls=%fused_computation.1 | loop fusion | flops 2097152 | bytes 2101248 | tf_op jit(solution)/shard_map/convert_element_type | solution.py:512
  38.5 0.0 copy-done.4
  38.5 6.4 %weights.1.w_hbm = bf16[16,512,512]{2,1,0:T(8,128)(2,1)} custom-call(s32[16]{0:T(128)} %copy-done.4), custom_call_target="tpu_custom_call" | custom-call | flops 20000000 | bytes 6000000 | tf_op jit(solution)/shard_map/weights/pallas_call | solution.py:385
  45.0 8.5 %collective-permute-done.chan_ref = s32[256]{0:T(256)S(1)} collective-permute-done((s32[256]{0:T(256)S(1)}, s32[256]{0:T(256)S(1)}, u32[]{:S(2)}, u32[]{:S(2)}) %collective-permute-start) | collective-permute-done | bytes 1056 | tf_op jit(solution)/shard_map/ppermute | solution.py:508
  53.5 7.1 %all-to-all-done.first_ref.odd_ref.next_ref = bf16[64,128,128]{2,1,0:T(8,128)(2,1)S(1)} async-done(((bf16[64,128,128]{2,1,0:T(8,128)(2,1)}), bf16[64,128,128]{2,1,0:T(8,128)(2,1)S(1)}, u32[]{:S(2)}, u32[]{:S(2)}) %all-to-all-start) | async-done | bytes 2097184 | tf_op jit(solution)/shard_map/all_to_all | solution.py:499
  60.6 0.0 copy-start.3
  60.6 0.0 copy-start.1
  60.6 8.8 %beams.1 = bf16[1024,128]{1,0:T(8,128)(2,1)} custom-call(f32[16,32]{1,0:T(8,128)S(1)} %maximum_multiply_fusion.east_ref, s32[256]{0:T(256)S(1)} %collective-permute-done.chan_ref, s32[1]{0:T(128)} %bitcast.residue_ref, bf16[64,128,128]{2,1,0:T(8,128)(2,1)S(1)} %all-to-all-done.first_ref.odd_ref.next_ref, ...), custom_call_target="tpu_custom_call" | custom-call | flops 2000000000 | bytes 13000000 | tf_op jit(solution)/shard_map/beams/pallas_call | solution.py:325
  69.4 3.5 %all-to-all-start.1 = ((bf16[16,64,128]{2,1,0:T(8,128)(2,1)}), bf16[16,64,128]{2,1,0:T(8,128)(2,1)S(1)}, u32[]{:S(2)}, u32[]{:S(2)}) async-start(bf16[16,64,128]{2,1,0:T(8,128)(2,1)} %bitcast.4), calls=%async_computation.1 | async-start | bytes 524288 | tf_op jit(solution)/shard_map/all_to_all | solution.py:517
  72.9 0.0 copy-done.3
  73.0 8.3 %all-to-all-done.1.x_ref = bf16[16,64,128]{2,1,0:T(8,128)(2,1)S(1)} async-done(((bf16[16,64,128]{2,1,0:T(8,128)(2,1)}), bf16[16,64,128]{2,1,0:T(8,128)(2,1)S(1)}, u32[]{:S(2)}, u32[]{:S(2)}) %all-to-all-start.1) | async-done | bytes 262176 | tf_op jit(solution)/shard_map/all_to_all | solution.py:517
  81.2 0.1 residues.1
  81.4 18.4 %all_to_all.15.x_ref = bf16[16,24,128]{2,1,0:T(8,128)(2,1)S(1)} all-to-all(bf16[16,24,128]{2,1,0:T(8,128)(2,1)S(1)} %residues.1), channel_id=1, replica_groups={{0,1,2,3,4,5,6,7,8,9,10,11,12,13,14,15},{16,17,18,19,20,21,22,23,24,25,..., dimensions={0} | all-to-all | bytes 196608 | tf_op jit(solution)/shard_map/all_to_all | solution.py:523
  99.7 0.0 copy-done.1
  99.7 2.2 %series.1 = f32[64,16,128]{2,1,0:T(8,128)} custom-call(bf16[16,24,128]{2,1,0:T(8,128)(2,1)S(1)} %all_to_all.15.x_ref, bf16[4,128,256]{2,1,0:T(8,128)(2,1)S(1)} %copy-done.1), custom_call_target="tpu_custom_call" | custom-call | flops 600000000 | bytes 1000000 | tf_op jit(solution)/shard_map/series/pallas_call | solution.py:477
  (5 shorter events, 0.0 us)
Async XLA Ops:
  1.0 17.2 %collective-permute-start.1 = (bf16[2,32,2048]{2,1,0:T(8,128)(2,1)S(1)}, bf16[2,32,2048]{2,1,0:T(8,128)(2,1)S(1)}, u32[]{:S(2)}, u32[]{:S(2)}) collective-permute-start(bf16[2,32,2048]{2,1,0:T(8,128)(2,1)S(1)} %slice.20), channel_id=1, source_target_pairs={{0,1},{1,2},{2,3},{4,5},{5,6},{6,7},{8,9},{9,10},{10,11},{12,13},{... | collective-permute-start | bytes 786440 | tf_op jit(solution)/shard_map/ppermute | solution.py:158
  7.6 10.6 %collective-permute-start.2 = (bf16[1,32,2048]{2,1,0:T(8,128)(2,1)S(1)}, bf16[1,32,2048]{2,1,0:T(8,128)(2,1)S(1)}, u32[]{:S(2)}, u32[]{:S(2)}) collective-permute-start(bf16[1,32,2048]{2,1,0:T(8,128)(2,1)S(1)} %slice.21), channel_id=1, source_target_pairs={{0,3},{1,0},{2,1},{3,2},{4,7},{5,4},{6,5},{7,6},{8,11},{9,8},{10,9... | collective-permute-start | bytes 393224 | tf_op jit(solution)/shard_map/ppermute | solution.py:159
  11.3 6.9 %copy-start = (f32[4,2048]{1,0:T(4,128)S(1)}, f32[4,2048]{1,0:T(4,128)}, u32[]{:S(2)}) copy-start(f32[4,2048]{1,0:T(4,128)} %constant.69.clone.win_ref) | copy-start | bytes 98308
  21.9 9.1 %copy-start.5 = (s32[256]{0:T(256)S(1)}, s32[256]{0:T(256)}, u32[]{:S(2)}) copy-start(s32[256]{0:T(256)} %param.9) | copy-start | bytes 3076
  21.9 14.9 %copy-start.2 = (s32[2,1024]{1,0:T(2,128)S(1)}, s32[2,1024]{1,0:T(2,128)}, u32[]{:S(2)}) copy-start(s32[2,1024]{1,0:T(2,128)} %param.8) | copy-start | bytes 24580
  21.9 38.6 %all-to-all-start = ((bf16[64,128,128]{2,1,0:T(8,128)(2,1)}), bf16[64,128,128]{2,1,0:T(8,128)(2,1)S(1)}, u32[]{:S(2)}, u32[]{:S(2)}) async-start(bf16[64,128,128]{2,1,0:T(8,128)(2,1)} %bitcast.9), calls=%async_computation | async-start | bytes 4194304 | tf_op jit(solution)/shard_map/all_to_all | solution.py:499
  31.0 22.5 %collective-permute-start = (s32[256]{0:T(256)S(1)}, s32[256]{0:T(256)S(1)}, u32[]{:S(2)}, u32[]{:S(2)}) collective-permute-start(s32[256]{0:T(256)S(1)} %copy-done.5), channel_id=1, source_target_pairs={{0,0},{1,4},{2,8},{3,12},{4,1},{5,5},{6,9},{7,13},{8,2},{9,6},{10,... | collective-permute-start | bytes 3080 | tf_op jit(solution)/shard_map/ppermute | solution.py:508
  36.6 2.0 %copy-start.4 = (s32[16]{0:T(128)}, s32[16]{0:T(128)S(1)}, u32[]{:S(2)}) copy-start(s32[16]{0:T(128)S(1)} %add_subtract_fusion.step_ref) | copy-start | bytes 196
  60.6 12.3 %copy-start.3 = (s32[512,4]{0,1:T(4,128)S(1)}, s32[512,4]{0,1:T(4,128)}, u32[]{:S(2)}) copy-start(s32[512,4]{0,1:T(4,128)} %param.10) | copy-start | bytes 24580
  60.6 39.2 %copy-start.1 = (bf16[4,128,256]{2,1,0:T(8,128)(2,1)S(1)}, bf16[4,128,256]{2,1,0:T(8,128)(2,1)}, u32[]{:S(2)}) copy-start(bf16[4,128,256]{2,1,0:T(8,128)(2,1)} %constant.71.clone.tab_ref) | copy-start | bytes 786436
  69.4 11.9 %all-to-all-start.1 = ((bf16[16,64,128]{2,1,0:T(8,128)(2,1)}), bf16[16,64,128]{2,1,0:T(8,128)(2,1)S(1)}, u32[]{:S(2)}, u32[]{:S(2)}) async-start(bf16[16,64,128]{2,1,0:T(8,128)(2,1)} %bitcast.4), calls=%async_computation.1 | async-start | bytes 524288 | tf_op jit(solution)/shard_map/all_to_all | solution.py:517

commit v7 on v6

--- a/solution.py
+++ b/solution.py
@@ -457,17 +457,13 @@
     lane = lax.broadcasted_iota(jnp.int32, (16, 128), 1) % 64
     for at in range(8):
         rows, cols = slice(16 * (at // 2), 16 * (at // 2) + 16), slice(128 * (at % 2), 128 * (at % 2) + 128)
-        block = series[rows, cols]
+        block = series[rows, cols].astype(BF16)
         for t in range(16):
             x = block
             if t:
                 x = jnp.where(lane < 64 - t, pltpu.roll(x, 128 - t, 1), pltpu.roll(x, 64 - t, 1))
-            top = x.astype(BF16)
-            left_ref[0, 16 * t : 16 * t + 16, 128 * at : 128 * at + 128] = top
-            left_ref[1, 16 * t : 16 * t + 16, 128 * at : 128 * at + 128] = (x - top.astype(F32)).astype(BF16)
-    hot = hot_ref[...]
-    out = lax.dot_general(left_ref[0], hot, NN, preferred_element_type=F32)
-    out = out + lax.dot_general(left_ref[1], hot, NN, preferred_element_type=F32)
+            left_ref[16 * t : 16 * t + 16, 128 * at : 128 * at + 128] = x
+    out = lax.dot_general(left_ref[...], hot_ref[...], NN, preferred_element_type=F32)
     for th in range(4):
         out_ref[16 * th : 16 * th + 16] = out[:, 128 * th : 128 * th + 128].reshape(16, 16, 128)
 
@@ -480,7 +476,7 @@
         out_shape=jax.ShapeDtypeStruct((64, 16, 128), F32),
         in_specs=[vmem] * 2,
         out_specs=vmem,
-        scratch_shapes=[pltpu.VMEM((1024, 512), BF16), pltpu.VMEM((2, 256, 1024), BF16)],
+        scratch_shapes=[pltpu.VMEM((1024, 512), BF16), pltpu.VMEM((256, 1024), BF16)],
         compiler_params=pltpu.CompilerParams(vmem_limit_bytes=8 * MIB),
         cost_estimate=pl.CostEstimate(
             flops=600_000_000, bytes_accessed=1_000_000, transcendentals=0

time: 102 us -> 102 us (level)
  no operation moved by 1% of the time
where the time goes in v7:
time: 102 us; the launch traced here: 101 us
  starting transfers between devices  26.2 us (26%)
  waiting for transfers between devices  25.8 us (25%)
  Pallas kernels  25.6 us (25%)
  blocking collectives  18.4 us (18%)
  local copies, waits for them, and re-layouts  3.17 us (3%)
  other arithmetic  1.96 us (2%)
    all_to_all x1, blocking collectives, local(): lax.all_to_all(gather_residues(pieces, notes), ('grp', 'band'), split_axi...  18.4 us
    all_to_all x1, starting transfers between devices, local(): lax.all_to_all(chunks, 'grp', split_axis=0, concat_axis=0, tiled=True)  9.04 us
    pallas_call x1, Pallas kernels, beams(): pl.pallas_call(beam_kernel, name='beams', grid=(4,), out_shape=jax.ShapeD...  8.77 us
    ppermute x1, waiting for transfers between devices, local(): quarter_subs = lax.ppermute(chan_sub, ('grp', 'band'), swap)  8.48 us
    all_to_all x1, waiting for transfers between devices, local(): lax.all_to_all(sums, 'grp', split_axis=0, concat_axis=0, tiled=True, axis...  8.28 us
    all_to_all x1, waiting for transfers between devices, local(): lax.all_to_all(chunks, 'grp', split_axis=0, concat_axis=0, tiled=True)  7.11 us
    pallas_call x1, Pallas kernels, beam_weights(): pl.pallas_call(weight_kernel, name='weights', grid=(8,), out_shape=jax.Sh...  6.44 us
    ppermute x1, starting transfers between devices, spectra(): lax.ppermute(voltages[14:16], 'band', [(i, i + 1) for i in range(band_cou...  5.73 us
  transfers between devices with their start and end apart: 5, of which 4 were waited for; matrix products, arithmetic and copies ran while one was open for 4% of the time, Pallas kernels for 11%

profile of v7, /device:TPU:1, one launch (start us, length us, event | category | flops | bytes accessed | tf_op | source)
XLA Modules:
  0.0 101.4 jit_solution(7240895959005395406)
XLA Ops:
  0.0 1.0 slice.20
  1.0 5.7 %collective-permute-start.1 = (bf16[2,32,2048]{2,1,0:T(8,128)(2,1)S(1)}, bf16[2,32,2048]{2,1,0:T(8,128)(2,1)S(1)}, u32[]{:S(2)}, u32[]{:S(2)}) collective-permute-start(bf16[2,32,2048]{2,1,0:T(8,128)(2,1)S(1)} %slice.20), channel_id=1, source_target_pairs={{0,1},{1,2},{2,3},{4,5},{5,6},{6,7},{8,9},{9,10},{10,11},{12,13},{... | collective-permute-start | bytes 786440 | tf_op jit(solution)/shard_map/ppermute | solution.py:158
  6.7 0.9 slice.21
  7.6 2.5 %collective-permute-start.2 = (bf16[1,32,2048]{2,1,0:T(8,128)(2,1)S(1)}, bf16[1,32,2048]{2,1,0:T(8,128)(2,1)S(1)}, u32[]{:S(2)}, u32[]{:S(2)}) collective-permute-start(bf16[1,32,2048]{2,1,0:T(8,128)(2,1)S(1)} %slice.21), channel_id=1, source_target_pairs={{0,3},{1,0},{2,1},{3,2},{4,7},{5,4},{6,5},{7,6},{8,11},{9,8},{10,9... | collective-permute-start | bytes 393224 | tf_op jit(solution)/shard_map/ppermute | solution.py:159
  10.1 1.2 %fusion.6 = (bf16[3,32,2048]{2,1,0:T(8,128)(2,1)S(1)}, bf16[3,32,2048]{2,1,0:T(8,128)(2,1)S(1)}) fusion(bf16[16,32,2048]{2,1,0:T(8,128)(2,1)} %v_ref.1), kind=kLoop, calls=%fused_computation.17 | loop fusion | bytes 1572864 | tf_op jit(solution)/shard_map/slice | solution.py:190
  11.3 0.0 copy-start
  11.3 5.0 %inner_frames.1.part_hbm = bf16[8,512,256]{2,1,0:T(8,128)(2,1)} custom-call(bf16[16,32,2048]{2,1,0:T(8,128)(2,1)} %v_ref.1, f32[4,2048]{1,0:T(4,128)} %constant.69.clone.win_ref), custom_call_target="tpu_custom_call" | custom-call | flops 20000000 | bytes 4000000 | tf_op jit(solution)/shard_map/inner_frames/pallas_call | solution.py:163
  16.3 1.9 %collective-permute-done.2.next_ref = bf16[1,32,2048]{2,1,0:T(8,128)(2,1)S(1)} collective-permute-done((bf16[1,32,2048]{2,1,0:T(8,128)(2,1)S(1)}, bf16[1,32,2048]{2,1,0:T(8,128)(2,1)S(1)}, u32[]{:S(2)}, u32[]{:S(2)}) %collective-permute-start.2) | collective-permute-done | bytes 131104 | tf_op jit(solution)/shard_map/ppermute | solution.py:159
  18.2 0.0 collective-permute-done.1.prev_ref
  18.2 0.0 copy-done
  18.2 3.7 %spectra.1 = bf16[16,4,128,128]{3,2,1,0:T(8,128)(2,1)} custom-call(s32[1]{0:T(128)} %bitcast.1.band_ref, bf16[8,512,256]{2,1,0:T(8,128)(2,1)} %inner_frames.1.part_hbm, bf16[3,32,2048]{2,1,0:T(8,128)(2,1)S(1)} %get-tuple-element.6.first_ref, bf16[3,32,2048]{2,1,0:T(8,128)(2,1)S(1)} %get-tuple-element.5.last_ref, ...), custom_call_target="tpu_custom_call" | custom-call | flops 600000000 | bytes 6000000 | tf_op jit(solution)/shard_map/spectra/pallas_call | solution.py:172
  21.9 0.0 copy-start.5
  21.9 0.0 copy-start.2
  21.9 9.0 %all-to-all-start = ((bf16[64,128,128]{2,1,0:T(8,128)(2,1)}), bf16[64,128,128]{2,1,0:T(8,128)(2,1)S(1)}, u32[]{:S(2)}, u32[]{:S(2)}) async-start(bf16[64,128,128]{2,1,0:T(8,128)(2,1)} %bitcast.9), calls=%async_computation | async-start | bytes 4194304 | tf_op jit(solution)/shard_map/all_to_all | solution.py:495
  31.0 0.0 copy-done.5
  31.0 5.5 %collective-permute-start = (s32[256]{0:T(256)S(1)}, s32[256]{0:T(256)S(1)}, u32[]{:S(2)}, u32[]{:S(2)}) collective-permute-start(s32[256]{0:T(256)S(1)} %copy-done.5), channel_id=1, source_target_pairs={{0,0},{1,4},{2,8},{3,12},{4,1},{5,5},{6,9},{7,13},{8,2},{9,6},{10,... | collective-permute-start | bytes 3080 | tf_op jit(solution)/shard_map/ppermute | solution.py:504
  36.5 0.1 mul.72
  36.6 0.0 copy-start.4
  36.6 0.1 fusion.5
  36.7 0.1 maximum_multiply_fusion.east_ref
  36.8 0.0 copy-done.2
  36.8 1.7 %fusion.hot_hbm = bf16[1024,1024]{1,0:T(8,128)(2,1)} fusion(s32[1024]{0:T(1024)S(1)} %bitcast.10), kind=kLoop, calls=%fused_computation.1 | loop fusion | flops 2097152 | bytes 2101248 | tf_op jit(solution)/shard_map/convert_element_type | solution.py:508
  38.5 0.0 copy-done.4
  38.5 6.4 %weights.1.w_hbm = bf16[16,512,512]{2,1,0:T(8,128)(2,1)} custom-call(s32[16]{0:T(128)} %copy-done.4), custom_call_target="tpu_custom_call" | custom-call | flops 20000000 | bytes 6000000 | tf_op jit(solution)/shard_map/weights/pallas_call | solution.py:385
  45.0 8.5 %collective-permute-done.chan_ref = s32[256]{0:T(256)S(1)} collective-permute-done((s32[256]{0:T(256)S(1)}, s32[256]{0:T(256)S(1)}, u32[]{:S(2)}, u32[]{:S(2)}) %collective-permute-start) | collective-permute-done | bytes 1056 | tf_op jit(solution)/shard_map/ppermute | solution.py:504
  53.5 7.1 %all-to-all-done.first_ref.odd_ref.next_ref = bf16[64,128,128]{2,1,0:T(8,128)(2,1)S(1)} async-done(((bf16[64,128,128]{2,1,0:T(8,128)(2,1)}), bf16[64,128,128]{2,1,0:T(8,128)(2,1)S(1)}, u32[]{:S(2)}, u32[]{:S(2)}) %all-to-all-start) | async-done | bytes 2097184 | tf_op jit(solution)/shard_map/all_to_all | solution.py:495
  60.6 0.0 copy-start.3
  60.6 0.0 copy-start.1
  60.6 8.8 %beams.1 = bf16[1024,128]{1,0:T(8,128)(2,1)} custom-call(f32[16,32]{1,0:T(8,128)S(1)} %maximum_multiply_fusion.east_ref, s32[256]{0:T(256)S(1)} %collective-permute-done.chan_ref, s32[1]{0:T(128)} %bitcast.residue_ref, bf16[64,128,128]{2,1,0:T(8,128)(2,1)S(1)} %all-to-all-done.first_ref.odd_ref.next_ref, ...), custom_call_target="tpu_custom_call" | custom-call | flops 2000000000 | bytes 13000000 | tf_op jit(solution)/shard_map/beams/pallas_call | solution.py:325
  69.4 3.5 %all-to-all-start.1 = ((bf16[16,64,128]{2,1,0:T(8,128)(2,1)}), bf16[16,64,128]{2,1,0:T(8,128)(2,1)S(1)}, u32[]{:S(2)}, u32[]{:S(2)}) async-start(bf16[16,64,128]{2,1,0:T(8,128)(2,1)} %bitcast.4), calls=%async_computation.1 | async-start | bytes 524288 | tf_op jit(solution)/shard_map/all_to_all | solution.py:513
  72.9 0.0 copy-done.3
  73.0 8.3 %all-to-all-done.1.x_ref = bf16[16,64,128]{2,1,0:T(8,128)(2,1)S(1)} async-done(((bf16[16,64,128]{2,1,0:T(8,128)(2,1)}), bf16[16,64,128]{2,1,0:T(8,128)(2,1)S(1)}, u32[]{:S(2)}, u32[]{:S(2)}) %all-to-all-start.1) | async-done | bytes 262176 | tf_op jit(solution)/shard_map/all_to_all | solution.py:513
  81.2 0.1 residues.1
  81.4 18.4 %all_to_all.15.x_ref = bf16[16,24,128]{2,1,0:T(8,128)(2,1)S(1)} all-to-all(bf16[16,24,128]{2,1,0:T(8,128)(2,1)S(1)} %residues.1), channel_id=1, replica_groups={{0,1,2,3,4,5,6,7,8,9,10,11,12,13,14,15},{16,17,18,19,20,21,22,23,24,25,..., dimensions={0} | all-to-all | bytes 196608 | tf_op jit(solution)/shard_map/all_to_all | solution.py:519
  99.7 0.0 copy-done.1
  99.7 1.6 %series.1 = f32[64,16,128]{2,1,0:T(8,128)} custom-call(bf16[16,24,128]{2,1,0:T(8,128)(2,1)S(1)} %all_to_all.15.x_ref, bf16[4,128,256]{2,1,0:T(8,128)(2,1)S(1)} %copy-done.1), custom_call_target="tpu_custom_call" | custom-call | flops 600000000 | bytes 1000000 | tf_op jit(solution)/shard_map/series/pallas_call | solution.py:473
  (5 shorter events, 0.0 us)
Async XLA Ops:
  1.0 17.2 %collective-permute-start.1 = (bf16[2,32,2048]{2,1,0:T(8,128)(2,1)S(1)}, bf16[2,32,2048]{2,1,0:T(8,128)(2,1)S(1)}, u32[]{:S(2)}, u32[]{:S(2)}) collective-permute-start(bf16[2,32,2048]{2,1,0:T(8,128)(2,1)S(1)} %slice.20), channel_id=1, source_target_pairs={{0,1},{1,2},{2,3},{4,5},{5,6},{6,7},{8,9},{9,10},{10,11},{12,13},{... | collective-permute-start | bytes 786440 | tf_op jit(solution)/shard_map/ppermute | solution.py:158
  7.6 10.6 %collective-permute-start.2 = (bf16[1,32,2048]{2,1,0:T(8,128)(2,1)S(1)}, bf16[1,32,2048]{2,1,0:T(8,128)(2,1)S(1)}, u32[]{:S(2)}, u32[]{:S(2)}) collective-permute-start(bf16[1,32,2048]{2,1,0:T(8,128)(2,1)S(1)} %slice.21), channel_id=1, source_target_pairs={{0,3},{1,0},{2,1},{3,2},{4,7},{5,4},{6,5},{7,6},{8,11},{9,8},{10,9... | collective-permute-start | bytes 393224 | tf_op jit(solution)/shard_map/ppermute | solution.py:159
  11.3 6.9 %copy-start = (f32[4,2048]{1,0:T(4,128)S(1)}, f32[4,2048]{1,0:T(4,128)}, u32[]{:S(2)}) copy-start(f32[4,2048]{1,0:T(4,128)} %constant.69.clone.win_ref) | copy-start | bytes 98308
  21.9 9.1 %copy-start.5 = (s32[256]{0:T(256)S(1)}, s32[256]{0:T(256)}, u32[]{:S(2)}) copy-start(s32[256]{0:T(256)} %param.9) | copy-start | bytes 3076
  21.9 14.9 %copy-start.2 = (s32[2,1024]{1,0:T(2,128)S(1)}, s32[2,1024]{1,0:T(2,128)}, u32[]{:S(2)}) copy-start(s32[2,1024]{1,0:T(2,128)} %param.8) | copy-start | bytes 24580
  21.9 38.6 %all-to-all-start = ((bf16[64,128,128]{2,1,0:T(8,128)(2,1)}), bf16[64,128,128]{2,1,0:T(8,128)(2,1)S(1)}, u32[]{:S(2)}, u32[]{:S(2)}) async-start(bf16[64,128,128]{2,1,0:T(8,128)(2,1)} %bitcast.9), calls=%async_computation | async-start | bytes 4194304 | tf_op jit(solution)/shard_map/all_to_all | solution.py:495
  31.0 22.5 %collective-permute-start = (s32[256]{0:T(256)S(1)}, s32[256]{0:T(256)S(1)}, u32[]{:S(2)}, u32[]{:S(2)}) collective-permute-start(s32[256]{0:T(256)S(1)} %copy-done.5), channel_id=1, source_target_pairs={{0,0},{1,4},{2,8},{3,12},{4,1},{5,5},{6,9},{7,13},{8,2},{9,6},{10,... | collective-permute-start | bytes 3080 | tf_op jit(solution)/shard_map/ppermute | solution.py:504
  36.6 2.0 %copy-start.4 = (s32[16]{0:T(128)}, s32[16]{0:T(128)S(1)}, u32[]{:S(2)}) copy-start(s32[16]{0:T(128)S(1)} %add_subtract_fusion.step_ref) | copy-start | bytes 196
  60.6 12.3 %copy-start.3 = (s32[512,4]{0,1:T(4,128)S(1)}, s32[512,4]{0,1:T(4,128)}, u32[]{:S(2)}) copy-start(s32[512,4]{0,1:T(4,128)} %param.10) | copy-start | bytes 24580
  60.6 39.2 %copy-start.1 = (bf16[4,128,256]{2,1,0:T(8,128)(2,1)S(1)}, bf16[4,128,256]{2,1,0:T(8,128)(2,1)}, u32[]{:S(2)}) copy-start(bf16[4,128,256]{2,1,0:T(8,128)(2,1)} %constant.71.clone.tab_ref) | copy-start | bytes 786436
  69.4 11.9 %all-to-all-start.1 = ((bf16[16,64,128]{2,1,0:T(8,128)(2,1)}), bf16[16,64,128]{2,1,0:T(8,128)(2,1)S(1)}, u32[]{:S(2)}, u32[]{:S(2)}) async-start(bf16[16,64,128]{2,1,0:T(8,128)(2,1)} %bitcast.4), calls=%async_computation.1 | async-start | bytes 524288 | tf_op jit(solution)/shard_map/all_to_all | solution.py:513
